TPU v7x, 256 devices: a whole 4x4x8 slice. The times are simulated.
256 devices in a mesh: chan: 4 (over x), mset: 8 (over y, core), blk: 8 (over z).
Axes of the slice: x: 4, y: 4, z: 8, core: 2. Of those that a mesh axis runs over, the one named last changes fastest.
Arguments:
- harmonics: bfloat16 [2, 3, 64, 1536], P(None, None, ('mset', 'blk'), 'chan'), may hold values from -6 to 6
- mixing: float32 [12, 3], replicated, may hold values from 0.2 to 1.2
- beam_window: float32 [12, 1536], P(None, 'chan'), may hold values from 0.2 to 1
- prior_inv: float32 [3, 1536], P(None, 'chan'), may hold values from 0.3 to 3
- legendre: bfloat16 [64, 1536, 8192], P(('mset', 'blk'), 'chan'), may hold values from -0.15625 to 0.15625
- inv_noise: bfloat16 [12, 8192, 8192], P('chan', ('mset', 'blk')), may hold values from 0.0099487305 to 0.099609375
- mode_index: int32 [64], replicated, may hold values from 0 to 1535, as said below
- cycle_pixels: int32 [12], replicated, may hold values from 2048 to 8192, as said below
Outputs:
- applied: float32 [2, 3, 64, 1536], P(None, None, ('mset', 'blk'), 'chan')
Inputs may be any that keep to these rules, and one draw needn't show every extreme that they name: `mode_index`: distinct values; 0 and 1535 are always among them. `cycle_pixels`: each value is 2048, 4096 or 8192; every draw holds both the smallest and the largest.
All inputs are finite; a program needn't handle non-finite values.
Results may differ from a plain program's by a relative error of at most 0.005.
Values may be sent and summed in bfloat16 or wider, within the bound.
No kernel may reach another device: no remote copies, remote signals or barrier semaphores. Data moves between devices by JAX's collectives and lax.ppermute only.
A program may use at most 128 MiB of HBM per device.

v0:
```python
import math

import jax
import jax.numpy as jnp
from jax import lax
from jax.sharding import PartitionSpec as P


def make_table(mode_index, npix, pixels, mode_count):
    fine_width = 128
    coarse_count = pixels // fine_width
    twice = 2 * npix
    coarse_idx = jnp.arange(coarse_count)
    fine_idx = jnp.arange(fine_width)
    coarse_res = mode_index[:, None] * (2 * fine_width * coarse_idx)[None, :] % twice
    fine_res = mode_index[:, None] * (2 * fine_idx + 1)[None, :] % twice
    scale = jnp.pi / npix.astype(jnp.float32)
    coarse_phase = scale * coarse_res.astype(jnp.float32)
    fine_phase = scale * fine_res.astype(jnp.float32)
    coarse_cos = jnp.cos(coarse_phase)[:, :, None]
    coarse_sin = jnp.sin(coarse_phase)[:, :, None]
    fine_cos = jnp.cos(fine_phase)[:, None, :]
    fine_sin = jnp.sin(fine_phase)[:, None, :]
    cos_full = (coarse_cos * fine_cos - coarse_sin * fine_sin).reshape(mode_count, pixels)
    sin_full = (coarse_sin * fine_cos + coarse_cos * fine_sin).reshape(mode_count, pixels)
    pix_index = jnp.arange(pixels)
    inside = pix_index[None, :] < npix
    weight = jnp.where(mode_index == 0, 1.0, 2.0).astype(jnp.float32)[:, None] / math.sqrt(
        2 * mode_count
    )
    cos_part = jnp.where(inside, weight * cos_full, 0.0)
    sin_part = jnp.where(inside, -weight * sin_full, 0.0)
    return jnp.concatenate([cos_part, sin_part], axis=0).astype(jnp.bfloat16)


def on_device(
    harmonics, mixing, beam_window, prior_inv, legendre, inv_noise, mode_index, cycle_pixels
):
    chan_count = lax.axis_size("chan")
    chan_pos = lax.axis_index("chan")
    chan_slots = inv_noise.shape[0]
    cycle_dev = inv_noise.shape[1]
    pixels = inv_noise.shape[2]
    channels = mixing.shape[0]
    mode_shard = legendre.shape[0]
    local_deg = legendre.shape[1]
    mode_count = mode_index.shape[0]
    total_deg = local_deg * chan_count
    degrees = chan_pos * local_deg + jnp.arange(local_deg)
    band_limit = total_deg * cycle_pixels // pixels - 1
    filter_bank = jnp.where(degrees[None, :] <= band_limit[:, None], beam_window, 0.0)
    coeffs = harmonics.astype(jnp.float32)
    mixture = (
        jnp.sum(mixing[:, None, :, None, None] * coeffs[None], axis=2)
        * filter_bank[:, None, None, :]
    )
    channel_harmonic_coeffs = mixture.astype(jnp.bfloat16).reshape(
        2 * channels, mode_shard, local_deg
    )
    partial_value = jnp.einsum(
        "ijn,jnw->ijw", channel_harmonic_coeffs, legendre, preferred_element_type=jnp.float32
    )
    reduced_sum = lax.psum_scatter(
        partial_value.astype(jnp.bfloat16), "chan", scatter_dimension=0, tiled=True
    )
    cycle_data = lax.all_to_all(
        reduced_sum, ("mset", "blk"), split_axis=2, concat_axis=1, tiled=True
    )
    own_pixels = lax.dynamic_slice_in_dim(cycle_pixels, chan_pos * chan_slots, chan_slots)
    tables = jax.vmap(lambda npix: make_table(mode_index, npix, pixels, mode_count))(own_pixels)
    spectra = cycle_data.reshape(chan_slots, 2 * mode_count, cycle_dev)
    sky_map = jnp.einsum("cnr,cnp->crp", spectra, tables, preferred_element_type=jnp.float32)
    noisy_map = (sky_map * inv_noise).astype(jnp.bfloat16)
    mode_spectra = jnp.einsum("cnp,crp->cnr", tables, noisy_map, preferred_element_type=jnp.float32)
    mode_spectra = mode_spectra.astype(jnp.bfloat16).reshape(2 * chan_slots, mode_count, cycle_dev)
    returned = lax.all_to_all(
        mode_spectra, ("mset", "blk"), split_axis=1, concat_axis=2, tiled=True
    )
    collected_rows = lax.all_gather(returned, "chan", axis=0, tiled=True)
    harmonic_back = jnp.einsum(
        "ogb,gfb->ogf", collected_rows, legendre, preferred_element_type=jnp.float32
    )
    harmonic_back = harmonic_back.reshape(channels, 2, mode_shard, local_deg)
    weighted = harmonic_back * filter_bank[:, None, None, :]
    transposed = jnp.einsum("ck,ciml->ikml", mixing, weighted, precision=lax.Precision.HIGHEST)
    return prior_inv[None, :, None, :] * coeffs + transposed


def solution(mesh):
    placed = (
        P(None, None, ("mset", "blk"), "chan"),
        P(),
        P(None, "chan"),
        P(None, "chan"),
        P(("mset", "blk"), "chan", None),
        P("chan", ("mset", "blk"), None),
        P(),
        P(),
    )
    return jax.shard_map(
        on_device,
        mesh=mesh,
        in_specs=placed,
        out_specs=P(None, None, ("mset", "blk"), "chan"),
        check_vma=False,
    )
```

profile of v0, /device:TPU:1, one launch (start us, length us, event | category | flops | bytes accessed | tf_op | source)
XLA Modules:
  0.0 188.3 jit_solution(135521996411559418)
XLA Ops:
  0.0 0.7 fusion.28
  0.7 0.7 convert_bitcast_fusion
  1.4 0.8 copy.33
  2.2 0.1 multiply_reduce_fusion
  2.3 0.8 compare_select_fusion
  3.2 3.7 %fusion.1 = bf16[24,1,8192]{2,0,1:T(8,128)(2,1)S(1)} fusion(bf16[24,384]{1,0:T(8,128)(2,1)S(1)} %convert_element_type.71, bf16[1,384,8192]{2,1,0:T(8,128)(2,1)} %param.12), kind=kOutput, calls=%fused_computation.2 | convolution fusion | flops 151191552 | bytes 6703104 | tf_op jit(solution)/shard_map/ijn,jnw->ijw/dot_general | solution.py:60
  6.9 12.9 %fusion = bf16[8,8192]{1,0:T(8,128)(2,1)S(1)} fusion(bf16[24,1,8192]{2,0,1:T(8,128)(2,1)S(1)} %fusion.1), kind=kCustom, calls=%all-reduce-scatter | all-reduce-scatter fusion | flops 262145 | bytes 525312
  19.8 2.5 %collective-permute-start = (bf16[6,8192]{1,0:T(8,128)(2,1)S(1)}, bf16[6,8192]{1,0:T(8,128)(2,1)S(1)}, u32[]{:S(2)}, u32[]{:S(2)}) collective-permute-start(bf16[6,8192]{1,0:T(8,128)(2,1)S(1)} %slice), channel_id=1, source_target_pairs={{0,64},{64,128},{128,192},{1,65},{65,129},{129,193},{2,66},{66,130... | collective-permute-start | bytes 294920
  22.7 1.4 fusion.16
  24.1 1.4 fusion.20
  25.5 7.1 %multiply_subtract_fusion = (f32[3,64,64,128]{3,2,1,0:T(8,128)}, f32[3,64,64,128]{3,2,1,0:T(8,128)}) fusion(f32[3,64,128]{2,1,0:T(8,128)S(1)} %get-tuple-element.12, f32[3,64,64]{2,1,0:T(8,128)S(1)} %get-tuple-element.10, f32[3,64,128]{2,1,0:T(8,128)S(1)} %get-tuple-element.11, f32[3,64,64]{2,1,0:T(8,128)S(1)} %get-tuple-element.9), kind=kLoop, calls=%fused_computation.10 | loop fusion | flops 9437184 | bytes 12877824 | tf_op jit(solution)/shard_map/vmap()/sub | solution.py:24
  32.6 7.2 %add.77 = f32[3,64,8192]{2,1,0:T(8,128)} reshape(f32[3,64,64,128]{3,2,1,0:T(8,128)} %get-tuple-element.8) | data formatting | bytes 12582912 | tf_op jit(solution)/shard_map/vmap()/add | solution.py:25
  39.8 7.2 %sub.15 = f32[3,64,8192]{2,1,0:T(8,128)} reshape(f32[3,64,64,128]{3,2,1,0:T(8,128)} %get-tuple-element.7) | data formatting | bytes 12582912 | tf_op jit(solution)/shard_map/vmap()/sub | solution.py:24
  47.0 0.6 dynamic-slice.4
  48.2 0.4 concatenate.5
  48.7 6.9 %copy.35 = bf16[6,1,8192]{0,1,2:T(2,128)(2,1)} copy(bf16[6,1,8192]{2,0,1:T(8,128)(2,1)S(1)} %dynamic-slice_bitcast_fusion) | data formatting | bytes 196608 | tf_op jit(solution)/shard_map/reduce_scatter | solution.py:63
  55.6 0.5 broadcast.259
  56.1 45.2 %reduce.1 = bf16[8192,6]{1,0:T(8,128)(2,1)S(1)} reduce(bf16[8192,1,6]{2,1,0:T(2,128)(2,1)} %bitcast.55, bf16[]{:T(256)} %broadcast.259), dimensions={1}, to_apply=%bitcast.51.reduce_sub_computation | reduce | bytes 196610
  101.3 4.1 %reshape.214 = bf16[64,2,384]{2,1,0:T(2,128)(2,1)} reshape(bf16[8192,6]{1,0:T(8,128)(2,1)S(1)} %reduce.1) | data formatting | bytes 196608
  105.4 15.2 %all-to-all-start = ((bf16[64,2,384]{2,1,0:T(2,128)(2,1)}), bf16[64,2,384]{2,1,0:T(2,128)(2,1)S(1)}, u32[]{:S(2)}, u32[]{:S(2)}) async-start(bf16[64,2,384]{2,1,0:T(2,128)(2,1)} %reshape.214), calls=%async_computation | async-start | bytes 196608 | tf_op jit(solution)/shard_map/all_to_all | solution.py:66
  120.6 8.0 %select_convert_fusion.1 = (bf16[3,64,8192]{2,1,0:T(8,128)(2,1)S(1)}, bf16[3,64,8192]{2,1,0:T(8,128)(2,1)}) fusion(f32[3,64,8192]{2,1,0:T(8,128)} %sub.15, f32[64]{0:T(128)S(1)} %get-tuple-element.15, pred[3,8192]{1,0:T(4,128)(4,1)S(1)} %iota_compare_fusion, f32[3,64,8192]{2,1,0:T(8,128)} %add.77, f32[64]{0:T(128)S(1)} %get-tuple-element.16), kind=kLoop, calls=%fused_computation.9 | loop fusion | flops 9437184 | bytes 18899456 | tf_op jit(solution)/shard_map/convert
  128.6 1.7 all-to-all-done
  130.4 8.3 %reshape.215 = bf16[8192,1,6]{2,1,0:T(2,128)(2,1)} reshape(bf16[64,2,384]{2,1,0:T(2,128)(2,1)S(1)} %all-to-all-done) | data formatting | bytes 196608
  138.6 8.1 %copy.36 = bf16[6,1,8192]{2,0,1:T(8,128)(2,1)S(1)} copy(bf16[6,1,8192]{0,1,2:T(2,128)(2,1)} %bitcast.56) | data formatting | bytes 196608 | tf_op jit(solution)/shard_map/all_to_all | solution.py:66
  146.8 0.2 reshape.206
  146.9 6.8 %fusion.6 = bf16[3,128,128]{2,1,0:T(8,128)(2,1)S(1)} fusion(bf16[3,128,8192]{2,1,0:T(8,128)(2,1)} %param.13, bf16[3,128,128]{2,1,0:T(8,128)(2,1)S(1)} %reshape.206, bf16[3,64,8192]{2,1,0:T(8,128)(2,1)} %get-tuple-element.14, bf16[3,64,8192]{2,1,0:T(8,128)(2,1)S(1)} %get-tuple-element.13), kind=kOutput, calls=%fused_computation.12 | convolution fusion | flops 1645264896 | bytes 12779520 | tf_op jit(solution)/shard_map/cnp,crp->cnr/dot_general | solution.py:74
  153.9 18.3 %all_to_all.21 = bf16[6,64,128]{2,0,1:T(8,128)(2,1)S(1)} all-to-all(bf16[6,64,128]{2,0,1:T(8,128)(2,1)S(1)} %copy.38), channel_id=1, replica_groups=mesh['chan'=4,'mset'=8,'blk'=8] {'mset','blk'}, dimensions={1} | all-to-all | bytes 196608 | tf_op jit(solution)/shard_map/all_to_all | solution.py:76
  172.2 0.2 copy.39
  172.4 10.4 %all_gather.3 = bf16[24,1,8192]{2,1,0:T(2,128)(2,1)S(1)} all-gather(bf16[6,1,8192]{2,1,0:T(2,128)(2,1)S(1)} %copy.39), channel_id=1, replica_groups=mesh['chan'=4,'mset'=8,'blk'=8] {'chan'}, dimensions={0}, use_global_device_ids=true | all-gather | bytes 491520 | tf_op jit(solution)/shard_map/all_gather | solution.py:79
  182.8 4.6 %fusion.7 = f32[24,1,384]{2,0,1:T(8,128)S(1)} fusion(bf16[1,384,8192]{2,1,0:T(8,128)(2,1)} %param.12, bf16[24,1,8192]{2,1,0:T(2,128)(2,1)S(1)} %all_gather.3), kind=kOutput, calls=%fused_computation.13 | convolution fusion | flops 150994944 | bytes 6721536 | tf_op jit(solution)/shard_map/ogb,gfb->ogf/dot_general | solution.py:80
  187.5 0.2 fusion.10
  187.7 0.6 copy.41
  (31 shorter events, 0.7 us)
Async XLA Ops:
  0.0 22.3 %copy-start.4 = (s32[12]{0:T(128)S(1)}, s32[12]{0:T(128)}, u32[]{:S(2)}) copy-start(s32[12]{0:T(128)} %param.15) | copy-start | bytes 148
  0.0 22.5 %copy-start.3 = (s32[64]{0:T(128)S(1)}, s32[64]{0:T(128)}, u32[]{:S(2)}) copy-start(s32[64]{0:T(128)} %param.14) | copy-start | bytes 772
  19.8 28.4 %collective-permute-start = (bf16[6,8192]{1,0:T(8,128)(2,1)S(1)}, bf16[6,8192]{1,0:T(8,128)(2,1)S(1)}, u32[]{:S(2)}, u32[]{:S(2)}) collective-permute-start(bf16[6,8192]{1,0:T(8,128)(2,1)S(1)} %slice), channel_id=1, source_target_pairs={{0,64},{64,128},{128,192},{1,65},{65,129},{129,193},{2,66},{66,130... | collective-permute-start | bytes 294920
  39.8 7.2 %copy-start.5 = (u32[256]{0:T(256)S(1)}, u32[256]{0:T(256)}, u32[]{:S(2)}) copy-start(u32[256]{0:T(256)} %constant.68) | copy-start | bytes 3076
  105.4 24.9 %all-to-all-start = ((bf16[64,2,384]{2,1,0:T(2,128)(2,1)}), bf16[64,2,384]{2,1,0:T(2,128)(2,1)S(1)}, u32[]{:S(2)}, u32[]{:S(2)}) async-start(bf16[64,2,384]{2,1,0:T(2,128)(2,1)} %reshape.214), calls=%async_computation | async-start | bytes 196608 | tf_op jit(solution)/shard_map/all_to_all | solution.py:66
  153.8 33.7 %copy-start = (bf16[2,3,1,384]{3,0,2,1:T(2,128)(2,1)S(1)}, bf16[2,3,1,384]{3,0,2,1:T(2,128)(2,1)}, u32[]{:S(2)}) copy-start(bf16[2,3,1,384]{3,0,2,1:T(2,128)(2,1)} %param.8) | copy-start | bytes 13828
  153.8 33.7 %copy-start.1 = (f32[12,3]{0,1:T(4,128)S(1)}, f32[12,3]{0,1:T(4,128)}, u32[]{:S(2)}) copy-start(f32[12,3]{0,1:T(4,128)} %param.9) | copy-start | bytes 436
  153.8 33.7 %copy-start.2 = (f32[3,384]{1,0:T(4,128)S(1)}, f32[3,384]{1,0:T(4,128)}, u32[]{:S(2)}) copy-start(f32[3,384]{1,0:T(4,128)} %param.11) | copy-start | bytes 13828
where the time goes:
time: 192 us; the launch traced here: 188 us
  other arithmetic  65.8 us (34%)
  local copies, waits for them, and re-layouts  45.2 us (24%)
  blocking collectives  41.6 us (22%)
  starting transfers between devices  17.7 us (9%)
  matrix products  15.3 us (8%)
    unnamed x1, other arithmetic  45.2 us
    all_to_all x1, blocking collectives, on_device(): lax.all_to_all(mode_spectra, ('mset', 'blk'), split_axis=1, concat_axis=2...  18.3 us
    all_to_all x1, starting transfers between devices, on_device(): lax.all_to_all(reduced_sum, ('mset', 'blk'), split_axis=2, concat_axis=1,...  15.2 us
    unnamed x20, local copies, waits for them, and re-layouts  14.8 us
    unnamed x1, blocking collectives  12.9 us
    all_gather x1, blocking collectives, on_device(): collected_rows = lax.all_gather(returned, 'chan', axis=0, tiled=True)  10.4 us
    all_to_all x1, local copies, waits for them, and re-layouts, on_device(): lax.all_to_all(reduced_sum, ('mset', 'blk'), split_axis=2, concat_axis=1,...  8.11 us
    another operation x1, other arithmetic  7.99 us
  transfers between devices with their start and end apart: 2, of which 1 were waited for; matrix products, arithmetic and copies ran while one was open for 18% of the time, Pallas kernels for 0%

commit v1 on v0

v1 whole, which is shorter than its diff:
```python
import functools
import math

import jax
import jax.numpy as jnp
from jax import lax
from jax.experimental import pallas as pl
from jax.experimental.pallas import tpu as pltpu
from jax.sharding import PartitionSpec as P

MIB = 1 << 20
LANES = 128
ROWS = 8


def whole(space=pltpu.VMEM):
    return pl.BlockSpec(memory_space=space)


def filter_row(beam_ref, npix_ref, channel, degrees, total_deg, pixels):
    band_limit = total_deg * npix_ref[channel] // pixels - 1
    return jnp.where(degrees <= band_limit, beam_ref[pl.ds(channel, 1), :], 0.0)


def degrees_of(shape, chan_pos):
    return chan_pos * shape[-1] + lax.broadcasted_iota(jnp.int32, shape, len(shape) - 1)


def forward_body(chans, slots, pixels, npix_ref, mix_ref, harm_ref, beam_ref, leg_ref, *rest):
    outs, rows_ref = rest[:chans], rest[chans]
    step = pl.program_id(0)

    @pl.when(step == 0)
    def _():
        chan_pos = lax.axis_index("chan")
        local_deg = beam_ref.shape[1]
        degrees = degrees_of((1, local_deg), chan_pos)
        comps = [harm_ref[k].astype(jnp.float32) for k in range(harm_ref.shape[0])]
        for s in range(chans):
            group = (chan_pos + s) % chans
            for j in range(slots):
                c = group * slots + j
                mixture = sum(mix_ref[k, c] * comps[k] for k in range(len(comps)))
                filt = filter_row(beam_ref, npix_ref, c, degrees, local_deg * chans, pixels)
                rows_ref[pl.ds(s * ROWS + 2 * j, 2), :] = mixture * filt
            rest_rows = ROWS - 2 * slots
            rows_ref[pl.ds(s * ROWS + 2 * slots, rest_rows), :] = jnp.zeros(
                (rest_rows, local_deg), jnp.float32
            )

    rows = rows_ref[...].astype(jnp.bfloat16)
    partial = jnp.dot(rows, leg_ref[0], preferred_element_type=jnp.float32)
    for s in range(chans):
        outs[s][...] = partial[s * ROWS : (s + 1) * ROWS].astype(jnp.bfloat16)


def forward(npix, mixing_t, harm, beam, legendre, chans, slots, pixels, block):
    _, local_deg, cycles = legendre.shape
    return pl.pallas_call(
        functools.partial(forward_body, chans, slots, pixels),
        grid=(cycles // block,),
        in_specs=[
            whole(pltpu.SMEM),
            whole(pltpu.SMEM),
            whole(),
            whole(),
            pl.BlockSpec((1, local_deg, block), lambda r: (0, 0, r)),
        ],
        out_specs=[pl.BlockSpec((ROWS, block), lambda r: (0, r))] * chans,
        out_shape=[jax.ShapeDtypeStruct((ROWS, cycles), jnp.bfloat16)] * chans,
        scratch_shapes=[pltpu.VMEM((chans * ROWS, local_deg), jnp.float32)],
        compiler_params=pltpu.CompilerParams(vmem_limit_bytes=16 * MIB),
        cost_estimate=pl.CostEstimate(
            flops=2 * chans * ROWS * local_deg * cycles,
            bytes_accessed=2 * local_deg * cycles,
            transcendentals=0,
        ),
        name="forward",
    )(npix, mixing_t, harm, beam, legendre)


def gather_body(*refs):
    out_ref = refs[-1]
    total = refs[0][...].astype(jnp.float32)
    for ref in refs[1:-1]:
        total = total + ref[...].astype(jnp.float32)
    total = total.astype(jnp.bfloat16)
    for b in range(out_ref.shape[0]):
        out_ref[b] = total[:, b * LANES : (b + 1) * LANES]


def add_parts(parts):
    cycles = parts[0].shape[1]
    return pl.pallas_call(
        gather_body,
        in_specs=[whole()] * len(parts),
        out_specs=whole(),
        out_shape=jax.ShapeDtypeStruct((cycles // LANES, ROWS, LANES), jnp.bfloat16),
        compiler_params=pltpu.CompilerParams(vmem_limit_bytes=8 * MIB),
        name="add_parts",
    )(*parts)


def table_body(slots, npix_ref, mode_ref, out_ref):
    chan_pos = lax.axis_index("chan")
    modes = mode_ref[...]
    mode_count = modes.shape[0]
    pixels = out_ref.shape[2]
    coarse_count = pixels // LANES
    weight = jnp.where(modes == 0, 1.0, 2.0).astype(jnp.float32) / math.sqrt(2 * mode_count)
    lane = lax.broadcasted_iota(jnp.int32, (mode_count, LANES), 1)
    quarter = pixels // 4
    for j in range(slots):
        npix = npix_ref[chan_pos * slots + j]
        scale = jnp.float32(jnp.pi) / npix.astype(jnp.float32)
        fine_phase = ((modes * (2 * lane + 1)) & (2 * npix - 1)).astype(jnp.float32) * scale
        coarse_phase = ((modes * (2 * LANES * lane)) & (2 * npix - 1)).astype(jnp.float32) * scale
        fine_cos = jnp.cos(fine_phase) * weight
        fine_sin = jnp.sin(fine_phase) * weight
        coarse_cos = jnp.cos(coarse_phase)
        coarse_sin = jnp.sin(coarse_phase)
        for q in range(4):

            @pl.when(q * quarter < npix)
            def _():
                for a in range(q * coarse_count // 4, (q + 1) * coarse_count // 4):
                    cc = coarse_cos[:, a : a + 1]
                    cs = coarse_sin[:, a : a + 1]
                    cols = slice(a * LANES, (a + 1) * LANES)
                    cos_part = cc * fine_cos - cs * fine_sin
                    sin_part = -(cs * fine_cos + cc * fine_sin)
                    out_ref[j, :mode_count, cols] = cos_part.astype(jnp.bfloat16)
                    out_ref[j, mode_count:, cols] = sin_part.astype(jnp.bfloat16)


def make_tables(npix, modes, slots, pixels):
    mode_count = modes.shape[0]
    return pl.pallas_call(
        functools.partial(table_body, slots),
        in_specs=[whole(pltpu.SMEM), whole()],
        out_specs=whole(),
        out_shape=jax.ShapeDtypeStruct((slots, 2 * mode_count, pixels), jnp.bfloat16),
        compiler_params=pltpu.CompilerParams(vmem_limit_bytes=16 * MIB),
        cost_estimate=pl.CostEstimate(
            flops=10 * slots * mode_count * pixels,
            bytes_accessed=4 * slots * mode_count * pixels,
            transcendentals=4 * slots * mode_count * LANES,
        ),
        name="make_tables",
    )(npix, modes)


def middle_body(slots, block, npix_ref, spec_ref, table_ref, noise_ref, out_ref, full_ref, turned_ref, acc_ref):
    j = pl.program_id(0)
    p = pl.program_id(1)
    last = pl.num_programs(1) - 1
    mode_count = spec_ref.shape[0]
    flat = mode_count * ROWS

    @pl.when((j == 0) & (p == 0))
    def _():
        full_ref[...] = spec_ref[...].reshape(flat, LANES).astype(jnp.float32)
        for s in range(slots):
            halves = [full_ref[pl.ds(2 * s + i, mode_count, stride=ROWS), :] for i in range(2)]
            turned_ref[s] = jnp.concatenate(halves, axis=0).T.astype(jnp.bfloat16)
        full_ref[...] = jnp.zeros((flat, LANES), jnp.float32)

    @pl.when(p == 0)
    def _():
        acc_ref[...] = jnp.zeros(acc_ref.shape, jnp.float32)

    @pl.when(p * block < npix_ref[j])
    def _():
        table = table_ref[0]
        sky = jnp.dot(turned_ref[j], table, preferred_element_type=jnp.float32)
        noisy = (noise_ref[0].astype(jnp.float32) * sky).astype(jnp.bfloat16)
        acc_ref[...] += lax.dot_general(
            table, noisy, (((1,), (1,)), ((), ())), preferred_element_type=jnp.float32
        )

    @pl.when(p == last)
    def _():
        for i in range(2):
            full_ref[pl.ds(2 * j + i, mode_count, stride=ROWS), :] = acc_ref[
                i * mode_count : (i + 1) * mode_count
            ]

    @pl.when((p == last) & (j == slots - 1))
    def _():
        out_ref[...] = full_ref[...].reshape(mode_count, ROWS, LANES).astype(jnp.bfloat16)


def middle(npix_own, spectra, tables, inv_noise, block):
    slots, cycle_dev, pixels = inv_noise.shape
    mode_count = spectra.shape[0]

    def at(j, p, npix_ref):
        return (j, 0, jnp.minimum(p, npix_ref[j] // block - 1))

    return pl.pallas_call(
        functools.partial(middle_body, slots, block),
        grid_spec=pltpu.PrefetchScalarGridSpec(
            num_scalar_prefetch=1,
            grid=(slots, pixels // block),
            in_specs=[
                whole(),
                pl.BlockSpec((1, 2 * mode_count, block), at),
                pl.BlockSpec((1, cycle_dev, block), at),
            ],
            out_specs=whole(),
            scratch_shapes=[
                pltpu.VMEM((mode_count * ROWS, LANES), jnp.float32),
                pltpu.VMEM((slots, cycle_dev, 2 * mode_count), jnp.bfloat16),
                pltpu.VMEM((2 * mode_count, cycle_dev), jnp.float32),
            ],
        ),
        out_shape=jax.ShapeDtypeStruct(spectra.shape, jnp.bfloat16),
        compiler_params=pltpu.CompilerParams(vmem_limit_bytes=16 * MIB),
        name="middle",
    )(npix_own, spectra, tables, inv_noise)


def backward_body(chans, slots, pixels, npix_ref, mix_ref, harm_ref, beam_ref, prior_ref, leg_ref, *rest):
    parts, out_ref, acc_ref = rest[:chans], rest[chans], rest[chans + 1]
    step = pl.program_id(0)

    @pl.when(step == 0)
    def _():
        acc_ref[...] = jnp.zeros(acc_ref.shape, jnp.float32)

    rows = [
        jnp.concatenate([part[b] for b in range(part.shape[0])], axis=1) for part in parts
    ]
    rows = jnp.concatenate(rows, axis=0)
    acc_ref[...] += lax.dot_general(
        rows, leg_ref[0], (((1,), (1,)), ((), ())), preferred_element_type=jnp.float32
    )

    @pl.when(step == pl.num_programs(0) - 1)
    def _():
        chan_pos = lax.axis_index("chan")
        local_deg = beam_ref.shape[1]
        degrees = degrees_of((1, local_deg), chan_pos)
        comps = harm_ref.shape[0]
        totals = [prior_ref[k : k + 1, :] * harm_ref[k].astype(jnp.float32) for k in range(comps)]
        for s in range(chans):
            group = (chan_pos + chans - s) % chans
            for j in range(slots):
                c = group * slots + j
                filt = filter_row(beam_ref, npix_ref, c, degrees, local_deg * chans, pixels)
                weighted = acc_ref[pl.ds(s * ROWS + 2 * j, 2), :] * filt
                for k in range(comps):
                    totals[k] = totals[k] + mix_ref[k, c] * weighted
        for k in range(comps):
            for i in range(2):
                out_ref[i, k] = totals[k][i : i + 1]


def backward(npix, mixing_t, harm, beam, prior, legendre, parts, slots, pixels, block):
    chans = len(parts)
    _, local_deg, cycles = legendre.shape
    comps = harm.shape[0]
    return pl.pallas_call(
        functools.partial(backward_body, chans, slots, pixels),
        grid=(cycles // block,),
        in_specs=[
            whole(pltpu.SMEM),
            whole(pltpu.SMEM),
            whole(),
            whole(),
            whole(),
            pl.BlockSpec((1, local_deg, block), lambda r: (0, 0, r)),
        ]
        + [pl.BlockSpec((block // LANES, ROWS, LANES), lambda r: (r, 0, 0))] * chans,
        out_specs=whole(),
        out_shape=jax.ShapeDtypeStruct((2, comps, 1, local_deg), jnp.float32),
        scratch_shapes=[pltpu.VMEM((chans * ROWS, local_deg), jnp.float32)],
        compiler_params=pltpu.CompilerParams(vmem_limit_bytes=16 * MIB),
        name="backward",
    )(npix, mixing_t, harm, beam, prior, legendre, *parts)


def on_device(
    harmonics, mixing, beam_window, prior_inv, legendre, inv_noise, mode_index, cycle_pixels
):
    chans = lax.axis_size("chan")
    chan_pos = lax.axis_index("chan")
    slots, _, pixels = inv_noise.shape
    mixing_t = mixing.T
    harm = harmonics[:, :, 0, :].transpose(1, 0, 2)

    def shift(x, s):
        return lax.ppermute(x, "chan", [(d, (d + s) % chans) for d in range(chans)])

    parts = forward(cycle_pixels, mixing_t, harm, beam_window, legendre, chans, slots, pixels, 2048)
    parts = [parts[0]] + [shift(parts[s], s) for s in range(1, chans)]
    tables = make_tables(cycle_pixels, mode_index[:, None], slots, pixels)
    chunks = add_parts(parts)
    spectra = lax.all_to_all(chunks, ("mset", "blk"), split_axis=0, concat_axis=0, tiled=True)
    own_pixels = lax.dynamic_slice_in_dim(cycle_pixels, chan_pos * slots, slots)
    returned = middle(own_pixels, spectra, tables, inv_noise, 2048)
    own = lax.all_to_all(returned, ("mset", "blk"), split_axis=0, concat_axis=0, tiled=True)
    gathered = [own] + [shift(own, s) for s in range(1, chans)]
    return backward(
        cycle_pixels, mixing_t, harm, beam_window, prior_inv, legendre, gathered, slots, pixels, 2048
    )


def solution(mesh):
    placed = (
        P(None, None, ("mset", "blk"), "chan"),
        P(),
        P(None, "chan"),
        P(None, "chan"),
        P(("mset", "blk"), "chan", None),
        P("chan", ("mset", "blk"), None),
        P(),
        P(),
    )
    return jax.shard_map(
        on_device,
        mesh=mesh,
        in_specs=placed,
        out_specs=P(None, None, ("mset", "blk"), "chan"),
        check_vma=False,
    )
```

time: 192 us -> 86.4 us (0.45); the launches traced: 188 us -> 86.8 us
  other arithmetic: 65.8 us -> 0 us
  local copies, waits for them, and re-layouts: 45.2 us -> 14 us
  blocking collectives: 41.6 us -> 16.6 us
  Pallas kernels: 0 us -> 16 us
  matrix products: 15.3 us -> 0 us
  waiting for transfers between devices: 1.74 us -> 14.4 us
  starting transfers between devices: 17.7 us -> 25.8 us
    unnamed x1 -> x0, other arithmetic: 45.2 us -> none
    pallas_call x0 -> x5, Pallas kernels: none -> 16 us  [the longest x1 5.03 us: middle(): pl.pallas_call(functools.partial(middle_body, slots, block), grid_spec=pl...]
    dot_general x4 -> x0, matrix products: 15.3 us -> none  [the longest x1 6.84 us: on_device(): jnp.einsum('cnp,crp->cnr', tables, noisy_map, preferred_element_type=jnp....]
    unnamed x1 -> x0, blocking collectives: 12.9 us -> none
    ppermute x0 -> x6, starting transfers between devices: none -> 12.6 us  [shift(): return lax.ppermute(x, 'chan', [(d, (d + s) % chans) for d in range(chans)])]
    ppermute x0 -> x6, waiting for transfers between devices: none -> 10.9 us  [shift(): return lax.ppermute(x, 'chan', [(d, (d + s) % chans) for d in range(chans)])]
    all_gather x1 -> x0, blocking collectives: 10.4 us -> none  [on_device(): collected_rows = lax.all_gather(returned, 'chan', axis=0, tiled=True)]
    all_to_all x2 -> x0, local copies, waits for them, and re-layouts: 8.26 us -> none  [the longest x1 8.11 us: on_device(): lax.all_to_all(reduced_sum, ('mset', 'blk'), split_axis=2, concat_axis=1,...]
  transfers between devices with their start and end apart: 2 -> 7, of which waited for: 1 -> 4; matrix products, arithmetic and copies ran while one was open for 18% -> 0% of each run, Pallas kernels for 0% -> 4%
where the time goes in v1:
time: 86.4 us; the launch traced here: 86.8 us
  starting transfers between devices  25.8 us (30%)
  blocking collectives  16.6 us (19%)
  Pallas kernels  16 us (19%)
  waiting for transfers between devices  14.4 us (17%)
  local copies, waits for them, and re-layouts  14 us (16%)
    all_to_all x1, blocking collectives, on_device(): lax.all_to_all(returned, ('mset', 'blk'), split_axis=0, concat_axis=0, ti...  16.6 us
    unnamed x30, local copies, waits for them, and re-layouts  13.8 us
    all_to_all x1, starting transfers between devices, on_device(): lax.all_to_all(chunks, ('mset', 'blk'), split_axis=0, concat_axis=0, tile...  13.2 us
    ppermute x6, starting transfers between devices, shift(): return lax.ppermute(x, 'chan', [(d, (d + s) % chans) for d in range(chans)])  12.6 us
    ppermute x6, waiting for transfers between devices, shift(): return lax.ppermute(x, 'chan', [(d, (d + s) % chans) for d in range(chans)])  10.9 us
    pallas_call x1, Pallas kernels, middle(): pl.pallas_call(functools.partial(middle_body, slots, block), grid_spec=pl...  5.03 us
    pallas_call x1, Pallas kernels, backward(): pl.pallas_call(functools.partial(backward_body, chans, slots, pixels), gr...  4.03 us
    pallas_call x1, Pallas kernels, make_tables(): pl.pallas_call(functools.partial(table_body, slots), in_specs=[whole(pltp...  3.62 us
  transfers between devices with their start and end apart: 7, of which 4 were waited for; matrix products, arithmetic and copies ran while one was open for 0% of the time, Pallas kernels for 4%

profile of v1, /device:TPU:1, one launch (start us, length us, event | category | flops | bytes accessed | tf_op | source)
XLA Modules:
  0.0 86.8 jit_solution(9342059014727958835)
XLA Ops:
  0.0 2.8 %copy-done.2 = bf16[1,384,8192]{2,1,0:T(8,128)(2,1)S(1)} copy-done((bf16[1,384,8192]{2,1,0:T(8,128)(2,1)S(1)}, bf16[1,384,8192]{2,1,0:T(8,128)(2,1)}, u32[]{:S(2)}) %copy-start.2) | copy-done | bytes 6291480
  2.8 0.7 copy-done.5
  3.6 0.7 copy-done.7
  4.2 0.7 copy-done.9
  4.9 0.7 copy-done.12
  5.6 2.6 %forward.1 = (bf16[8,8192]{1,0:T(8,128)(2,1)S(1)}, bf16[8,8192]{1,0:T(8,128)(2,1)S(1)}, bf16[8,8192]{1,0:T(8,128)(2,1)S(1)}, bf16[8,8192]{1,0:T(8,128)(2,1)S(1)}) custom-call(s32[12]{0:T(128)S(1)} %copy-done.12, f32[3,12]{1,0:T(4,128)S(1)} %bitcast.7, bf16[3,2,384]{2,1,0:T(2,128)(2,1)S(1)} %bitcast.5, f32[12,384]{1,0:T(8,128)S(1)} %copy-done.5, ...), custom_call_target="tpu_custom_call" | custom-call | flops 201326592 | bytes 6291456 | tf_op jit(solution)/shard_map/forward/pallas_call | solution.py:59
  8.2 2.1 %collective-permute-start = (bf16[8,8192]{1,0:T(8,128)(2,1)S(1)}, bf16[8,8192]{1,0:T(8,128)(2,1)S(1)}, u32[]{:S(2)}, u32[]{:S(2)}) collective-permute-start(bf16[8,8192]{1,0:T(8,128)(2,1)S(1)} %get-tuple-element.10), channel_id=1, source_target_pairs={{0,64},{64,128},{128,192},{192,0},{1,65},{65,129},{129,193},{193,1... | collective-permute-start | bytes 393224 | tf_op jit(solution)/shard_map/ppermute | solution.py:293
  10.3 2.5 %collective-permute-start.1 = (bf16[8,8192]{1,0:T(8,128)(2,1)S(1)}, bf16[8,8192]{1,0:T(8,128)(2,1)S(1)}, u32[]{:S(2)}, u32[]{:S(2)}) collective-permute-start(bf16[8,8192]{1,0:T(8,128)(2,1)S(1)} %get-tuple-element.11), channel_id=1, source_target_pairs={{0,128},{64,192},{128,0},{192,64},{1,129},{65,193},{129,1},{193,65... | collective-permute-start | bytes 393224 | tf_op jit(solution)/shard_map/ppermute | solution.py:293
  12.7 1.2 %collective-permute-start.2 = (bf16[8,8192]{1,0:T(8,128)(2,1)S(1)}, bf16[8,8192]{1,0:T(8,128)(2,1)S(1)}, u32[]{:S(2)}, u32[]{:S(2)}) collective-permute-start(bf16[8,8192]{1,0:T(8,128)(2,1)S(1)} %get-tuple-element.12), channel_id=1, source_target_pairs={{0,192},{64,0},{128,64},{192,128},{1,193},{65,1},{129,65},{193,129... | collective-permute-start | bytes 393224 | tf_op jit(solution)/shard_map/ppermute | solution.py:293
  13.9 0.0 collective-permute-done.refs_1_
  13.9 4.5 %collective-permute-done.1.refs_2_ = bf16[8,8192]{1,0:T(8,128)(2,1)S(1)} collective-permute-done((bf16[8,8192]{1,0:T(8,128)(2,1)S(1)}, bf16[8,8192]{1,0:T(8,128)(2,1)S(1)}, u32[]{:S(2)}, u32[]{:S(2)}) %collective-permute-start.1) | collective-permute-done | bytes 131104 | tf_op jit(solution)/shard_map/ppermute | solution.py:293
  18.5 0.0 collective-permute-done.2.refs_3_
  18.5 0.7 add_parts.1
  19.2 13.2 %all-to-all-start = ((bf16[64,8,128]{2,1,0:T(8,128)(2,1)}), bf16[64,8,128]{2,1,0:T(8,128)(2,1)S(1)}, u32[]{:S(2)}, u32[]{:S(2)}) async-start(bf16[64,8,128]{2,1,0:T(8,128)(2,1)} %add_parts.1), calls=%async_computation | async-start | bytes 262144 | tf_op jit(solution)/shard_map/all_to_all | solution.py:299
  32.4 0.1 dynamic_slice.3.npix_ref
  32.5 0.1 copy.9.mode_ref
  32.6 3.6 %make_tables.1.table_ref = bf16[3,128,8192]{2,1,0:T(8,128)(2,1)S(1)} custom-call(s32[12]{0:T(128)S(1)} %copy-done.13, s32[64,1]{1,0:T(8,128)S(1)} %copy.9.mode_ref), custom_call_target="tpu_custom_call" | custom-call | flops 15728640 | bytes 6291456 | tf_op jit(solution)/shard_map/make_tables/pallas_call | solution.py:138
  36.2 0.0 copy-start
  36.2 2.6 %copy-done = bf16[3,128,8192]{2,1,0:T(8,128)(2,1)} copy-done((bf16[3,128,8192]{2,1,0:T(8,128)(2,1)}, bf16[3,128,8192]{2,1,0:T(8,128)(2,1)S(1)}, u32[]{:S(2)}) %copy-start) | copy-done | bytes 6291480
  38.9 3.5 %all-to-all-done.spec_ref = bf16[64,8,128]{2,1,0:T(8,128)(2,1)S(1)} async-done(((bf16[64,8,128]{2,1,0:T(8,128)(2,1)}), bf16[64,8,128]{2,1,0:T(8,128)(2,1)S(1)}, u32[]{:S(2)}, u32[]{:S(2)}) %all-to-all-start) | async-done | bytes 131104 | tf_op jit(solution)/shard_map/all_to_all | solution.py:299
  42.3 2.8 %copy-done.1 = bf16[3,128,8192]{2,1,0:T(8,128)(2,1)S(1)} copy-done((bf16[3,128,8192]{2,1,0:T(8,128)(2,1)S(1)}, bf16[3,128,8192]{2,1,0:T(8,128)(2,1)}, u32[]{:S(2)}) %copy-start.1) | copy-done | bytes 6291480
  45.1 2.8 %copy-done.4 = bf16[3,128,8192]{2,1,0:T(8,128)(2,1)S(1)} copy-done((bf16[3,128,8192]{2,1,0:T(8,128)(2,1)S(1)}, bf16[3,128,8192]{2,1,0:T(8,128)(2,1)}, u32[]{:S(2)}) %copy-start.4) | copy-done | bytes 6291480
  47.9 0.0 copy-start.11
  47.9 5.0 %middle.1 = bf16[64,8,128]{2,1,0:T(8,128)(2,1)S(1)} custom-call(s32[3]{0:T(128)S(1)} %dynamic_slice.3.npix_ref, bf16[64,8,128]{2,1,0:T(8,128)(2,1)S(1)} %all-to-all-done.spec_ref, bf16[3,128,8192]{2,1,0:T(8,128)(2,1)S(1)} %copy-done.1, bf16[3,128,8192]{2,1,0:T(8,128)(2,1)S(1)} %copy-done.4), custom_call_target="tpu_custom_call" | custom-call | tf_op jit(solution)/shard_map/middle/pallas_call | solution.py:200
  53.0 16.6 %all_to_all.10.rest_0_ = bf16[64,8,128]{2,1,0:T(8,128)(2,1)S(1)} all-to-all(bf16[64,8,128]{2,1,0:T(8,128)(2,1)S(1)} %middle.1), channel_id=1, replica_groups=mesh['chan'=4,'mset'=8,'blk'=8] {'mset','blk'}, dimensions={0} | all-to-all | bytes 262144 | tf_op jit(solution)/shard_map/all_to_all | solution.py:302
  69.5 3.8 %collective-permute-start.5 = (bf16[64,8,128]{2,1,0:T(8,128)(2,1)S(1)}, bf16[64,8,128]{2,1,0:T(8,128)(2,1)S(1)}, u32[]{:S(2)}, u32[]{:S(2)}) collective-permute-start(bf16[64,8,128]{2,1,0:T(8,128)(2,1)S(1)} %all_to_all.10.rest_0_), channel_id=1, source_target_pairs={{0,192},{64,0},{128,64},{192,128},{1,193},{65,1},{129,65},{193,129... | collective-permute-start | bytes 393224 | tf_op jit(solution)/shard_map/ppermute | solution.py:293
  73.3 2.2 %collective-permute-start.4 = (bf16[64,8,128]{2,1,0:T(8,128)(2,1)S(1)}, bf16[64,8,128]{2,1,0:T(8,128)(2,1)S(1)}, u32[]{:S(2)}, u32[]{:S(2)}) collective-permute-start(bf16[64,8,128]{2,1,0:T(8,128)(2,1)S(1)} %all_to_all.10.rest_0_), channel_id=1, source_target_pairs={{0,128},{64,192},{128,0},{192,64},{1,129},{65,193},{129,1},{193,65... | collective-permute-start | bytes 393224 | tf_op jit(solution)/shard_map/ppermute | solution.py:293
  75.6 0.9 collective-permute-start.3
  76.4 0.0 collective-permute-done.5.rest_3_
  76.4 2.2 %collective-permute-done.4.rest_2_ = bf16[64,8,128]{2,1,0:T(8,128)(2,1)S(1)} collective-permute-done((bf16[64,8,128]{2,1,0:T(8,128)(2,1)S(1)}, bf16[64,8,128]{2,1,0:T(8,128)(2,1)S(1)}, u32[]{:S(2)}, u32[]{:S(2)}) %collective-permute-start.4) | collective-permute-done | bytes 131104 | tf_op jit(solution)/shard_map/ppermute | solution.py:293
  78.7 4.1 %collective-permute-done.3.rest_1_ = bf16[64,8,128]{2,1,0:T(8,128)(2,1)S(1)} collective-permute-done((bf16[64,8,128]{2,1,0:T(8,128)(2,1)S(1)}, bf16[64,8,128]{2,1,0:T(8,128)(2,1)S(1)}, u32[]{:S(2)}, u32[]{:S(2)}) %collective-permute-start.3) | collective-permute-done | bytes 131104 | tf_op jit(solution)/shard_map/ppermute | solution.py:293
  82.8 4.0 %backward.1 = f32[2,3,1,384]{3,2,1,0:T(1,128)} custom-call(s32[12]{0:T(128)S(1)} %copy-done.13, f32[3,12]{1,0:T(4,128)S(1)} %bitcast.8, bf16[3,2,384]{2,1,0:T(2,128)(2,1)S(1)} %bitcast.6, f32[12,384]{1,0:T(8,128)S(1)} %copy-done.6, f32[3,384]{1,0:T(4,128)S(1)} %copy-done.11, bf16[1,384,8192]{2,1,0:T(8,128)(2,1)S(1)} %copy-done.3, ...), custom_call_target="tpu_custom_call" | custom-call | tf_op jit(solution)/shard_map/backward/pallas_call | solution.py:263
  (20 shorter events, 0.0 us)
Async XLA Ops:
  0.0 32.4 %copy-start.13 = (s32[12]{0:T(128)S(1)}, s32[12]{0:T(128)}, u32[]{:S(2)}) copy-start(s32[12]{0:T(128)} %npix_ref.5) | copy-start | bytes 148
  0.0 32.5 %copy-start.14 = (s32[64]{0:T(128)S(1)}, s32[64]{0:T(128)}, u32[]{:S(2)}) copy-start(s32[64]{0:T(128)} %param.14) | copy-start | bytes 772
  0.0 2.8 %copy-start.2 = (bf16[1,384,8192]{2,1,0:T(8,128)(2,1)S(1)}, bf16[1,384,8192]{2,1,0:T(8,128)(2,1)}, u32[]{:S(2)}) copy-start(bf16[1,384,8192]{2,1,0:T(8,128)(2,1)} %leg_ref.3) | copy-start | bytes 18874372
  2.8 0.7 copy-start.5
  3.6 0.7 copy-start.7
  4.2 0.7 copy-start.9
  4.9 0.7 copy-start.12
  8.2 5.7 %collective-permute-start = (bf16[8,8192]{1,0:T(8,128)(2,1)S(1)}, bf16[8,8192]{1,0:T(8,128)(2,1)S(1)}, u32[]{:S(2)}, u32[]{:S(2)}) collective-permute-start(bf16[8,8192]{1,0:T(8,128)(2,1)S(1)} %get-tuple-element.10), channel_id=1, source_target_pairs={{0,64},{64,128},{128,192},{192,0},{1,65},{65,129},{129,193},{193,1... | collective-permute-start | bytes 393224 | tf_op jit(solution)/shard_map/ppermute | solution.py:293
  10.3 8.2 %collective-permute-start.1 = (bf16[8,8192]{1,0:T(8,128)(2,1)S(1)}, bf16[8,8192]{1,0:T(8,128)(2,1)S(1)}, u32[]{:S(2)}, u32[]{:S(2)}) collective-permute-start(bf16[8,8192]{1,0:T(8,128)(2,1)S(1)} %get-tuple-element.11), channel_id=1, source_target_pairs={{0,128},{64,192},{128,0},{192,64},{1,129},{65,193},{129,1},{193,65... | collective-permute-start | bytes 393224 | tf_op jit(solution)/shard_map/ppermute | solution.py:293
  12.7 5.7 %collective-permute-start.2 = (bf16[8,8192]{1,0:T(8,128)(2,1)S(1)}, bf16[8,8192]{1,0:T(8,128)(2,1)S(1)}, u32[]{:S(2)}, u32[]{:S(2)}) collective-permute-start(bf16[8,8192]{1,0:T(8,128)(2,1)S(1)} %get-tuple-element.12), channel_id=1, source_target_pairs={{0,192},{64,0},{128,64},{192,128},{1,193},{65,1},{129,65},{193,129... | collective-permute-start | bytes 393224 | tf_op jit(solution)/shard_map/ppermute | solution.py:293
  19.2 23.1 %all-to-all-start = ((bf16[64,8,128]{2,1,0:T(8,128)(2,1)}), bf16[64,8,128]{2,1,0:T(8,128)(2,1)S(1)}, u32[]{:S(2)}, u32[]{:S(2)}) async-start(bf16[64,8,128]{2,1,0:T(8,128)(2,1)} %add_parts.1), calls=%async_computation | async-start | bytes 262144 | tf_op jit(solution)/shard_map/all_to_all | solution.py:299
  36.2 2.7 %copy-start = (bf16[3,128,8192]{2,1,0:T(8,128)(2,1)}, bf16[3,128,8192]{2,1,0:T(8,128)(2,1)S(1)}, u32[]{:S(2)}) copy-start(bf16[3,128,8192]{2,1,0:T(8,128)(2,1)S(1)} %make_tables.1.table_ref) | copy-start | bytes 18874372
  42.3 2.8 %copy-start.1 = (bf16[3,128,8192]{2,1,0:T(8,128)(2,1)S(1)}, bf16[3,128,8192]{2,1,0:T(8,128)(2,1)}, u32[]{:S(2)}) copy-start(bf16[3,128,8192]{2,1,0:T(8,128)(2,1)} %copy-done) | copy-start | bytes 18874372
  45.1 2.8 %copy-start.4 = (bf16[3,128,8192]{2,1,0:T(8,128)(2,1)S(1)}, bf16[3,128,8192]{2,1,0:T(8,128)(2,1)}, u32[]{:S(2)}) copy-start(bf16[3,128,8192]{2,1,0:T(8,128)(2,1)} %noise_ref.1) | copy-start | bytes 18874372
  47.9 34.8 %copy-start.3 = (bf16[1,384,8192]{2,1,0:T(8,128)(2,1)S(1)}, bf16[1,384,8192]{2,1,0:T(8,128)(2,1)}, u32[]{:S(2)}) copy-start(bf16[1,384,8192]{2,1,0:T(8,128)(2,1)} %leg_ref.3) | copy-start | bytes 18874372
  47.9 34.8 %copy-start.6 = (f32[12,384]{1,0:T(8,128)S(1)}, f32[12,384]{1,0:T(8,128)}, u32[]{:S(2)}) copy-start(f32[12,384]{1,0:T(8,128)} %beam_ref.3) | copy-start | bytes 55300
  47.9 34.8 %copy-start.8 = (bf16[2,3,1,384]{3,0,2,1:T(2,128)(2,1)S(1)}, bf16[2,3,1,384]{3,0,2,1:T(2,128)(2,1)}, u32[]{:S(2)}) copy-start(bf16[2,3,1,384]{3,0,2,1:T(2,128)(2,1)} %param.8) | copy-start | bytes 13828
  47.9 34.8 %copy-start.10 = (f32[12,3]{0,1:T(4,128)S(1)}, f32[12,3]{0,1:T(4,128)}, u32[]{:S(2)}) copy-start(f32[12,3]{0,1:T(4,128)} %param.9) | copy-start | bytes 436
  47.9 34.8 %copy-start.11 = (f32[3,384]{1,0:T(4,128)S(1)}, f32[3,384]{1,0:T(4,128)}, u32[]{:S(2)}) copy-start(f32[3,384]{1,0:T(4,128)} %prior_ref.1) | copy-start | bytes 13828
  69.5 6.9 %collective-permute-start.5 = (bf16[64,8,128]{2,1,0:T(8,128)(2,1)S(1)}, bf16[64,8,128]{2,1,0:T(8,128)(2,1)S(1)}, u32[]{:S(2)}, u32[]{:S(2)}) collective-permute-start(bf16[64,8,128]{2,1,0:T(8,128)(2,1)S(1)} %all_to_all.10.rest_0_), channel_id=1, source_target_pairs={{0,192},{64,0},{128,64},{192,128},{1,193},{65,1},{129,65},{193,129... | collective-permute-start | bytes 393224 | tf_op jit(solution)/shard_map/ppermute | solution.py:293
  73.3 5.3 %collective-permute-start.4 = (bf16[64,8,128]{2,1,0:T(8,128)(2,1)S(1)}, bf16[64,8,128]{2,1,0:T(8,128)(2,1)S(1)}, u32[]{:S(2)}, u32[]{:S(2)}) collective-permute-start(bf16[64,8,128]{2,1,0:T(8,128)(2,1)S(1)} %all_to_all.10.rest_0_), channel_id=1, source_target_pairs={{0,128},{64,192},{128,0},{192,64},{1,129},{65,193},{129,1},{193,65... | collective-permute-start | bytes 393224 | tf_op jit(solution)/shard_map/ppermute | solution.py:293
  75.6 7.2 %collective-permute-start.3 = (bf16[64,8,128]{2,1,0:T(8,128)(2,1)S(1)}, bf16[64,8,128]{2,1,0:T(8,128)(2,1)S(1)}, u32[]{:S(2)}, u32[]{:S(2)}) collective-permute-start(bf16[64,8,128]{2,1,0:T(8,128)(2,1)S(1)} %all_to_all.10.rest_0_), channel_id=1, source_target_pairs={{0,64},{64,128},{128,192},{192,0},{1,65},{65,129},{129,193},{193,1... | collective-permute-start | bytes 393224 | tf_op jit(solution)/shard_map/ppermute | solution.py:293

commit v2 on v1

--- a/solution.py
+++ b/solution.py
@@ -15,6 +15,10 @@
 
 def whole(space=pltpu.VMEM):
     return pl.BlockSpec(memory_space=space)
+
+
+def in_hbm(*arrays):
+    return [pltpu.with_memory_space_constraint(x, pltpu.HBM) for x in arrays]
 
 
 def filter_row(beam_ref, npix_ref, channel, degrees, total_deg, pixels):
@@ -76,7 +80,7 @@
             transcendentals=0,
         ),
         name="forward",
-    )(npix, mixing_t, harm, beam, legendre)
+    )(*in_hbm(npix, mixing_t, harm, beam, legendre))
 
 
 def gather_body(*refs):
@@ -139,7 +143,7 @@
         functools.partial(table_body, slots),
         in_specs=[whole(pltpu.SMEM), whole()],
         out_specs=whole(),
-        out_shape=jax.ShapeDtypeStruct((slots, 2 * mode_count, pixels), jnp.bfloat16),
+        out_shape=pltpu.VMEM((slots, 2 * mode_count, pixels), jnp.bfloat16),
         compiler_params=pltpu.CompilerParams(vmem_limit_bytes=16 * MIB),
         cost_estimate=pl.CostEstimate(
             flops=10 * slots * mode_count * pixels,
@@ -171,7 +175,7 @@
 
     @pl.when(p * block < npix_ref[j])
     def _():
-        table = table_ref[0]
+        table = table_ref[j, :, pl.ds(pl.multiple_of(p * block, block), block)]
         sky = jnp.dot(turned_ref[j], table, preferred_element_type=jnp.float32)
         noisy = (noise_ref[0].astype(jnp.float32) * sky).astype(jnp.bfloat16)
         acc_ref[...] += lax.dot_general(
@@ -204,7 +208,7 @@
             grid=(slots, pixels // block),
             in_specs=[
                 whole(),
-                pl.BlockSpec((1, 2 * mode_count, block), at),
+                whole(),
                 pl.BlockSpec((1, cycle_dev, block), at),
             ],
             out_specs=whole(),
@@ -217,7 +221,7 @@
         out_shape=jax.ShapeDtypeStruct(spectra.shape, jnp.bfloat16),
         compiler_params=pltpu.CompilerParams(vmem_limit_bytes=16 * MIB),
         name="middle",
-    )(npix_own, spectra, tables, inv_noise)
+    )(npix_own, spectra, pltpu.with_memory_space_constraint(tables, pltpu.VMEM), *in_hbm(inv_noise))
 
 
 def backward_body(chans, slots, pixels, npix_ref, mix_ref, harm_ref, beam_ref, prior_ref, leg_ref, *rest):
@@ -295,9 +299,10 @@
     parts = forward(cycle_pixels, mixing_t, harm, beam_window, legendre, chans, slots, pixels, 2048)
     parts = [parts[0]] + [shift(parts[s], s) for s in range(1, chans)]
     tables = make_tables(cycle_pixels, mode_index[:, None], slots, pixels)
+    own_pixels = lax.dynamic_slice_in_dim(cycle_pixels, chan_pos * slots, slots)
+    tables, own_pixels, parts = lax.optimization_barrier((tables, own_pixels, parts))
     chunks = add_parts(parts)
     spectra = lax.all_to_all(chunks, ("mset", "blk"), split_axis=0, concat_axis=0, tiled=True)
-    own_pixels = lax.dynamic_slice_in_dim(cycle_pixels, chan_pos * slots, slots)
     returned = middle(own_pixels, spectra, tables, inv_noise, 2048)
     own = lax.all_to_all(returned, ("mset", "blk"), split_axis=0, concat_axis=0, tiled=True)
     gathered = [own] + [shift(own, s) for s in range(1, chans)]

time: 86.4 us -> 76.6 us (0.89); the launches traced: 86.8 us -> 75.5 us
  blocking collectives: 16.6 us -> 38.3 us
  starting transfers between devices: 25.8 us -> 10 us
  local copies, waits for them, and re-layouts: 14 us -> 0.2 us
  waiting for transfers between devices: 14.4 us -> 6.49 us
  Pallas kernels: 16 us -> 20.4 us
    all_to_all x0 -> x1, blocking collectives: none -> 23.2 us  [on_device(): lax.all_to_all(chunks, ('mset', 'blk'), split_axis=0, concat_axis=0, tile...]
    unnamed x30 -> x16, local copies, waits for them, and re-layouts: 13.8 us -> 0.03 us
    all_to_all x1 -> x0, starting transfers between devices: 13.2 us -> none  [on_device(): lax.all_to_all(chunks, ('mset', 'blk'), split_axis=0, concat_axis=0, tile...]
    ppermute x6, waiting for transfers between devices: 10.9 us -> 6.49 us  [shift(): return lax.ppermute(x, 'chan', [(d, (d + s) % chans) for d in range(chans)])]
    all_to_all x1 -> x0, waiting for transfers between devices: 3.48 us -> none  [on_device(): lax.all_to_all(chunks, ('mset', 'blk'), split_axis=0, concat_axis=0, tile...]
    pallas_call x1, Pallas kernels: 5.03 us -> 7.93 us  [middle(): pl.pallas_call(functools.partial(middle_body, slots, block), grid_spec=pl...]
    ppermute x6, starting transfers between devices: 12.6 us -> 10 us  [shift(): return lax.ppermute(x, 'chan', [(d, (d + s) % chans) for d in range(chans)])]
    pallas_call x1, Pallas kernels: 2.62 us -> 4.35 us  [forward(): pl.pallas_call(functools.partial(forward_body, chans, slots, pixels), gri...]
  transfers between devices with their start and end apart: 7 -> 6, of which waited for: 4 -> 4; matrix products, arithmetic and copies ran while one was open for 0% -> 0% of each run, Pallas kernels for 4% -> 5%
where the time goes in v2:
time: 76.6 us; the launch traced here: 75.5 us
  blocking collectives  38.3 us (50%)
  Pallas kernels  20.4 us (27%)
  starting transfers between devices  10 us (13%)
  waiting for transfers between devices  6.49 us (8%)
    all_to_all x1, blocking collectives, on_device(): lax.all_to_all(chunks, ('mset', 'blk'), split_axis=0, concat_axis=0, tile...  23.2 us
    all_to_all x1, blocking collectives, on_device(): lax.all_to_all(returned, ('mset', 'blk'), split_axis=0, concat_axis=0, ti...  15.1 us
    ppermute x6, starting transfers between devices, shift(): return lax.ppermute(x, 'chan', [(d, (d + s) % chans) for d in range(chans)])  10 us
    pallas_call x1, Pallas kernels, middle(): pl.pallas_call(functools.partial(middle_body, slots, block), grid_spec=pl...  7.93 us
    ppermute x6, waiting for transfers between devices, shift(): return lax.ppermute(x, 'chan', [(d, (d + s) % chans) for d in range(chans)])  6.49 us
    pallas_call x1, Pallas kernels, forward(): pl.pallas_call(functools.partial(forward_body, chans, slots, pixels), gri...  4.35 us
    pallas_call x1, Pallas kernels, backward(): pl.pallas_call(functools.partial(backward_body, chans, slots, pixels), gr...  4.03 us
    pallas_call x1, Pallas kernels, make_tables(): pl.pallas_call(functools.partial(table_body, slots), in_specs=[whole(pltp...  3.99 us
  transfers between devices with their start and end apart: 6, of which 4 were waited for; matrix products, arithmetic and copies ran while one was open for 0% of the time, Pallas kernels for 5%

profile of v2, /device:TPU:1, one launch (start us, length us, event | category | flops | bytes accessed | tf_op | source)
XLA Modules:
  0.0 75.5 jit_solution(3002230264872454681)
XLA Ops:
  0.0 0.0 copy-start.4
  0.0 0.0 copy-start.5
  0.0 4.4 %forward.1 = (bf16[8,8192]{1,0:T(8,128)(2,1)S(1)}, bf16[8,8192]{1,0:T(8,128)(2,1)S(1)}, bf16[8,8192]{1,0:T(8,128)(2,1)S(1)}, bf16[8,8192]{1,0:T(8,128)(2,1)S(1)}) custom-call(s32[12]{0:T(128)} %npix_ref.5, f32[3,12]{1,0:T(4,128)} %bitcast.9, bf16[3,2,384]{2,1,0:T(2,128)(2,1)} %bitcast.7, f32[12,384]{1,0:T(8,128)} %beam_ref.3, bf16[1,384,8192]{2,1,0:T(8,128)(2,1)} %leg_ref.3), custom_call_target="tpu_custom_call" | custom-call | flops 201326592 | bytes 6291456 | tf_op jit(solution)/shard_map/forward/pallas_call | solution.py:63
  4.4 2.1 %collective-permute-start = (bf16[8,8192]{1,0:T(8,128)(2,1)S(1)}, bf16[8,8192]{1,0:T(8,128)(2,1)S(1)}, u32[]{:S(2)}, u32[]{:S(2)}) collective-permute-start(bf16[8,8192]{1,0:T(8,128)(2,1)S(1)} %get-tuple-element.16), channel_id=1, source_target_pairs={{0,64},{64,128},{128,192},{192,0},{1,65},{65,129},{129,193},{193,1... | collective-permute-start | bytes 393224 | tf_op jit(solution)/shard_map/ppermute | solution.py:297
  6.5 2.5 %collective-permute-start.1 = (bf16[8,8192]{1,0:T(8,128)(2,1)S(1)}, bf16[8,8192]{1,0:T(8,128)(2,1)S(1)}, u32[]{:S(2)}, u32[]{:S(2)}) collective-permute-start(bf16[8,8192]{1,0:T(8,128)(2,1)S(1)} %get-tuple-element.17), channel_id=1, source_target_pairs={{0,128},{64,192},{128,0},{192,64},{1,129},{65,193},{129,1},{193,65... | collective-permute-start | bytes 393224 | tf_op jit(solution)/shard_map/ppermute | solution.py:297
  8.9 1.1 %collective-permute-start.2 = (bf16[8,8192]{1,0:T(8,128)(2,1)S(1)}, bf16[8,8192]{1,0:T(8,128)(2,1)S(1)}, u32[]{:S(2)}, u32[]{:S(2)}) collective-permute-start(bf16[8,8192]{1,0:T(8,128)(2,1)S(1)} %get-tuple-element.18), channel_id=1, source_target_pairs={{0,192},{64,0},{128,64},{192,128},{1,193},{65,1},{129,65},{193,129... | collective-permute-start | bytes 393224 | tf_op jit(solution)/shard_map/ppermute | solution.py:297
  10.1 0.0 copy-done.4
  10.1 0.1 dynamic_slice.3.npix_ref
  10.1 0.0 copy-done.5
  10.2 0.1 copy.9.mode_ref
  10.2 4.0 %make_tables.1.table_ref = bf16[3,128,8192]{2,1,0:T(8,128)(2,1)S(1)} custom-call(s32[12]{0:T(128)S(1)} %copy-done.4, s32[64,1]{1,0:T(8,128)S(1)} %copy.9.mode_ref), custom_call_target="tpu_custom_call" | custom-call | flops 15728640 | bytes 6291456 | tf_op jit(solution)/shard_map/make_tables/pallas_call | solution.py:142
  14.2 0.0 collective-permute-done.refs_1_
  14.2 0.4 collective-permute-done.1.refs_2_
  14.6 0.0 collective-permute-done.2.refs_3_
  14.7 0.1 add_parts.1
  14.7 23.2 %all_to_all.10.spec_ref = bf16[64,8,128]{2,1,0:T(8,128)(2,1)S(1)} all-to-all(bf16[64,8,128]{2,1,0:T(8,128)(2,1)S(1)} %add_parts.1), channel_id=1, replica_groups=mesh['chan'=4,'mset'=8,'blk'=8] {'mset','blk'}, dimensions={0} | all-to-all | bytes 262144 | tf_op jit(solution)/shard_map/all_to_all | solution.py:305
  37.9 0.0 copy-start.3
  37.9 7.9 %middle.1 = bf16[64,8,128]{2,1,0:T(8,128)(2,1)S(1)} custom-call(s32[3]{0:T(128)S(1)} %dynamic_slice.3.npix_ref, bf16[64,8,128]{2,1,0:T(8,128)(2,1)S(1)} %all_to_all.10.spec_ref, bf16[3,128,8192]{2,1,0:T(8,128)(2,1)S(1)} %make_tables.1.table_ref, bf16[3,128,8192]{2,1,0:T(8,128)(2,1)} %noise_ref.1), custom_call_target="tpu_custom_call" | custom-call | tf_op jit(solution)/shard_map/middle/pallas_call | solution.py:204
  45.9 15.1 %all_to_all.11.rest_0_ = bf16[64,8,128]{2,1,0:T(8,128)(2,1)S(1)} all-to-all(bf16[64,8,128]{2,1,0:T(8,128)(2,1)S(1)} %middle.1), channel_id=1, replica_groups=mesh['chan'=4,'mset'=8,'blk'=8] {'mset','blk'}, dimensions={0} | all-to-all | bytes 262144 | tf_op jit(solution)/shard_map/all_to_all | solution.py:307
  60.9 0.5 collective-permute-start.5
  61.4 3.9 %collective-permute-start.4 = (bf16[64,8,128]{2,1,0:T(8,128)(2,1)S(1)}, bf16[64,8,128]{2,1,0:T(8,128)(2,1)S(1)}, u32[]{:S(2)}, u32[]{:S(2)}) collective-permute-start(bf16[64,8,128]{2,1,0:T(8,128)(2,1)S(1)} %all_to_all.11.rest_0_), channel_id=1, source_target_pairs={{0,128},{64,192},{128,0},{192,64},{1,129},{65,193},{129,1},{193,65... | collective-permute-start | bytes 393224 | tf_op jit(solution)/shard_map/ppermute | solution.py:297
  65.3 0.0 collective-permute-start.3
  65.3 0.6 collective-permute-done.5.rest_3_
  65.8 1.8 %collective-permute-done.4.rest_2_ = bf16[64,8,128]{2,1,0:T(8,128)(2,1)S(1)} collective-permute-done((bf16[64,8,128]{2,1,0:T(8,128)(2,1)S(1)}, bf16[64,8,128]{2,1,0:T(8,128)(2,1)S(1)}, u32[]{:S(2)}, u32[]{:S(2)}) %collective-permute-start.4) | collective-permute-done | bytes 131104 | tf_op jit(solution)/shard_map/ppermute | solution.py:297
  67.6 3.7 %collective-permute-done.3.rest_1_ = bf16[64,8,128]{2,1,0:T(8,128)(2,1)S(1)} collective-permute-done((bf16[64,8,128]{2,1,0:T(8,128)(2,1)S(1)}, bf16[64,8,128]{2,1,0:T(8,128)(2,1)S(1)}, u32[]{:S(2)}, u32[]{:S(2)}) %collective-permute-start.3) | collective-permute-done | bytes 131104 | tf_op jit(solution)/shard_map/ppermute | solution.py:297
  71.4 0.0 slice-done
  71.4 0.0 slice-done.1
  71.4 0.0 copy-done
  71.4 0.0 copy-done.1
  71.4 0.0 copy-done.2
  71.4 0.0 copy-done.3
  71.4 4.0 %backward.1 = f32[2,3,1,384]{3,2,1,0:T(1,128)} custom-call(s32[12]{0:T(128)S(1)} %copy-done.4, f32[3,12]{1,0:T(4,128)S(1)} %bitcast.10, bf16[3,2,384]{2,1,0:T(2,128)(2,1)S(1)} %bitcast.8, f32[12,384]{1,0:T(8,128)S(1)} %copy-done, f32[3,384]{1,0:T(4,128)S(1)} %copy-done.3, bf16[1,384,8192]{2,1,0:T(8,128)(2,1)S(1)} %bitcast.6, ...), custom_call_target="tpu_custom_call" | custom-call | tf_op jit(solution)/shard_map/backward/pallas_call | solution.py:267
  (6 shorter events, 0.0 us)
Async XLA Ops:
  0.0 10.1 %copy-start.4 = (s32[12]{0:T(128)S(1)}, s32[12]{0:T(128)}, u32[]{:S(2)}) copy-start(s32[12]{0:T(128)} %npix_ref.5) | copy-start | bytes 148
  0.0 10.1 %copy-start.5 = (s32[64]{0:T(128)S(1)}, s32[64]{0:T(128)}, u32[]{:S(2)}) copy-start(s32[64]{0:T(128)} %param.14) | copy-start | bytes 772
  4.4 9.9 %collective-permute-start = (bf16[8,8192]{1,0:T(8,128)(2,1)S(1)}, bf16[8,8192]{1,0:T(8,128)(2,1)S(1)}, u32[]{:S(2)}, u32[]{:S(2)}) collective-permute-start(bf16[8,8192]{1,0:T(8,128)(2,1)S(1)} %get-tuple-element.16), channel_id=1, source_target_pairs={{0,64},{64,128},{128,192},{192,0},{1,65},{65,129},{129,193},{193,1... | collective-permute-start | bytes 393224 | tf_op jit(solution)/shard_map/ppermute | solution.py:297
  6.5 8.2 %collective-permute-start.1 = (bf16[8,8192]{1,0:T(8,128)(2,1)S(1)}, bf16[8,8192]{1,0:T(8,128)(2,1)S(1)}, u32[]{:S(2)}, u32[]{:S(2)}) collective-permute-start(bf16[8,8192]{1,0:T(8,128)(2,1)S(1)} %get-tuple-element.17), channel_id=1, source_target_pairs={{0,128},{64,192},{128,0},{192,64},{1,129},{65,193},{129,1},{193,65... | collective-permute-start | bytes 393224 | tf_op jit(solution)/shard_map/ppermute | solution.py:297
  8.9 5.7 %collective-permute-start.2 = (bf16[8,8192]{1,0:T(8,128)(2,1)S(1)}, bf16[8,8192]{1,0:T(8,128)(2,1)S(1)}, u32[]{:S(2)}, u32[]{:S(2)}) collective-permute-start(bf16[8,8192]{1,0:T(8,128)(2,1)S(1)} %get-tuple-element.18), channel_id=1, source_target_pairs={{0,192},{64,0},{128,64},{192,128},{1,193},{65,1},{129,65},{193,129... | collective-permute-start | bytes 393224 | tf_op jit(solution)/shard_map/ppermute | solution.py:297
  14.6 56.7 %slice-start = ((s8[6291456]{0:T(1024)(128)(4,1)}), s8[4194304]{0:T(1024)(128)(4,1)S(1)}, s32[]{:S(2)}) async-start(s8[6291456]{0:T(1024)(128)(4,1)} %bitcast.5), calls=%async_computation.2 | async-start | bytes 8388608
  37.9 33.4 %slice-start.1 = ((s8[6291456]{0:T(1024)(128)(4,1)}), s8[2097152]{0:T(1024)(128)(4,1)S(1)}, s32[]{:S(2)}) async-start(s8[6291456]{0:T(1024)(128)(4,1)} %bitcast.5), calls=%async_computation.3 | async-start | bytes 4194304
  37.9 33.4 %copy-start = (f32[12,384]{1,0:T(8,128)S(1)}, f32[12,384]{1,0:T(8,128)}, u32[]{:S(2)}) copy-start(f32[12,384]{1,0:T(8,128)} %beam_ref.3) | copy-start | bytes 55300
  37.9 33.5 %copy-start.1 = (bf16[2,3,1,384]{3,0,2,1:T(2,128)(2,1)S(1)}, bf16[2,3,1,384]{3,0,2,1:T(2,128)(2,1)}, u32[]{:S(2)}) copy-start(bf16[2,3,1,384]{3,0,2,1:T(2,128)(2,1)} %param.8) | copy-start | bytes 13828
  37.9 33.5 %copy-start.2 = (f32[12,3]{0,1:T(4,128)S(1)}, f32[12,3]{0,1:T(4,128)}, u32[]{:S(2)}) copy-start(f32[12,3]{0,1:T(4,128)} %param.9) | copy-start | bytes 436
  37.9 33.5 %copy-start.3 = (f32[3,384]{1,0:T(4,128)S(1)}, f32[3,384]{1,0:T(4,128)}, u32[]{:S(2)}) copy-start(f32[3,384]{1,0:T(4,128)} %prior_ref.1) | copy-start | bytes 13828
  60.9 4.9 %collective-permute-start.5 = (bf16[64,8,128]{2,1,0:T(8,128)(2,1)S(1)}, bf16[64,8,128]{2,1,0:T(8,128)(2,1)S(1)}, u32[]{:S(2)}, u32[]{:S(2)}) collective-permute-start(bf16[64,8,128]{2,1,0:T(8,128)(2,1)S(1)} %all_to_all.11.rest_0_), channel_id=1, source_target_pairs={{0,192},{64,0},{128,64},{192,128},{1,193},{65,1},{129,65},{193,129... | collective-permute-start | bytes 393224 | tf_op jit(solution)/shard_map/ppermute | solution.py:297
  61.4 6.2 %collective-permute-start.4 = (bf16[64,8,128]{2,1,0:T(8,128)(2,1)S(1)}, bf16[64,8,128]{2,1,0:T(8,128)(2,1)S(1)}, u32[]{:S(2)}, u32[]{:S(2)}) collective-permute-start(bf16[64,8,128]{2,1,0:T(8,128)(2,1)S(1)} %all_to_all.11.rest_0_), channel_id=1, source_target_pairs={{0,128},{64,192},{128,0},{192,64},{1,129},{65,193},{129,1},{193,65... | collective-permute-start | bytes 393224 | tf_op jit(solution)/shard_map/ppermute | solution.py:297
  65.3 6.1 %collective-permute-start.3 = (bf16[64,8,128]{2,1,0:T(8,128)(2,1)S(1)}, bf16[64,8,128]{2,1,0:T(8,128)(2,1)S(1)}, u32[]{:S(2)}, u32[]{:S(2)}) collective-permute-start(bf16[64,8,128]{2,1,0:T(8,128)(2,1)S(1)} %all_to_all.11.rest_0_), channel_id=1, source_target_pairs={{0,64},{64,128},{128,192},{192,0},{1,65},{65,129},{129,193},{193,1... | collective-permute-start | bytes 393224 | tf_op jit(solution)/shard_map/ppermute | solution.py:297

commit v3 on v2

v3 whole, which is shorter than its diff:
```python
import functools
import math

import jax
import jax.numpy as jnp
from jax import lax
from jax.experimental import pallas as pl
from jax.experimental.pallas import tpu as pltpu
from jax.sharding import PartitionSpec as P

MIB = 1 << 20
LANES = 128
ROWS = 8
QUARTERS = 4


def whole(space=pltpu.VMEM):
    return pl.BlockSpec(memory_space=space)


def in_hbm(*arrays):
    return [pltpu.with_memory_space_constraint(x, pltpu.HBM) for x in arrays]


def in_vmem(*arrays):
    return [pltpu.with_memory_space_constraint(x, pltpu.VMEM) for x in arrays]


def filter_row(beam_ref, npix_ref, channel, degrees, total_deg, pixels):
    band_limit = total_deg * npix_ref[channel] // pixels - 1
    return jnp.where(degrees <= band_limit, beam_ref[pl.ds(channel, 1), :], 0.0)


def degrees_of(shape, chan_pos):
    return chan_pos * shape[-1] + lax.broadcasted_iota(jnp.int32, shape, len(shape) - 1)


def forward_body(chans, slots, pixels, steps, npix_any, mix_any, harm_any, beam_any, leg_any, *rest):
    outs = rest[:chans]
    npix_ref, mix_ref, harm_ref, beam_ref, rows_ref, leg_ref, sems, small = rest[chans:]
    small_copies = [
        pltpu.make_async_copy(src, dst, small.at[n])
        for n, (src, dst) in enumerate(
            [
                (npix_any, npix_ref),
                (mix_any, mix_ref),
                (harm_any, harm_ref),
                (beam_any, beam_ref),
            ]
        )
    ]
    local_deg, cycles = leg_ref.shape
    block = cycles // steps
    copies = [
        pltpu.make_async_copy(
            leg_any.at[0, :, pl.ds(q * block, block)],
            leg_ref.at[:, pl.ds(q * block, block)],
            sems.at[q],
        )
        for q in range(steps)
    ]
    for copy in small_copies + copies:
        copy.start()
    for copy in small_copies:
        copy.wait()
    chan_pos = lax.axis_index("chan")
    degrees = degrees_of((1, local_deg), chan_pos)
    comps = [harm_ref[k].astype(jnp.float32) for k in range(harm_ref.shape[0])]
    for s in range(chans):
        group = (chan_pos + s) % chans
        for j in range(slots):
            c = group * slots + j
            mixture = sum(mix_ref[k, c] * comps[k] for k in range(len(comps)))
            filt = filter_row(beam_ref, npix_ref, c, degrees, local_deg * chans, pixels)
            rows_ref[pl.ds(s * ROWS + 2 * j, 2), :] = mixture * filt
        rest_rows = ROWS - 2 * slots
        rows_ref[pl.ds(s * ROWS + 2 * slots, rest_rows), :] = jnp.zeros(
            (rest_rows, local_deg), jnp.float32
        )
    rows = rows_ref[...].astype(jnp.bfloat16)
    used = 2 * slots
    for q in range(steps):
        copies[q].wait()
        partial = jnp.dot(
            rows, leg_ref[:, q * block : (q + 1) * block], preferred_element_type=jnp.float32
        )
        for s in range(chans):
            outs[s][q * used : (q + 1) * used, :] = partial[s * ROWS : s * ROWS + used].astype(
                jnp.bfloat16
            )


def forward(npix, mixing_t, harm, beam, legendre, chans, slots, pixels):
    _, local_deg, cycles = legendre.shape
    used = 2 * slots
    return pl.pallas_call(
        functools.partial(forward_body, chans, slots, pixels, QUARTERS),
        in_specs=[whole(pl.ANY)] * 5,
        out_specs=[whole()] * chans,
        out_shape=[jax.ShapeDtypeStruct((QUARTERS * used, cycles // QUARTERS), jnp.bfloat16)] * chans,
        scratch_shapes=[
            pltpu.SMEM(npix.shape, npix.dtype),
            pltpu.SMEM(mixing_t.shape, mixing_t.dtype),
            pltpu.VMEM(harm.shape, harm.dtype),
            pltpu.VMEM(beam.shape, beam.dtype),
            pltpu.VMEM((chans * ROWS, local_deg), jnp.float32),
            pltpu.VMEM((local_deg, cycles), jnp.bfloat16),
            pltpu.SemaphoreType.DMA((QUARTERS,)),
            pltpu.SemaphoreType.DMA((4,)),
        ],
        compiler_params=pltpu.CompilerParams(vmem_limit_bytes=16 * MIB),
        cost_estimate=pl.CostEstimate(
            flops=2 * chans * ROWS * local_deg * cycles,
            bytes_accessed=2 * local_deg * cycles,
            transcendentals=0,
        ),
        name="forward",
    )(*in_hbm(npix, mixing_t, harm, beam, legendre))


def gather_body(used, *refs):
    out_ref = refs[-1]
    total = refs[0][...].astype(jnp.float32)
    for ref in refs[1:-1]:
        total = total + ref[...].astype(jnp.float32)
    width = total.shape[1]
    per = width // LANES
    pad = jnp.zeros((ROWS - used, width), jnp.float32)
    for q in range(total.shape[0] // used):
        part = jnp.concatenate([total[q * used : (q + 1) * used], pad], axis=0).astype(jnp.bfloat16)
        for b in range(per):
            out_ref[q * per + b] = part[:, b * LANES : (b + 1) * LANES]


def add_parts(parts):
    height, width = parts[0].shape
    used = height // QUARTERS
    return pl.pallas_call(
        functools.partial(gather_body, used),
        in_specs=[whole()] * len(parts),
        out_specs=whole(),
        out_shape=jax.ShapeDtypeStruct((QUARTERS * width // LANES, ROWS, LANES), jnp.bfloat16),
        compiler_params=pltpu.CompilerParams(vmem_limit_bytes=8 * MIB),
        name="add_parts",
    )(*parts)


def table_body(slots, npix_ref, mode_ref, noise_any, out_ref, noise_ref, sems):
    chan_pos = lax.axis_index("chan")
    modes = mode_ref[...]
    mode_count = modes.shape[0]
    pixels = out_ref.shape[2]
    coarse_count = pixels // LANES
    quarter = pixels // 4

    def noise_copy(j, q):
        cols = pl.ds(q * quarter, quarter)
        return pltpu.make_async_copy(noise_any.at[j, :, cols], noise_ref.at[j, :, cols], sems.at[j, q])

    for j in range(slots):
        for q in range(4):

            @pl.when(q * quarter < npix_ref[chan_pos * slots + j])
            def _():
                noise_copy(j, q).start()

    weight = jnp.where(modes == 0, 1.0, 2.0).astype(jnp.float32) / math.sqrt(2 * mode_count)
    lane = lax.broadcasted_iota(jnp.int32, (mode_count, LANES), 1)
    for j in range(slots):
        npix = npix_ref[chan_pos * slots + j]
        scale = jnp.float32(jnp.pi) / npix.astype(jnp.float32)
        fine_phase = ((modes * (2 * lane + 1)) & (2 * npix - 1)).astype(jnp.float32) * scale
        coarse_phase = ((modes * (2 * LANES * lane)) & (2 * npix - 1)).astype(jnp.float32) * scale
        fine_cos = jnp.cos(fine_phase) * weight
        fine_sin = jnp.sin(fine_phase) * weight
        coarse_cos = jnp.cos(coarse_phase)
        coarse_sin = jnp.sin(coarse_phase)
        for q in range(4):

            @pl.when(q * quarter < npix)
            def _():
                for a in range(q * coarse_count // 4, (q + 1) * coarse_count // 4):
                    cc = coarse_cos[:, a : a + 1]
                    cs = coarse_sin[:, a : a + 1]
                    cols = slice(a * LANES, (a + 1) * LANES)
                    cos_part = cc * fine_cos - cs * fine_sin
                    sin_part = -(cs * fine_cos + cc * fine_sin)
                    out_ref[j, :mode_count, cols] = cos_part.astype(jnp.bfloat16)
                    out_ref[j, mode_count:, cols] = sin_part.astype(jnp.bfloat16)

    for j in range(slots):
        for q in range(4):

            @pl.when(q * quarter < npix_ref[chan_pos * slots + j])
            def _():
                noise_copy(j, q).wait()


def make_tables(npix, modes, inv_noise):
    slots, _, pixels = inv_noise.shape
    mode_count = modes.shape[0]
    return pl.pallas_call(
        functools.partial(table_body, slots),
        in_specs=[whole(pltpu.SMEM), whole(), whole(pl.ANY)],
        out_specs=[whole(), whole()],
        out_shape=[
            pltpu.VMEM((slots, 2 * mode_count, pixels), jnp.bfloat16),
            pltpu.VMEM(inv_noise.shape, jnp.bfloat16),
        ],
        scratch_shapes=[pltpu.SemaphoreType.DMA((slots, 4))],
        compiler_params=pltpu.CompilerParams(vmem_limit_bytes=16 * MIB),
        cost_estimate=pl.CostEstimate(
            flops=10 * slots * mode_count * pixels,
            bytes_accessed=4 * slots * mode_count * pixels,
            transcendentals=4 * slots * mode_count * LANES,
        ),
        name="make_tables",
    )(npix, modes, *in_hbm(inv_noise))


def middle_body(npix_ref, spec_ref, table_ref, noise_ref, out_ref, full_ref, turned_ref):
    mode_count = spec_ref.shape[0]
    slots, _, pixels = noise_ref.shape
    flat = mode_count * ROWS
    chan_pos = lax.axis_index("chan")
    full_ref[...] = spec_ref[...].reshape(flat, LANES).astype(jnp.float32)
    for s in range(slots):
        halves = [full_ref[pl.ds(2 * s + i, mode_count, stride=ROWS), :] for i in range(2)]
        turned_ref[s] = jnp.concatenate(halves, axis=0).T.astype(jnp.bfloat16)
    full_ref[...] = jnp.zeros((flat, LANES), jnp.float32)

    def one_channel(j, carry):
        spectra = turned_ref[j]
        npix = npix_ref[chan_pos * slots + j]
        for width in (pixels // 4, pixels // 2, pixels):

            @pl.when(npix == width)
            def _():
                table = table_ref[j, :, :width]
                sky = jnp.dot(spectra, table, preferred_element_type=jnp.float32)
                noisy = (noise_ref[j, :, :width].astype(jnp.float32) * sky).astype(jnp.bfloat16)
                back = lax.dot_general(
                    table, noisy, (((1,), (1,)), ((), ())), preferred_element_type=jnp.float32
                )
                for i in range(2):
                    full_ref[pl.ds(2 * j + i, mode_count, stride=ROWS), :] = back[
                        i * mode_count : (i + 1) * mode_count
                    ]

        return carry

    lax.fori_loop(0, slots, one_channel, 0)
    out_ref[...] = full_ref[...].reshape(mode_count, ROWS, LANES).astype(jnp.bfloat16)


def middle(npix, spectra, tables, noise):
    slots, cycle_dev, _ = noise.shape
    mode_count = spectra.shape[0]
    return pl.pallas_call(
        middle_body,
        in_specs=[whole(pltpu.SMEM), whole(), whole(), whole()],
        out_specs=whole(),
        out_shape=jax.ShapeDtypeStruct(spectra.shape, jnp.bfloat16),
        scratch_shapes=[
            pltpu.VMEM((mode_count * ROWS, LANES), jnp.float32),
            pltpu.VMEM((slots, cycle_dev, 2 * mode_count), jnp.bfloat16),
        ],
        compiler_params=pltpu.CompilerParams(vmem_limit_bytes=20 * MIB),
        name="middle",
    )(npix, spectra, *in_vmem(tables, noise))


def backward_body(chans, slots, pixels, npix_ref, mix_ref, harm_ref, beam_ref, prior_ref, leg_ref, *rest):
    parts, out_ref, acc_ref = rest[:chans], rest[chans], rest[chans + 1]
    rows = [
        jnp.concatenate([part[b] for b in range(part.shape[0])], axis=1) for part in parts
    ]
    rows = jnp.concatenate(rows, axis=0)
    acc_ref[...] = lax.dot_general(
        leg_ref[0], rows, (((1,), (1,)), ((), ())), preferred_element_type=jnp.float32
    ).T
    chan_pos = lax.axis_index("chan")
    local_deg = beam_ref.shape[1]
    degrees = degrees_of((1, local_deg), chan_pos)
    comps = harm_ref.shape[0]
    totals = [prior_ref[k : k + 1, :] * harm_ref[k].astype(jnp.float32) for k in range(comps)]
    for s in range(chans):
        group = (chan_pos + chans - s) % chans
        for j in range(slots):
            c = group * slots + j
            filt = filter_row(beam_ref, npix_ref, c, degrees, local_deg * chans, pixels)
            weighted = acc_ref[pl.ds(s * ROWS + 2 * j, 2), :] * filt
            for k in range(comps):
                totals[k] = totals[k] + mix_ref[k, c] * weighted
    for k in range(comps):
        for i in range(2):
            out_ref[i, k] = totals[k][i : i + 1]


def backward(npix, mixing_t, harm, beam, prior, legendre, parts, slots, pixels):
    chans = len(parts)
    local_deg = legendre.shape[1]
    comps = harm.shape[0]
    return pl.pallas_call(
        functools.partial(backward_body, chans, slots, pixels),
        in_specs=[whole(pltpu.SMEM), whole(pltpu.SMEM)] + [whole()] * (4 + chans),
        out_specs=whole(),
        out_shape=jax.ShapeDtypeStruct((2, comps, 1, local_deg), jnp.float32),
        scratch_shapes=[pltpu.VMEM((chans * ROWS, local_deg), jnp.float32)],
        compiler_params=pltpu.CompilerParams(vmem_limit_bytes=16 * MIB),
        name="backward",
    )(npix, mixing_t, harm, beam, prior, legendre, *parts)


def on_device(
    harmonics, mixing, beam_window, prior_inv, legendre, inv_noise, mode_index, cycle_pixels
):
    chans = lax.axis_size("chan")
    slots, _, pixels = inv_noise.shape
    mixing_t = mixing.T
    harm = harmonics[:, :, 0, :].transpose(1, 0, 2)

    def shift(x, s):
        return lax.ppermute(x, "chan", [(d, (d + s) % chans) for d in range(chans)])

    parts = forward(
        cycle_pixels, mixing_t, harm, beam_window, legendre, chans, slots, pixels
    )
    parts = [parts[0]] + [shift(parts[s], s) for s in range(1, chans)]
    tables, noise = make_tables(cycle_pixels, mode_index[:, None], inv_noise)
    tables, noise, parts = lax.optimization_barrier((tables, noise, parts))
    chunks = add_parts(parts)
    spectra = lax.all_to_all(chunks, ("mset", "blk"), split_axis=0, concat_axis=0, tiled=True)
    returned = middle(cycle_pixels, spectra, tables, noise)
    own = lax.all_to_all(returned, ("mset", "blk"), split_axis=0, concat_axis=0, tiled=True)
    gathered = [own] + [shift(own, s) for s in range(1, chans)]
    return backward(
        cycle_pixels, mixing_t, harm, beam_window, prior_inv, legendre, gathered, slots, pixels
    )


def solution(mesh):
    placed = (
        P(None, None, ("mset", "blk"), "chan"),
        P(),
        P(None, "chan"),
        P(None, "chan"),
        P(("mset", "blk"), "chan", None),
        P("chan", ("mset", "blk"), None),
        P(),
        P(),
    )
    return jax.shard_map(
        on_device,
        mesh=mesh,
        in_specs=placed,
        out_specs=P(None, None, ("mset", "blk"), "chan"),
        check_vma=False,
    )
```

time: 76.6 us -> 69.6 us (0.909); the launches traced: 75.5 us -> 69.7 us
  Pallas kernels: 20.4 us -> 15.4 us
  starting transfers between devices: 10 us -> 8.06 us
  waiting for transfers between devices: 6.49 us -> 7.76 us
    pallas_call x4, Pallas kernels: 16.4 us -> 10.9 us  [the longest x1 3.98 us: forward(): pl.pallas_call(functools.partial(forward_body, chans, slots, pixels, QUAR...]
    ppermute x6, starting transfers between devices: 10 us -> 8.06 us  [shift(): return lax.ppermute(x, 'chan', [(d, (d + s) % chans) for d in range(chans)])]
    ppermute x6, waiting for transfers between devices: 6.49 us -> 7.76 us  [shift(): return lax.ppermute(x, 'chan', [(d, (d + s) % chans) for d in range(chans)])]
  transfers between devices with their start and end apart: 6 -> 6, of which waited for: 4 -> 3; matrix products, arithmetic and copies ran while one was open for 0% -> 0% of each run, Pallas kernels for 5% -> 6%
where the time goes in v3:
time: 69.6 us; the launch traced here: 69.7 us
  blocking collectives  38.2 us (55%)
  Pallas kernels  15.4 us (22%)
  starting transfers between devices  8.06 us (12%)
  waiting for transfers between devices  7.76 us (11%)
    all_to_all x1, blocking collectives, on_device(): lax.all_to_all(chunks, ('mset', 'blk'), split_axis=0, concat_axis=0, tile...  23.2 us
    all_to_all x1, blocking collectives, on_device(): lax.all_to_all(returned, ('mset', 'blk'), split_axis=0, concat_axis=0, ti...  15 us
    ppermute x6, starting transfers between devices, shift(): return lax.ppermute(x, 'chan', [(d, (d + s) % chans) for d in range(chans)])  8.06 us
    ppermute x6, waiting for transfers between devices, shift(): return lax.ppermute(x, 'chan', [(d, (d + s) % chans) for d in range(chans)])  7.76 us
    pallas_call x1, Pallas kernels, make_tables(): pl.pallas_call(functools.partial(table_body, slots), in_specs=[whole(pltp...  4.5 us
    pallas_call x1, Pallas kernels, forward(): pl.pallas_call(functools.partial(forward_body, chans, slots, pixels, QUAR...  3.98 us
    pallas_call x1, Pallas kernels, middle(): pl.pallas_call(middle_body, in_specs=[whole(pltpu.SMEM), whole(), whole()...  3.78 us
    pallas_call x1, Pallas kernels, backward(): pl.pallas_call(functools.partial(backward_body, chans, slots, pixels), in...  3.04 us
  transfers between devices with their start and end apart: 6, of which 3 were waited for; matrix products, arithmetic and copies ran while one was open for 0% of the time, Pallas kernels for 6%

profile of v3, /device:TPU:1, one launch (start us, length us, event | category | flops | bytes accessed | tf_op | source)
XLA Modules:
  0.0 69.7 jit_solution(17278745847826856734)
XLA Ops:
  0.0 0.0 copy-start.3
  0.0 0.0 copy-start.5
  0.0 4.0 %forward.1 = (bf16[24,2048]{1,0:T(8,128)(2,1)S(1)}, bf16[24,2048]{1,0:T(8,128)(2,1)S(1)}, bf16[24,2048]{1,0:T(8,128)(2,1)S(1)}, bf16[24,2048]{1,0:T(8,128)(2,1)S(1)}) custom-call(s32[12]{0:T(128)} %npix_ref.5, f32[3,12]{1,0:T(4,128)} %bitcast.9, bf16[3,2,384]{2,1,0:T(2,128)(2,1)} %bitcast.7, f32[12,384]{1,0:T(8,128)} %beam_ref.1, bf16[1,384,8192]{2,1,0:T(8,128)(2,1)} %leg_ref.1), custom_call_target="tpu_custom_call" | custom-call | flops 201326592 | bytes 6291456 | tf_op jit(solution)/shard_map/forward/pallas_call | solution.py:96
  4.0 2.1 %collective-permute-start = (bf16[24,2048]{1,0:T(8,128)(2,1)S(1)}, bf16[24,2048]{1,0:T(8,128)(2,1)S(1)}, u32[]{:S(2)}, u32[]{:S(2)}) collective-permute-start(bf16[24,2048]{1,0:T(8,128)(2,1)S(1)} %get-tuple-element.20), channel_id=1, source_target_pairs={{0,64},{64,128},{128,192},{192,0},{1,65},{65,129},{129,193},{193,1... | collective-permute-start | bytes 294920 | tf_op jit(solution)/shard_map/ppermute | solution.py:324
  6.1 2.5 %collective-permute-start.1 = (bf16[24,2048]{1,0:T(8,128)(2,1)S(1)}, bf16[24,2048]{1,0:T(8,128)(2,1)S(1)}, u32[]{:S(2)}, u32[]{:S(2)}) collective-permute-start(bf16[24,2048]{1,0:T(8,128)(2,1)S(1)} %get-tuple-element.21), channel_id=1, source_target_pairs={{0,128},{64,192},{128,0},{192,64},{1,129},{65,193},{129,1},{193,65... | collective-permute-start | bytes 294920 | tf_op jit(solution)/shard_map/ppermute | solution.py:324
  8.5 1.1 %collective-permute-start.2 = (bf16[24,2048]{1,0:T(8,128)(2,1)S(1)}, bf16[24,2048]{1,0:T(8,128)(2,1)S(1)}, u32[]{:S(2)}, u32[]{:S(2)}) collective-permute-start(bf16[24,2048]{1,0:T(8,128)(2,1)S(1)} %get-tuple-element.22), channel_id=1, source_target_pairs={{0,192},{64,0},{128,64},{192,128},{1,193},{65,1},{129,65},{193,129... | collective-permute-start | bytes 294920 | tf_op jit(solution)/shard_map/ppermute | solution.py:324
  9.7 0.0 copy-done.5
  9.7 0.1 copy.9.mode_ref
  9.8 0.0 copy-done.3
  9.8 4.5 %make_tables.1 = (bf16[3,128,8192]{2,1,0:T(8,128)(2,1)S(1)}, bf16[3,128,8192]{2,1,0:T(8,128)(2,1)S(1)}) custom-call(s32[12]{0:T(128)S(1)} %copy-done.3, s32[64,1]{1,0:T(8,128)S(1)} %copy.9.mode_ref, bf16[3,128,8192]{2,1,0:T(8,128)(2,1)} %noise_any.1), custom_call_target="tpu_custom_call" | custom-call | flops 15728640 | bytes 6291456 | tf_op jit(solution)/shard_map/make_tables/pallas_call | solution.py:202
  14.3 0.0 collective-permute-done.refs_1_
  14.3 0.0 collective-permute-done.1.refs_2_
  14.3 0.0 collective-permute-done.2.refs_3_
  14.3 0.0 slice-start
  14.3 0.1 add_parts.1
  14.4 23.2 %all_to_all.10.spec_ref = bf16[64,8,128]{2,1,0:T(8,128)(2,1)S(1)} all-to-all(bf16[64,8,128]{2,1,0:T(8,128)(2,1)S(1)} %add_parts.1), channel_id=1, replica_groups=mesh['chan'=4,'mset'=8,'blk'=8] {'mset','blk'}, dimensions={0} | all-to-all | bytes 262144 | tf_op jit(solution)/shard_map/all_to_all | solution.py:333
  37.6 0.0 copy-start.4
  37.6 3.8 %middle.1 = bf16[64,8,128]{2,1,0:T(8,128)(2,1)S(1)} custom-call(s32[12]{0:T(128)S(1)} %copy-done.3, bf16[64,8,128]{2,1,0:T(8,128)(2,1)S(1)} %all_to_all.10.spec_ref, bf16[3,128,8192]{2,1,0:T(8,128)(2,1)S(1)} %get-tuple-element.27.table_ref, bf16[3,128,8192]{2,1,0:T(8,128)(2,1)S(1)} %get-tuple-element.28.noise_ref), custom_call_target="tpu_custom_call" | custom-call | tf_op jit(solution)/shard_map/middle/pallas_call | solution.py:259
  41.4 15.0 %all_to_all.11.rest_0_ = bf16[64,8,128]{2,1,0:T(8,128)(2,1)S(1)} all-to-all(bf16[64,8,128]{2,1,0:T(8,128)(2,1)S(1)} %middle.1), channel_id=1, replica_groups=mesh['chan'=4,'mset'=8,'blk'=8] {'mset','blk'}, dimensions={0} | all-to-all | bytes 262144 | tf_op jit(solution)/shard_map/all_to_all | solution.py:335
  56.5 1.2 %collective-permute-start.5 = (bf16[64,8,128]{2,1,0:T(8,128)(2,1)S(1)}, bf16[64,8,128]{2,1,0:T(8,128)(2,1)S(1)}, u32[]{:S(2)}, u32[]{:S(2)}) collective-permute-start(bf16[64,8,128]{2,1,0:T(8,128)(2,1)S(1)} %all_to_all.11.rest_0_), channel_id=1, source_target_pairs={{0,192},{64,0},{128,64},{192,128},{1,193},{65,1},{129,65},{193,129... | collective-permute-start | bytes 393224 | tf_op jit(solution)/shard_map/ppermute | solution.py:324
  57.7 0.3 collective-permute-start.4
  58.0 0.9 %collective-permute-start.3 = (bf16[64,8,128]{2,1,0:T(8,128)(2,1)S(1)}, bf16[64,8,128]{2,1,0:T(8,128)(2,1)S(1)}, u32[]{:S(2)}, u32[]{:S(2)}) collective-permute-start(bf16[64,8,128]{2,1,0:T(8,128)(2,1)S(1)} %all_to_all.11.rest_0_), channel_id=1, source_target_pairs={{0,64},{64,128},{128,192},{192,0},{1,65},{65,129},{129,193},{193,1... | collective-permute-start | bytes 393224 | tf_op jit(solution)/shard_map/ppermute | solution.py:324
  58.8 1.5 %collective-permute-done.5.rest_3_ = bf16[64,8,128]{2,1,0:T(8,128)(2,1)S(1)} collective-permute-done((bf16[64,8,128]{2,1,0:T(8,128)(2,1)S(1)}, bf16[64,8,128]{2,1,0:T(8,128)(2,1)S(1)}, u32[]{:S(2)}, u32[]{:S(2)}) %collective-permute-start.5) | collective-permute-done | bytes 131104 | tf_op jit(solution)/shard_map/ppermute | solution.py:324
  60.3 2.8 %collective-permute-done.4.rest_2_ = bf16[64,8,128]{2,1,0:T(8,128)(2,1)S(1)} collective-permute-done((bf16[64,8,128]{2,1,0:T(8,128)(2,1)S(1)}, bf16[64,8,128]{2,1,0:T(8,128)(2,1)S(1)}, u32[]{:S(2)}, u32[]{:S(2)}) %collective-permute-start.4) | collective-permute-done | bytes 131104 | tf_op jit(solution)/shard_map/ppermute | solution.py:324
  63.1 3.5 %collective-permute-done.3.rest_1_ = bf16[64,8,128]{2,1,0:T(8,128)(2,1)S(1)} collective-permute-done((bf16[64,8,128]{2,1,0:T(8,128)(2,1)S(1)}, bf16[64,8,128]{2,1,0:T(8,128)(2,1)S(1)}, u32[]{:S(2)}, u32[]{:S(2)}) %collective-permute-start.3) | collective-permute-done | bytes 131104 | tf_op jit(solution)/shard_map/ppermute | solution.py:324
  66.6 0.0 slice-done
  66.6 0.0 slice-done.1
  66.6 0.0 copy-done
  66.6 0.0 copy-done.1
  66.6 0.0 copy-done.2
  66.6 0.0 copy-done.4
  66.6 3.0 %backward.1 = f32[2,3,1,384]{3,2,1,0:T(1,128)} custom-call(s32[12]{0:T(128)S(1)} %copy-done.3, f32[3,12]{1,0:T(4,128)S(1)} %bitcast.10, bf16[3,2,384]{2,1,0:T(2,128)(2,1)S(1)} %bitcast.8, f32[12,384]{1,0:T(8,128)S(1)} %copy-done, f32[3,384]{1,0:T(4,128)S(1)} %copy-done.4, bf16[1,384,8192]{2,1,0:T(8,128)(2,1)S(1)} %bitcast.6, ...), custom_call_target="tpu_custom_call" | custom-call | tf_op jit(solution)/shard_map/backward/pallas_call | solution.py:304
  (5 shorter events, 0.0 us)
Async XLA Ops:
  0.0 9.8 %copy-start.3 = (s32[12]{0:T(128)S(1)}, s32[12]{0:T(128)}, u32[]{:S(2)}) copy-start(s32[12]{0:T(128)} %npix_ref.5) | copy-start | bytes 148
  0.0 9.7 %copy-start.5 = (s32[64]{0:T(128)S(1)}, s32[64]{0:T(128)}, u32[]{:S(2)}) copy-start(s32[64]{0:T(128)} %param.14) | copy-start | bytes 772
  4.0 10.3 %collective-permute-start = (bf16[24,2048]{1,0:T(8,128)(2,1)S(1)}, bf16[24,2048]{1,0:T(8,128)(2,1)S(1)}, u32[]{:S(2)}, u32[]{:S(2)}) collective-permute-start(bf16[24,2048]{1,0:T(8,128)(2,1)S(1)} %get-tuple-element.20), channel_id=1, source_target_pairs={{0,64},{64,128},{128,192},{192,0},{1,65},{65,129},{129,193},{193,1... | collective-permute-start | bytes 294920 | tf_op jit(solution)/shard_map/ppermute | solution.py:324
  6.1 8.2 %collective-permute-start.1 = (bf16[24,2048]{1,0:T(8,128)(2,1)S(1)}, bf16[24,2048]{1,0:T(8,128)(2,1)S(1)}, u32[]{:S(2)}, u32[]{:S(2)}) collective-permute-start(bf16[24,2048]{1,0:T(8,128)(2,1)S(1)} %get-tuple-element.21), channel_id=1, source_target_pairs={{0,128},{64,192},{128,0},{192,64},{1,129},{65,193},{129,1},{193,65... | collective-permute-start | bytes 294920 | tf_op jit(solution)/shard_map/ppermute | solution.py:324
  8.5 5.8 %collective-permute-start.2 = (bf16[24,2048]{1,0:T(8,128)(2,1)S(1)}, bf16[24,2048]{1,0:T(8,128)(2,1)S(1)}, u32[]{:S(2)}, u32[]{:S(2)}) collective-permute-start(bf16[24,2048]{1,0:T(8,128)(2,1)S(1)} %get-tuple-element.22), channel_id=1, source_target_pairs={{0,192},{64,0},{128,64},{192,128},{1,193},{65,1},{129,65},{193,129... | collective-permute-start | bytes 294920 | tf_op jit(solution)/shard_map/ppermute | solution.py:324
  14.3 52.3 %slice-start = ((s8[6291456]{0:T(1024)(128)(4,1)}), s8[4194304]{0:T(1024)(128)(4,1)S(1)}, s32[]{:S(2)}) async-start(s8[6291456]{0:T(1024)(128)(4,1)} %bitcast.5), calls=%async_computation.2 | async-start | bytes 8388608
  37.6 29.0 %slice-start.1 = ((s8[6291456]{0:T(1024)(128)(4,1)}), s8[2097152]{0:T(1024)(128)(4,1)S(1)}, s32[]{:S(2)}) async-start(s8[6291456]{0:T(1024)(128)(4,1)} %bitcast.5), calls=%async_computation.3 | async-start | bytes 4194304
  37.6 29.0 %copy-start = (f32[12,384]{1,0:T(8,128)S(1)}, f32[12,384]{1,0:T(8,128)}, u32[]{:S(2)}) copy-start(f32[12,384]{1,0:T(8,128)} %beam_ref.1) | copy-start | bytes 55300
  37.6 29.0 %copy-start.1 = (bf16[2,3,1,384]{3,0,2,1:T(2,128)(2,1)S(1)}, bf16[2,3,1,384]{3,0,2,1:T(2,128)(2,1)}, u32[]{:S(2)}) copy-start(bf16[2,3,1,384]{3,0,2,1:T(2,128)(2,1)} %param.8) | copy-start | bytes 13828
  37.6 29.0 %copy-start.2 = (f32[12,3]{0,1:T(4,128)S(1)}, f32[12,3]{0,1:T(4,128)}, u32[]{:S(2)}) copy-start(f32[12,3]{0,1:T(4,128)} %param.9) | copy-start | bytes 436
  37.6 29.0 %copy-start.4 = (f32[3,384]{1,0:T(4,128)S(1)}, f32[3,384]{1,0:T(4,128)}, u32[]{:S(2)}) copy-start(f32[3,384]{1,0:T(4,128)} %prior_ref.1) | copy-start | bytes 13828
  56.5 3.8 %collective-permute-start.5 = (bf16[64,8,128]{2,1,0:T(8,128)(2,1)S(1)}, bf16[64,8,128]{2,1,0:T(8,128)(2,1)S(1)}, u32[]{:S(2)}, u32[]{:S(2)}) collective-permute-start(bf16[64,8,128]{2,1,0:T(8,128)(2,1)S(1)} %all_to_all.11.rest_0_), channel_id=1, source_target_pairs={{0,192},{64,0},{128,64},{192,128},{1,193},{65,1},{129,65},{193,129... | collective-permute-start | bytes 393224 | tf_op jit(solution)/shard_map/ppermute | solution.py:324
  57.7 5.4 %collective-permute-start.4 = (bf16[64,8,128]{2,1,0:T(8,128)(2,1)S(1)}, bf16[64,8,128]{2,1,0:T(8,128)(2,1)S(1)}, u32[]{:S(2)}, u32[]{:S(2)}) collective-permute-start(bf16[64,8,128]{2,1,0:T(8,128)(2,1)S(1)} %all_to_all.11.rest_0_), channel_id=1, source_target_pairs={{0,128},{64,192},{128,0},{192,64},{1,129},{65,193},{129,1},{193,65... | collective-permute-start | bytes 393224 | tf_op jit(solution)/shard_map/ppermute | solution.py:324
  58.0 8.6 %collective-permute-start.3 = (bf16[64,8,128]{2,1,0:T(8,128)(2,1)S(1)}, bf16[64,8,128]{2,1,0:T(8,128)(2,1)S(1)}, u32[]{:S(2)}, u32[]{:S(2)}) collective-permute-start(bf16[64,8,128]{2,1,0:T(8,128)(2,1)S(1)} %all_to_all.11.rest_0_), channel_id=1, source_target_pairs={{0,64},{64,128},{128,192},{192,0},{1,65},{65,129},{129,193},{193,1... | collective-permute-start | bytes 393224 | tf_op jit(solution)/shard_map/ppermute | solution.py:324

commit v4 on v3

--- a/solution.py
+++ b/solution.py
@@ -12,6 +12,8 @@
 LANES = 128
 ROWS = 8
 QUARTERS = 4
+FINE = 64
+SINE = [(-1) ** n / math.factorial(2 * n + 1) for n in range(6)]
 
 
 def whole(space=pltpu.VMEM):
@@ -145,51 +147,64 @@
     )(*parts)
 
 
-def table_body(slots, npix_ref, mode_ref, noise_any, out_ref, noise_ref, sems):
+def cos_turn(residue, npix, scale):
+    residue = residue & (2 * npix - 1)
+    x = (jnp.abs(residue - npix) - npix // 2).astype(jnp.float32) * scale
+    square = x * x
+    series = SINE[-1]
+    for coefficient in SINE[-2::-1]:
+        series = series * square + coefficient
+    return series * x
+
+
+def table_body(slots, npix_ref, mode_ref, noise_any, out_ref, noise_ref, coarse_ref, sems):
     chan_pos = lax.axis_index("chan")
     modes = mode_ref[...]
-    mode_count = modes.shape[0]
-    pixels = out_ref.shape[2]
-    coarse_count = pixels // LANES
-    quarter = pixels // 4
+    modes = jnp.concatenate([modes, modes], axis=1)
+    width = modes.shape[1]
+    pixels = out_ref.shape[1]
+    quarter = pixels // QUARTERS
 
     def noise_copy(j, q):
         cols = pl.ds(q * quarter, quarter)
         return pltpu.make_async_copy(noise_any.at[j, :, cols], noise_ref.at[j, :, cols], sems.at[j, q])
 
     for j in range(slots):
-        for q in range(4):
+        for q in range(QUARTERS):
 
             @pl.when(q * quarter < npix_ref[chan_pos * slots + j])
             def _():
                 noise_copy(j, q).start()
 
-    weight = jnp.where(modes == 0, 1.0, 2.0).astype(jnp.float32) / math.sqrt(2 * mode_count)
-    lane = lax.broadcasted_iota(jnp.int32, (mode_count, LANES), 1)
+    weight = jnp.where(modes == 0, 1.0, 2.0).astype(jnp.float32) / math.sqrt(width)
+    lane = lax.broadcasted_iota(jnp.int32, (1, width), 1)
+    imag = jnp.where(lane >= width // 2, 1, 0)
+    fine_row = lax.broadcasted_iota(jnp.int32, (FINE, width), 0)
+    coarse_row = lax.broadcasted_iota(jnp.int32, (pixels // FINE, width), 0)
+    per = quarter // FINE
     for j in range(slots):
         npix = npix_ref[chan_pos * slots + j]
         scale = jnp.float32(jnp.pi) / npix.astype(jnp.float32)
-        fine_phase = ((modes * (2 * lane + 1)) & (2 * npix - 1)).astype(jnp.float32) * scale
-        coarse_phase = ((modes * (2 * LANES * lane)) & (2 * npix - 1)).astype(jnp.float32) * scale
-        fine_cos = jnp.cos(fine_phase) * weight
-        fine_sin = jnp.sin(fine_phase) * weight
-        coarse_cos = jnp.cos(coarse_phase)
-        coarse_sin = jnp.sin(coarse_phase)
-        for q in range(4):
-
-            @pl.when(q * quarter < npix)
-            def _():
-                for a in range(q * coarse_count // 4, (q + 1) * coarse_count // 4):
-                    cc = coarse_cos[:, a : a + 1]
-                    cs = coarse_sin[:, a : a + 1]
-                    cols = slice(a * LANES, (a + 1) * LANES)
-                    cos_part = cc * fine_cos - cs * fine_sin
-                    sin_part = -(cs * fine_cos + cc * fine_sin)
-                    out_ref[j, :mode_count, cols] = cos_part.astype(jnp.bfloat16)
-                    out_ref[j, mode_count:, cols] = sin_part.astype(jnp.bfloat16)
+        turn = npix // 2
+        fine = modes * (2 * fine_row + 1) + imag * turn
+        same = cos_turn(fine, npix, scale) * weight
+        cross = cos_turn(fine + turn, npix, scale) * weight
+        coarse = modes * (2 * FINE * coarse_row)
+        coarse_ref[0] = cos_turn(coarse, npix, scale)
+        coarse_ref[1] = cos_turn(coarse + 3 * turn, npix, scale)
+
+        def one_quarter(q, carry):
+            for a in range(per):
+                row = pl.ds(q * per + a, 1)
+                values = coarse_ref[0, row, :] * same + coarse_ref[1, row, :] * cross
+                start = pl.multiple_of(q * quarter + a * FINE, FINE)
+                out_ref[j, pl.ds(start, FINE), :] = values.astype(jnp.bfloat16)
+            return carry
+
+        lax.fori_loop(0, npix // quarter, one_quarter, 0)
 
     for j in range(slots):
-        for q in range(4):
+        for q in range(QUARTERS):
 
             @pl.when(q * quarter < npix_ref[chan_pos * slots + j])
             def _():
@@ -198,16 +213,19 @@
 
 def make_tables(npix, modes, inv_noise):
     slots, _, pixels = inv_noise.shape
-    mode_count = modes.shape[0]
+    mode_count = modes.shape[1]
     return pl.pallas_call(
         functools.partial(table_body, slots),
         in_specs=[whole(pltpu.SMEM), whole(), whole(pl.ANY)],
         out_specs=[whole(), whole()],
         out_shape=[
-            pltpu.VMEM((slots, 2 * mode_count, pixels), jnp.bfloat16),
+            pltpu.VMEM((slots, pixels, 2 * mode_count), jnp.bfloat16),
             pltpu.VMEM(inv_noise.shape, jnp.bfloat16),
         ],
-        scratch_shapes=[pltpu.SemaphoreType.DMA((slots, 4))],
+        scratch_shapes=[
+            pltpu.VMEM((2, pixels // FINE, 2 * mode_count), jnp.float32),
+            pltpu.SemaphoreType.DMA((slots, QUARTERS)),
+        ],
         compiler_params=pltpu.CompilerParams(vmem_limit_bytes=16 * MIB),
         cost_estimate=pl.CostEstimate(
             flops=10 * slots * mode_count * pixels,
@@ -236,12 +254,12 @@
 
             @pl.when(npix == width)
             def _():
-                table = table_ref[j, :, :width]
-                sky = jnp.dot(spectra, table, preferred_element_type=jnp.float32)
+                table = table_ref[j, :width, :]
+                sky = lax.dot_general(
+                    spectra, table, (((1,), (1,)), ((), ())), preferred_element_type=jnp.float32
+                )
                 noisy = (noise_ref[j, :, :width].astype(jnp.float32) * sky).astype(jnp.bfloat16)
-                back = lax.dot_general(
-                    table, noisy, (((1,), (1,)), ((), ())), preferred_element_type=jnp.float32
-                )
+                back = jnp.dot(noisy, table, preferred_element_type=jnp.float32).T
                 for i in range(2):
                     full_ref[pl.ds(2 * j + i, mode_count, stride=ROWS), :] = back[
                         i * mode_count : (i + 1) * mode_count
@@ -327,7 +345,7 @@
         cycle_pixels, mixing_t, harm, beam_window, legendre, chans, slots, pixels
     )
     parts = [parts[0]] + [shift(parts[s], s) for s in range(1, chans)]
-    tables, noise = make_tables(cycle_pixels, mode_index[:, None], inv_noise)
+    tables, noise = make_tables(cycle_pixels, mode_index[None, :], inv_noise)
     tables, noise, parts = lax.optimization_barrier((tables, noise, parts))
     chunks = add_parts(parts)
     spectra = lax.all_to_all(chunks, ("mset", "blk"), split_axis=0, concat_axis=0, tiled=True)

time: 69.6 us -> 69.6 us (level); the launches traced: 69.7 us -> 68.7 us
  Pallas kernels: 15.4 us -> 12.2 us
  starting transfers between devices: 8.06 us -> 9.21 us
  waiting for transfers between devices: 7.76 us -> 8.59 us
    pallas_call x1, Pallas kernels: 4.5 us -> 2.34 us  [make_tables(): pl.pallas_call(functools.partial(table_body, slots), in_specs=[whole(pltp...]
    ppermute x6, starting transfers between devices: 8.06 us -> 9.21 us  [shift(): return lax.ppermute(x, 'chan', [(d, (d + s) % chans) for d in range(chans)])]
    pallas_call x1, Pallas kernels: 3.78 us -> 2.82 us  [middle(): pl.pallas_call(middle_body, in_specs=[whole(pltpu.SMEM), whole(), whole()...]
    ppermute x6, waiting for transfers between devices: 7.76 us -> 8.59 us  [shift(): return lax.ppermute(x, 'chan', [(d, (d + s) % chans) for d in range(chans)])]
  transfers between devices with their start and end apart: 6 -> 6, of which waited for: 3 -> 4; matrix products, arithmetic and copies ran while one was open for 0% -> 0% of each run, Pallas kernels for 6% -> 3%
where the time goes in v4:
time: 69.6 us; the launch traced here: 68.7 us
  blocking collectives  38.6 us (55%)
  Pallas kernels  12.2 us (18%)
  starting transfers between devices  9.21 us (13%)
  waiting for transfers between devices  8.59 us (12%)
    all_to_all x1, blocking collectives, on_device(): lax.all_to_all(chunks, ('mset', 'blk'), split_axis=0, concat_axis=0, tile...  23.5 us
    all_to_all x1, blocking collectives, on_device(): lax.all_to_all(returned, ('mset', 'blk'), split_axis=0, concat_axis=0, ti...  15.1 us
    ppermute x6, starting transfers between devices, shift(): return lax.ppermute(x, 'chan', [(d, (d + s) % chans) for d in range(chans)])  9.21 us
    ppermute x6, waiting for transfers between devices, shift(): return lax.ppermute(x, 'chan', [(d, (d + s) % chans) for d in range(chans)])  8.59 us
    pallas_call x1, Pallas kernels, forward(): pl.pallas_call(functools.partial(forward_body, chans, slots, pixels, QUAR...  3.97 us
    pallas_call x1, Pallas kernels, backward(): pl.pallas_call(functools.partial(backward_body, chans, slots, pixels), in...  3.03 us
    pallas_call x1, Pallas kernels, middle(): pl.pallas_call(middle_body, in_specs=[whole(pltpu.SMEM), whole(), whole()...  2.82 us
    pallas_call x1, Pallas kernels, make_tables(): pl.pallas_call(functools.partial(table_body, slots), in_specs=[whole(pltp...  2.34 us
  transfers between devices with their start and end apart: 6, of which 4 were waited for; matrix products, arithmetic and copies ran while one was open for 0% of the time, Pallas kernels for 3%

profile of v4, /device:TPU:1, one launch (start us, length us, event | category | flops | bytes accessed | tf_op | source)
XLA Modules:
  0.0 68.7 jit_solution(5741735082285935489)
XLA Ops:
  0.0 0.0 copy-start.3
  0.0 4.0 %forward.1 = (bf16[24,2048]{1,0:T(8,128)(2,1)S(1)}, bf16[24,2048]{1,0:T(8,128)(2,1)S(1)}, bf16[24,2048]{1,0:T(8,128)(2,1)S(1)}, bf16[24,2048]{1,0:T(8,128)(2,1)S(1)}) custom-call(s32[12]{0:T(128)} %npix_ref.5, f32[3,12]{1,0:T(4,128)} %bitcast.9, bf16[3,2,384]{2,1,0:T(2,128)(2,1)} %bitcast.7, f32[12,384]{1,0:T(8,128)} %beam_ref.1, bf16[1,384,8192]{2,1,0:T(8,128)(2,1)} %leg_ref.1), custom_call_target="tpu_custom_call" | custom-call | flops 201326592 | bytes 6291456 | tf_op jit(solution)/shard_map/forward/pallas_call | solution.py:98
  4.0 2.1 %collective-permute-start = (bf16[24,2048]{1,0:T(8,128)(2,1)S(1)}, bf16[24,2048]{1,0:T(8,128)(2,1)S(1)}, u32[]{:S(2)}, u32[]{:S(2)}) collective-permute-start(bf16[24,2048]{1,0:T(8,128)(2,1)S(1)} %get-tuple-element.20), channel_id=1, source_target_pairs={{0,64},{64,128},{128,192},{192,0},{1,65},{65,129},{129,193},{193,1... | collective-permute-start | bytes 294920 | tf_op jit(solution)/shard_map/ppermute | solution.py:342
  6.1 2.4 %collective-permute-start.1 = (bf16[24,2048]{1,0:T(8,128)(2,1)S(1)}, bf16[24,2048]{1,0:T(8,128)(2,1)S(1)}, u32[]{:S(2)}, u32[]{:S(2)}) collective-permute-start(bf16[24,2048]{1,0:T(8,128)(2,1)S(1)} %get-tuple-element.21), channel_id=1, source_target_pairs={{0,128},{64,192},{128,0},{192,64},{1,129},{65,193},{129,1},{193,65... | collective-permute-start | bytes 294920 | tf_op jit(solution)/shard_map/ppermute | solution.py:342
  8.5 1.2 %collective-permute-start.2 = (bf16[24,2048]{1,0:T(8,128)(2,1)S(1)}, bf16[24,2048]{1,0:T(8,128)(2,1)S(1)}, u32[]{:S(2)}, u32[]{:S(2)}) collective-permute-start(bf16[24,2048]{1,0:T(8,128)(2,1)S(1)} %get-tuple-element.22), channel_id=1, source_target_pairs={{0,192},{64,0},{128,64},{192,128},{1,193},{65,1},{129,65},{193,129... | collective-permute-start | bytes 294920 | tf_op jit(solution)/shard_map/ppermute | solution.py:342
  9.7 0.0 copy-done.3
  9.7 0.0 copy-done.5
  9.7 2.3 %make_tables.1 = (bf16[3,8192,128]{2,1,0:T(8,128)(2,1)S(1)}, bf16[3,128,8192]{2,1,0:T(8,128)(2,1)S(1)}) custom-call(s32[12]{0:T(128)S(1)} %copy-done.3, s32[1,64]{1,0:T(1,128)S(1)} %bitcast.11, bf16[3,128,8192]{2,1,0:T(8,128)(2,1)} %noise_any.1), custom_call_target="tpu_custom_call" | custom-call | flops 15728640 | bytes 6291456 | tf_op jit(solution)/shard_map/make_tables/pallas_call | solution.py:217
  12.1 0.0 collective-permute-done.refs_1_
  12.1 0.5 collective-permute-done.1.refs_2_
  12.6 0.0 collective-permute-done.2.refs_3_
  12.6 0.0 slice-start
  12.6 0.1 add_parts.1
  12.7 23.5 %all_to_all.10.spec_ref = bf16[64,8,128]{2,1,0:T(8,128)(2,1)S(1)} all-to-all(bf16[64,8,128]{2,1,0:T(8,128)(2,1)S(1)} %add_parts.1), channel_id=1, replica_groups=mesh['chan'=4,'mset'=8,'blk'=8] {'mset','blk'}, dimensions={0} | all-to-all | bytes 262144 | tf_op jit(solution)/shard_map/all_to_all | solution.py:351
  36.2 0.0 slice-start.1
  36.2 0.0 copy-start
  36.2 0.0 copy-start.4
  36.2 2.8 %middle.1 = bf16[64,8,128]{2,1,0:T(8,128)(2,1)S(1)} custom-call(s32[12]{0:T(128)S(1)} %copy-done.3, bf16[64,8,128]{2,1,0:T(8,128)(2,1)S(1)} %all_to_all.10.spec_ref, bf16[3,8192,128]{2,1,0:T(8,128)(2,1)S(1)} %get-tuple-element.27.table_ref, bf16[3,128,8192]{2,1,0:T(8,128)(2,1)S(1)} %get-tuple-element.28.noise_ref), custom_call_target="tpu_custom_call" | custom-call | tf_op jit(solution)/shard_map/middle/pallas_call | solution.py:277
  39.0 15.1 %all_to_all.11.rest_0_ = bf16[64,8,128]{2,1,0:T(8,128)(2,1)S(1)} all-to-all(bf16[64,8,128]{2,1,0:T(8,128)(2,1)S(1)} %middle.1), channel_id=1, replica_groups=mesh['chan'=4,'mset'=8,'blk'=8] {'mset','blk'}, dimensions={0} | all-to-all | bytes 262144 | tf_op jit(solution)/shard_map/all_to_all | solution.py:353
  54.1 2.9 %collective-permute-start.5 = (bf16[64,8,128]{2,1,0:T(8,128)(2,1)S(1)}, bf16[64,8,128]{2,1,0:T(8,128)(2,1)S(1)}, u32[]{:S(2)}, u32[]{:S(2)}) collective-permute-start(bf16[64,8,128]{2,1,0:T(8,128)(2,1)S(1)} %all_to_all.11.rest_0_), channel_id=1, source_target_pairs={{0,192},{64,0},{128,64},{192,128},{1,193},{65,1},{129,65},{193,129... | collective-permute-start | bytes 393224 | tf_op jit(solution)/shard_map/ppermute | solution.py:342
  57.0 0.2 collective-permute-start.4
  57.2 0.4 collective-permute-start.3
  57.6 2.5 %collective-permute-done.5.rest_3_ = bf16[64,8,128]{2,1,0:T(8,128)(2,1)S(1)} collective-permute-done((bf16[64,8,128]{2,1,0:T(8,128)(2,1)S(1)}, bf16[64,8,128]{2,1,0:T(8,128)(2,1)S(1)}, u32[]{:S(2)}, u32[]{:S(2)}) %collective-permute-start.5) | collective-permute-done | bytes 131104 | tf_op jit(solution)/shard_map/ppermute | solution.py:342
  60.0 2.4 %collective-permute-done.4.rest_2_ = bf16[64,8,128]{2,1,0:T(8,128)(2,1)S(1)} collective-permute-done((bf16[64,8,128]{2,1,0:T(8,128)(2,1)S(1)}, bf16[64,8,128]{2,1,0:T(8,128)(2,1)S(1)}, u32[]{:S(2)}, u32[]{:S(2)}) %collective-permute-start.4) | collective-permute-done | bytes 131104 | tf_op jit(solution)/shard_map/ppermute | solution.py:342
  62.4 3.2 %collective-permute-done.3.rest_1_ = bf16[64,8,128]{2,1,0:T(8,128)(2,1)S(1)} collective-permute-done((bf16[64,8,128]{2,1,0:T(8,128)(2,1)S(1)}, bf16[64,8,128]{2,1,0:T(8,128)(2,1)S(1)}, u32[]{:S(2)}, u32[]{:S(2)}) %collective-permute-start.3) | collective-permute-done | bytes 131104 | tf_op jit(solution)/shard_map/ppermute | solution.py:342
  65.6 0.0 slice-done
  65.7 0.0 slice-done.1
  65.7 0.0 copy-done
  65.7 0.0 copy-done.1
  65.7 0.0 copy-done.2
  65.7 0.0 copy-done.4
  65.7 3.0 %backward.1 = f32[2,3,1,384]{3,2,1,0:T(1,128)} custom-call(s32[12]{0:T(128)S(1)} %copy-done.3, f32[3,12]{1,0:T(4,128)S(1)} %bitcast.10, bf16[3,2,384]{2,1,0:T(2,128)(2,1)S(1)} %bitcast.8, f32[12,384]{1,0:T(8,128)S(1)} %copy-done, f32[3,384]{1,0:T(4,128)S(1)} %copy-done.4, bf16[1,384,8192]{2,1,0:T(8,128)(2,1)S(1)} %bitcast.6, ...), custom_call_target="tpu_custom_call" | custom-call | tf_op jit(solution)/shard_map/backward/pallas_call | solution.py:322
  (4 shorter events, 0.0 us)
Async XLA Ops:
  0.0 9.7 %copy-start.3 = (s32[12]{0:T(128)S(1)}, s32[12]{0:T(128)}, u32[]{:S(2)}) copy-start(s32[12]{0:T(128)} %npix_ref.5) | copy-start | bytes 148
  0.0 9.7 %copy-start.5 = (s32[64]{0:T(128)S(1)}, s32[64]{0:T(128)}, u32[]{:S(2)}) copy-start(s32[64]{0:T(128)} %param.14) | copy-start | bytes 772
  4.0 8.1 %collective-permute-start = (bf16[24,2048]{1,0:T(8,128)(2,1)S(1)}, bf16[24,2048]{1,0:T(8,128)(2,1)S(1)}, u32[]{:S(2)}, u32[]{:S(2)}) collective-permute-start(bf16[24,2048]{1,0:T(8,128)(2,1)S(1)} %get-tuple-element.20), channel_id=1, source_target_pairs={{0,64},{64,128},{128,192},{192,0},{1,65},{65,129},{129,193},{193,1... | collective-permute-start | bytes 294920 | tf_op jit(solution)/shard_map/ppermute | solution.py:342
  6.1 6.5 %collective-permute-start.1 = (bf16[24,2048]{1,0:T(8,128)(2,1)S(1)}, bf16[24,2048]{1,0:T(8,128)(2,1)S(1)}, u32[]{:S(2)}, u32[]{:S(2)}) collective-permute-start(bf16[24,2048]{1,0:T(8,128)(2,1)S(1)} %get-tuple-element.21), channel_id=1, source_target_pairs={{0,128},{64,192},{128,0},{192,64},{1,129},{65,193},{129,1},{193,65... | collective-permute-start | bytes 294920 | tf_op jit(solution)/shard_map/ppermute | solution.py:342
  8.5 4.0 %collective-permute-start.2 = (bf16[24,2048]{1,0:T(8,128)(2,1)S(1)}, bf16[24,2048]{1,0:T(8,128)(2,1)S(1)}, u32[]{:S(2)}, u32[]{:S(2)}) collective-permute-start(bf16[24,2048]{1,0:T(8,128)(2,1)S(1)} %get-tuple-element.22), channel_id=1, source_target_pairs={{0,192},{64,0},{128,64},{192,128},{1,193},{65,1},{129,65},{193,129... | collective-permute-start | bytes 294920 | tf_op jit(solution)/shard_map/ppermute | solution.py:342
  12.6 53.1 %slice-start = ((s8[6291456]{0:T(1024)(128)(4,1)}), s8[4194304]{0:T(1024)(128)(4,1)S(1)}, s32[]{:S(2)}) async-start(s8[6291456]{0:T(1024)(128)(4,1)} %bitcast.5), calls=%async_computation.2 | async-start | bytes 8388608
  36.2 29.5 %slice-start.1 = ((s8[6291456]{0:T(1024)(128)(4,1)}), s8[2097152]{0:T(1024)(128)(4,1)S(1)}, s32[]{:S(2)}) async-start(s8[6291456]{0:T(1024)(128)(4,1)} %bitcast.5), calls=%async_computation.3 | async-start | bytes 4194304
  36.2 29.5 %copy-start = (f32[12,384]{1,0:T(8,128)S(1)}, f32[12,384]{1,0:T(8,128)}, u32[]{:S(2)}) copy-start(f32[12,384]{1,0:T(8,128)} %beam_ref.1) | copy-start | bytes 55300
  36.2 29.5 %copy-start.1 = (bf16[2,3,1,384]{3,0,2,1:T(2,128)(2,1)S(1)}, bf16[2,3,1,384]{3,0,2,1:T(2,128)(2,1)}, u32[]{:S(2)}) copy-start(bf16[2,3,1,384]{3,0,2,1:T(2,128)(2,1)} %param.8) | copy-start | bytes 13828
  36.2 29.5 %copy-start.2 = (f32[12,3]{0,1:T(4,128)S(1)}, f32[12,3]{0,1:T(4,128)}, u32[]{:S(2)}) copy-start(f32[12,3]{0,1:T(4,128)} %param.9) | copy-start | bytes 436
  36.2 29.5 %copy-start.4 = (f32[3,384]{1,0:T(4,128)S(1)}, f32[3,384]{1,0:T(4,128)}, u32[]{:S(2)}) copy-start(f32[3,384]{1,0:T(4,128)} %prior_ref.1) | copy-start | bytes 13828
  54.1 5.9 %collective-permute-start.5 = (bf16[64,8,128]{2,1,0:T(8,128)(2,1)S(1)}, bf16[64,8,128]{2,1,0:T(8,128)(2,1)S(1)}, u32[]{:S(2)}, u32[]{:S(2)}) collective-permute-start(bf16[64,8,128]{2,1,0:T(8,128)(2,1)S(1)} %all_to_all.11.rest_0_), channel_id=1, source_target_pairs={{0,192},{64,0},{128,64},{192,128},{1,193},{65,1},{129,65},{193,129... | collective-permute-start | bytes 393224 | tf_op jit(solution)/shard_map/ppermute | solution.py:342
  57.0 5.4 %collective-permute-start.4 = (bf16[64,8,128]{2,1,0:T(8,128)(2,1)S(1)}, bf16[64,8,128]{2,1,0:T(8,128)(2,1)S(1)}, u32[]{:S(2)}, u32[]{:S(2)}) collective-permute-start(bf16[64,8,128]{2,1,0:T(8,128)(2,1)S(1)} %all_to_all.11.rest_0_), channel_id=1, source_target_pairs={{0,128},{64,192},{128,0},{192,64},{1,129},{65,193},{129,1},{193,65... | collective-permute-start | bytes 393224 | tf_op jit(solution)/shard_map/ppermute | solution.py:342
  57.2 8.5 %collective-permute-start.3 = (bf16[64,8,128]{2,1,0:T(8,128)(2,1)S(1)}, bf16[64,8,128]{2,1,0:T(8,128)(2,1)S(1)}, u32[]{:S(2)}, u32[]{:S(2)}) collective-permute-start(bf16[64,8,128]{2,1,0:T(8,128)(2,1)S(1)} %all_to_all.11.rest_0_), channel_id=1, source_target_pairs={{0,64},{64,128},{128,192},{192,0},{1,65},{65,129},{129,193},{193,1... | collective-permute-start | bytes 393224 | tf_op jit(solution)/shard_map/ppermute | solution.py:342

commit v5 on v4

--- a/solution.py
+++ b/solution.py
@@ -12,6 +12,7 @@
 LANES = 128
 ROWS = 8
 QUARTERS = 4
+STEPS = 4
 FINE = 64
 SINE = [(-1) ** n / math.factorial(2 * n + 1) for n in range(6)]
 
@@ -37,9 +38,10 @@
     return chan_pos * shape[-1] + lax.broadcasted_iota(jnp.int32, shape, len(shape) - 1)
 
 
-def forward_body(chans, slots, pixels, steps, npix_any, mix_any, harm_any, beam_any, leg_any, *rest):
+def forward_body(chans, slots, pixels, npix_any, mix_any, harm_any, beam_any, prior_any, leg_any, *rest):
     outs = rest[:chans]
-    npix_ref, mix_ref, harm_ref, beam_ref, rows_ref, leg_ref, sems, small = rest[chans:]
+    base_ref, weight_ref, npix_ref, mix_ref, harm_ref, beam_ref, prior_ref = rest[chans : chans + 7]
+    rows_ref, leg_ref, sems, small = rest[chans + 7 :]
     small_copies = [
         pltpu.make_async_copy(src, dst, small.at[n])
         for n, (src, dst) in enumerate(
@@ -48,18 +50,20 @@
                 (mix_any, mix_ref),
                 (harm_any, harm_ref),
                 (beam_any, beam_ref),
+                (prior_any, prior_ref),
             ]
         )
     ]
     local_deg, cycles = leg_ref.shape
-    block = cycles // steps
+    block = cycles // STEPS
+    per = STEPS // QUARTERS
     copies = [
         pltpu.make_async_copy(
             leg_any.at[0, :, pl.ds(q * block, block)],
             leg_ref.at[:, pl.ds(q * block, block)],
             sems.at[q],
         )
-        for q in range(steps)
+        for q in range(STEPS)
     ]
     for copy in small_copies + copies:
         copy.start()
@@ -75,40 +79,51 @@
             mixture = sum(mix_ref[k, c] * comps[k] for k in range(len(comps)))
             filt = filter_row(beam_ref, npix_ref, c, degrees, local_deg * chans, pixels)
             rows_ref[pl.ds(s * ROWS + 2 * j, 2), :] = mixture * filt
+            for k in range(len(comps)):
+                row = ((chans - s) % chans * slots + j) * len(comps) + k
+                weight_ref[pl.ds(row, 1), :] = mix_ref[k, c] * filt
         rest_rows = ROWS - 2 * slots
         rows_ref[pl.ds(s * ROWS + 2 * slots, rest_rows), :] = jnp.zeros(
             (rest_rows, local_deg), jnp.float32
         )
+    for k in range(len(comps)):
+        base_ref[pl.ds(2 * k, 2), :] = prior_ref[k : k + 1, :] * comps[k]
     rows = rows_ref[...].astype(jnp.bfloat16)
     used = 2 * slots
-    for q in range(steps):
+    for q in range(STEPS):
         copies[q].wait()
         partial = jnp.dot(
             rows, leg_ref[:, q * block : (q + 1) * block], preferred_element_type=jnp.float32
         )
         for s in range(chans):
-            outs[s][q * used : (q + 1) * used, :] = partial[s * ROWS : s * ROWS + used].astype(
-                jnp.bfloat16
-            )
-
-
-def forward(npix, mixing_t, harm, beam, legendre, chans, slots, pixels):
+            outs[s][pl.ds(q // per * used, used), pl.ds(q % per * block, block)] = partial[
+                s * ROWS : s * ROWS + used
+            ].astype(jnp.bfloat16)
+
+
+def forward(npix, mixing_t, harm, beam, prior, legendre, chans, slots, pixels):
     _, local_deg, cycles = legendre.shape
+    comps = harm.shape[0]
     used = 2 * slots
     return pl.pallas_call(
-        functools.partial(forward_body, chans, slots, pixels, QUARTERS),
-        in_specs=[whole(pl.ANY)] * 5,
-        out_specs=[whole()] * chans,
-        out_shape=[jax.ShapeDtypeStruct((QUARTERS * used, cycles // QUARTERS), jnp.bfloat16)] * chans,
+        functools.partial(forward_body, chans, slots, pixels),
+        in_specs=[whole(pl.ANY)] * 6,
+        out_specs=[whole()] * (chans + 2),
+        out_shape=[jax.ShapeDtypeStruct((QUARTERS * used, cycles // QUARTERS), jnp.bfloat16)] * chans
+        + [
+            jax.ShapeDtypeStruct((2 * comps, local_deg), jnp.float32),
+            jax.ShapeDtypeStruct((chans * slots * comps, local_deg), jnp.float32),
+        ],
         scratch_shapes=[
             pltpu.SMEM(npix.shape, npix.dtype),
             pltpu.SMEM(mixing_t.shape, mixing_t.dtype),
             pltpu.VMEM(harm.shape, harm.dtype),
             pltpu.VMEM(beam.shape, beam.dtype),
+            pltpu.VMEM(prior.shape, prior.dtype),
             pltpu.VMEM((chans * ROWS, local_deg), jnp.float32),
             pltpu.VMEM((local_deg, cycles), jnp.bfloat16),
-            pltpu.SemaphoreType.DMA((QUARTERS,)),
-            pltpu.SemaphoreType.DMA((4,)),
+            pltpu.SemaphoreType.DMA((STEPS,)),
+            pltpu.SemaphoreType.DMA((5,)),
         ],
         compiler_params=pltpu.CompilerParams(vmem_limit_bytes=16 * MIB),
         cost_estimate=pl.CostEstimate(
@@ -117,7 +132,7 @@
             transcendentals=0,
         ),
         name="forward",
-    )(*in_hbm(npix, mixing_t, harm, beam, legendre))
+    )(*in_hbm(npix, mixing_t, harm, beam, prior, legendre))
 
 
 def gather_body(used, *refs):
@@ -157,7 +172,8 @@
     return series * x
 
 
-def table_body(slots, npix_ref, mode_ref, noise_any, out_ref, noise_ref, coarse_ref, sems):
+def table_body(npix_ref, mode_ref, noise_any, out_ref, noise_ref, coarse_ref, sems):
+    slots = out_ref.shape[0]
     chan_pos = lax.axis_index("chan")
     modes = mode_ref[...]
     modes = jnp.concatenate([modes, modes], axis=1)
@@ -215,9 +231,9 @@
     slots, _, pixels = inv_noise.shape
     mode_count = modes.shape[1]
     return pl.pallas_call(
-        functools.partial(table_body, slots),
+        table_body,
         in_specs=[whole(pltpu.SMEM), whole(), whole(pl.ANY)],
-        out_specs=[whole(), whole()],
+        out_specs=[whole()] * 2,
         out_shape=[
             pltpu.VMEM((slots, pixels, 2 * mode_count), jnp.bfloat16),
             pltpu.VMEM(inv_noise.shape, jnp.bfloat16),
@@ -288,46 +304,67 @@
     )(npix, spectra, *in_vmem(tables, noise))
 
 
-def backward_body(chans, slots, pixels, npix_ref, mix_ref, harm_ref, beam_ref, prior_ref, leg_ref, *rest):
-    parts, out_ref, acc_ref = rest[:chans], rest[chans], rest[chans + 1]
-    rows = [
-        jnp.concatenate([part[b] for b in range(part.shape[0])], axis=1) for part in parts
-    ]
-    rows = jnp.concatenate(rows, axis=0)
-    acc_ref[...] = lax.dot_general(
-        leg_ref[0], rows, (((1,), (1,)), ((), ())), preferred_element_type=jnp.float32
-    ).T
-    chan_pos = lax.axis_index("chan")
-    local_deg = beam_ref.shape[1]
-    degrees = degrees_of((1, local_deg), chan_pos)
-    comps = harm_ref.shape[0]
-    totals = [prior_ref[k : k + 1, :] * harm_ref[k].astype(jnp.float32) for k in range(comps)]
-    for s in range(chans):
-        group = (chan_pos + chans - s) % chans
-        for j in range(slots):
-            c = group * slots + j
-            filt = filter_row(beam_ref, npix_ref, c, degrees, local_deg * chans, pixels)
-            weighted = acc_ref[pl.ds(s * ROWS + 2 * j, 2), :] * filt
+def pack_body(used, chunk_ref, out_ref):
+    per = out_ref.shape[1] // LANES
+    for q in range(QUARTERS):
+        tiles = [chunk_ref[q * per + b] for b in range(per)]
+        rows = jnp.concatenate(tiles, axis=1).astype(jnp.float32)
+        out_ref[pl.ds(q * used, used), :] = rows[:used].astype(jnp.bfloat16)
+
+
+def pack(chunks, used):
+    blocks = chunks.shape[0]
+    return pl.pallas_call(
+        functools.partial(pack_body, used),
+        in_specs=[whole()],
+        out_specs=whole(),
+        out_shape=jax.ShapeDtypeStruct((QUARTERS * used, blocks // QUARTERS * LANES), chunks.dtype),
+        compiler_params=pltpu.CompilerParams(vmem_limit_bytes=8 * MIB),
+        name="pack",
+    )(chunks)
+
+
+def backward_body(base_ref, weight_ref, leg_ref, *rest):
+    parts, out_ref, acc_ref = rest[:-2], rest[-2], rest[-1]
+    height, block = parts[0].shape
+    used = height // QUARTERS
+    comps = base_ref.shape[0] // 2
+    rows = jnp.concatenate([part[...] for part in parts], axis=0)
+    owner = lax.broadcasted_iota(jnp.int32, rows.shape, 0) % height // used
+    total = None
+    for q in range(QUARTERS):
+        mine = jnp.where(owner == q, rows.astype(jnp.float32), 0.0).astype(jnp.bfloat16)
+        product = lax.dot_general(
+            leg_ref[0, :, q * block : (q + 1) * block],
+            mine,
+            (((1,), (1,)), ((), ())),
+            preferred_element_type=jnp.float32,
+        )
+        total = product if q == 0 else total + product
+    acc_ref[...] = total.T
+    sums = [base_ref[pl.ds(2 * k, 2), :] for k in range(comps)]
+    for s in range(len(parts)):
+        for j in range(used // 2):
+            value = sum(acc_ref[pl.ds(s * height + q * used + 2 * j, 2), :] for q in range(QUARTERS))
             for k in range(comps):
-                totals[k] = totals[k] + mix_ref[k, c] * weighted
+                row = (s * (used // 2) + j) * comps + k
+                sums[k] = sums[k] + weight_ref[pl.ds(row, 1), :] * value
     for k in range(comps):
         for i in range(2):
-            out_ref[i, k] = totals[k][i : i + 1]
-
-
-def backward(npix, mixing_t, harm, beam, prior, legendre, parts, slots, pixels):
-    chans = len(parts)
+            out_ref[i, k] = sums[k][i : i + 1]
+
+
+def backward(base, weights, legendre, parts):
     local_deg = legendre.shape[1]
-    comps = harm.shape[0]
-    return pl.pallas_call(
-        functools.partial(backward_body, chans, slots, pixels),
-        in_specs=[whole(pltpu.SMEM), whole(pltpu.SMEM)] + [whole()] * (4 + chans),
+    return pl.pallas_call(
+        backward_body,
+        in_specs=[whole()] * (3 + len(parts)),
         out_specs=whole(),
-        out_shape=jax.ShapeDtypeStruct((2, comps, 1, local_deg), jnp.float32),
-        scratch_shapes=[pltpu.VMEM((chans * ROWS, local_deg), jnp.float32)],
+        out_shape=jax.ShapeDtypeStruct((2, base.shape[0] // 2, 1, local_deg), jnp.float32),
+        scratch_shapes=[pltpu.VMEM((len(parts) * parts[0].shape[0], local_deg), jnp.float32)],
         compiler_params=pltpu.CompilerParams(vmem_limit_bytes=16 * MIB),
         name="backward",
-    )(npix, mixing_t, harm, beam, prior, legendre, *parts)
+    )(base, weights, legendre, *parts)
 
 
 def on_device(
@@ -341,8 +378,8 @@
     def shift(x, s):
         return lax.ppermute(x, "chan", [(d, (d + s) % chans) for d in range(chans)])
 
-    parts = forward(
-        cycle_pixels, mixing_t, harm, beam_window, legendre, chans, slots, pixels
+    *parts, base, weights = forward(
+        cycle_pixels, mixing_t, harm, beam_window, prior_inv, legendre, chans, slots, pixels
     )
     parts = [parts[0]] + [shift(parts[s], s) for s in range(1, chans)]
     tables, noise = make_tables(cycle_pixels, mode_index[None, :], inv_noise)
@@ -351,10 +388,9 @@
     spectra = lax.all_to_all(chunks, ("mset", "blk"), split_axis=0, concat_axis=0, tiled=True)
     returned = middle(cycle_pixels, spectra, tables, noise)
     own = lax.all_to_all(returned, ("mset", "blk"), split_axis=0, concat_axis=0, tiled=True)
+    own = pack(own, 2 * slots)
     gathered = [own] + [shift(own, s) for s in range(1, chans)]
-    return backward(
-        cycle_pixels, mixing_t, harm, beam_window, prior_inv, legendre, gathered, slots, pixels
-    )
+    return backward(base, weights, legendre, gathered)
 
 
 def solution(mesh):

time: 69.6 us -> 66.7 us (0.958)
  waiting for transfers between devices: 8.59 us -> 4.73 us
  starting transfers between devices: 9.21 us -> 11 us
    ppermute x6, waiting for transfers between devices: 8.59 us -> 4.73 us  [shift(): return lax.ppermute(x, 'chan', [(d, (d + s) % chans) for d in range(chans)])]
    ppermute x6, starting transfers between devices: 9.21 us -> 11 us  [shift(): return lax.ppermute(x, 'chan', [(d, (d + s) % chans) for d in range(chans)])]
    pallas_call x3 -> x4, Pallas kernels: 9.34 us -> 8.84 us  [the longest x1 3.96 us: forward(): pl.pallas_call(functools.partial(forward_body, chans, slots, pixels), in_...]
  transfers between devices with their start and end apart: 6 -> 6, of which waited for: 4 -> 3; matrix products, arithmetic and copies ran while one was open for 0% -> 0% of each run, Pallas kernels for 3% -> 4%
where the time goes in v5:
time: 66.7 us; the launch traced here: 66.1 us
  blocking collectives  38.5 us (58%)
  Pallas kernels  11.7 us (18%)
  starting transfers between devices  11 us (16%)
  waiting for transfers between devices  4.73 us (7%)
    all_to_all x1, blocking collectives, on_device(): lax.all_to_all(chunks, ('mset', 'blk'), split_axis=0, concat_axis=0, tile...  23.5 us
    all_to_all x1, blocking collectives, on_device(): lax.all_to_all(returned, ('mset', 'blk'), split_axis=0, concat_axis=0, ti...  15.1 us
    ppermute x6, starting transfers between devices, shift(): return lax.ppermute(x, 'chan', [(d, (d + s) % chans) for d in range(chans)])  11 us
    ppermute x6, waiting for transfers between devices, shift(): return lax.ppermute(x, 'chan', [(d, (d + s) % chans) for d in range(chans)])  4.73 us
    pallas_call x1, Pallas kernels, forward(): pl.pallas_call(functools.partial(forward_body, chans, slots, pixels), in_...  3.96 us
    pallas_call x1, Pallas kernels, middle(): pl.pallas_call(middle_body, in_specs=[whole(pltpu.SMEM), whole(), whole()...  2.82 us
    pallas_call x1, Pallas kernels, backward(): pl.pallas_call(backward_body, in_specs=[whole()] * (3 + len(parts)), out_...  2.52 us
    pallas_call x1, Pallas kernels, make_tables(): pl.pallas_call(table_body, in_specs=[whole(pltpu.SMEM), whole(), whole(pl...  2.34 us
  transfers between devices with their start and end apart: 6, of which 3 were waited for; matrix products, arithmetic and copies ran while one was open for 0% of the time, Pallas kernels for 4%

profile of v5, /device:TPU:1, one launch (start us, length us, event | category | flops | bytes accessed | tf_op | source)
XLA Modules:
  0.0 66.1 jit_solution(12316055767984488769)
XLA Ops:
  0.0 0.0 copy-start
  0.0 0.0 copy-start.1
  0.0 4.0 %forward.1 = (bf16[24,2048]{1,0:T(8,128)(2,1)S(1)}, bf16[24,2048]{1,0:T(8,128)(2,1)S(1)}, bf16[24,2048]{1,0:T(8,128)(2,1)S(1)}, bf16[24,2048]{1,0:T(8,128)(2,1)S...) custom-call(s32[12]{0:T(128)} %npix_ref.3, f32[3,12]{1,0:T(4,128)} %bitcast.9, bf16[3,2,384]{2,1,0:T(2,128)(2,1)} %bitcast.8, ...), custom_call_target="tpu_custom_call" | custom-call | flops 201326592 | bytes 6291456 | tf_op jit(solution)/shard_map/forward/pallas_call | solution.py:108
  4.0 2.1 %collective-permute-start = (bf16[24,2048]{1,0:T(8,128)(2,1)S(1)}, bf16[24,2048]{1,0:T(8,128)(2,1)S(1)}, u32[]{:S(2)}, u32[]{:S(2)}) collective-permute-start(bf16[24,2048]{1,0:T(8,128)(2,1)S(1)} %get-tuple-element.24), channel_id=1, source_target_pairs={{0,64},{64,128},{128,192},{192,0},{1,65},{65,129},{129,193},{193,1... | collective-permute-start | bytes 294920 | tf_op jit(solution)/shard_map/ppermute | solution.py:379
  6.1 2.5 %collective-permute-start.1 = (bf16[24,2048]{1,0:T(8,128)(2,1)S(1)}, bf16[24,2048]{1,0:T(8,128)(2,1)S(1)}, u32[]{:S(2)}, u32[]{:S(2)}) collective-permute-start(bf16[24,2048]{1,0:T(8,128)(2,1)S(1)} %get-tuple-element.25), channel_id=1, source_target_pairs={{0,128},{64,192},{128,0},{192,64},{1,129},{65,193},{129,1},{193,65... | collective-permute-start | bytes 294920 | tf_op jit(solution)/shard_map/ppermute | solution.py:379
  8.5 1.2 %collective-permute-start.2 = (bf16[24,2048]{1,0:T(8,128)(2,1)S(1)}, bf16[24,2048]{1,0:T(8,128)(2,1)S(1)}, u32[]{:S(2)}, u32[]{:S(2)}) collective-permute-start(bf16[24,2048]{1,0:T(8,128)(2,1)S(1)} %get-tuple-element.26), channel_id=1, source_target_pairs={{0,192},{64,0},{128,64},{192,128},{1,193},{65,1},{129,65},{193,129... | collective-permute-start | bytes 294920 | tf_op jit(solution)/shard_map/ppermute | solution.py:379
  9.7 0.0 copy-done
  9.7 0.0 copy-done.1
  9.7 2.3 %make_tables.1 = (bf16[3,8192,128]{2,1,0:T(8,128)(2,1)S(1)}, bf16[3,128,8192]{2,1,0:T(8,128)(2,1)S(1)}) custom-call(s32[12]{0:T(128)S(1)} %copy-done, s32[1,64]{1,0:T(1,128)S(1)} %bitcast.7, bf16[3,128,8192]{2,1,0:T(8,128)(2,1)} %noise_any.1), custom_call_target="tpu_custom_call" | custom-call | flops 15728640 | bytes 6291456 | tf_op jit(solution)/shard_map/make_tables/pallas_call | solution.py:233
  12.0 0.0 collective-permute-done.refs_1_
  12.1 0.5 collective-permute-done.1.refs_2_
  12.6 0.0 collective-permute-done.2.refs_3_
  12.6 0.0 slice-start
  12.6 0.1 add_parts.1
  12.6 23.5 %all_to_all.10.spec_ref = bf16[64,8,128]{2,1,0:T(8,128)(2,1)S(1)} all-to-all(bf16[64,8,128]{2,1,0:T(8,128)(2,1)S(1)} %add_parts.1), channel_id=1, replica_groups=mesh['chan'=4,'mset'=8,'blk'=8] {'mset','blk'}, dimensions={0} | all-to-all | bytes 262144 | tf_op jit(solution)/shard_map/all_to_all | solution.py:388
  36.1 0.0 slice-start.1
  36.1 2.8 %middle.1 = bf16[64,8,128]{2,1,0:T(8,128)(2,1)S(1)} custom-call(s32[12]{0:T(128)S(1)} %copy-done, bf16[64,8,128]{2,1,0:T(8,128)(2,1)S(1)} %all_to_all.10.spec_ref, bf16[3,8192,128]{2,1,0:T(8,128)(2,1)S(1)} %get-tuple-element.31.table_ref, bf16[3,128,8192]{2,1,0:T(8,128)(2,1)S(1)} %get-tuple-element.32.noise_ref), custom_call_target="tpu_custom_call" | custom-call | tf_op jit(solution)/shard_map/middle/pallas_call | solution.py:293
  39.0 15.1 %all_to_all.11.chunk_ref = bf16[64,8,128]{2,1,0:T(8,128)(2,1)S(1)} all-to-all(bf16[64,8,128]{2,1,0:T(8,128)(2,1)S(1)} %middle.1), channel_id=1, replica_groups=mesh['chan'=4,'mset'=8,'blk'=8] {'mset','blk'}, dimensions={0} | all-to-all | bytes 262144 | tf_op jit(solution)/shard_map/all_to_all | solution.py:390
  54.0 3.0 %collective-permute-start.5 = (bf16[24,2048]{1,0:T(8,128)(2,1)S(1)}, bf16[24,2048]{1,0:T(8,128)(2,1)S(1)}, u32[]{:S(2)}, u32[]{:S(2)}) collective-permute-start(bf16[24,2048]{1,0:T(8,128)(2,1)S(1)} %pack.1.rest_0_), channel_id=1, source_target_pairs={{0,192},{64,0},{128,64},{192,128},{1,193},{65,1},{129,65},{193,129... | collective-permute-start | bytes 294920 | tf_op jit(solution)/shard_map/ppermute | solution.py:379
  57.1 1.5 %collective-permute-start.4 = (bf16[24,2048]{1,0:T(8,128)(2,1)S(1)}, bf16[24,2048]{1,0:T(8,128)(2,1)S(1)}, u32[]{:S(2)}, u32[]{:S(2)}) collective-permute-start(bf16[24,2048]{1,0:T(8,128)(2,1)S(1)} %pack.1.rest_0_), channel_id=1, source_target_pairs={{0,128},{64,192},{128,0},{192,64},{1,129},{65,193},{129,1},{193,65... | collective-permute-start | bytes 294920 | tf_op jit(solution)/shard_map/ppermute | solution.py:379
  58.6 0.8 %collective-permute-start.3 = (bf16[24,2048]{1,0:T(8,128)(2,1)S(1)}, bf16[24,2048]{1,0:T(8,128)(2,1)S(1)}, u32[]{:S(2)}, u32[]{:S(2)}) collective-permute-start(bf16[24,2048]{1,0:T(8,128)(2,1)S(1)} %pack.1.rest_0_), channel_id=1, source_target_pairs={{0,64},{64,128},{128,192},{192,0},{1,65},{65,129},{129,193},{193,1... | collective-permute-start | bytes 294920 | tf_op jit(solution)/shard_map/ppermute | solution.py:379
  59.4 0.0 collective-permute-done.5.rest_3_
  59.4 2.7 %collective-permute-done.4.rest_2_ = bf16[24,2048]{1,0:T(8,128)(2,1)S(1)} collective-permute-done((bf16[24,2048]{1,0:T(8,128)(2,1)S(1)}, bf16[24,2048]{1,0:T(8,128)(2,1)S(1)}, u32[]{:S(2)}, u32[]{:S(2)}) %collective-permute-start.4) | collective-permute-done | bytes 98336 | tf_op jit(solution)/shard_map/ppermute | solution.py:379
  62.0 1.6 %collective-permute-done.3.rest_1_ = bf16[24,2048]{1,0:T(8,128)(2,1)S(1)} collective-permute-done((bf16[24,2048]{1,0:T(8,128)(2,1)S(1)}, bf16[24,2048]{1,0:T(8,128)(2,1)S(1)}, u32[]{:S(2)}, u32[]{:S(2)}) %collective-permute-start.3) | collective-permute-done | bytes 98336 | tf_op jit(solution)/shard_map/ppermute | solution.py:379
  63.6 0.0 slice-done
  63.6 0.0 slice-done.1
  63.6 2.5 %backward.1 = f32[2,3,1,384]{3,2,1,0:T(1,128)} custom-call(f32[6,384]{1,0:T(8,128)S(1)} %get-tuple-element.19.base_ref, f32[36,384]{1,0:T(8,128)S(1)} %get-tuple-element.20.weight_ref, bf16[1,384,8192]{2,1,0:T(8,128)(2,1)S(1)} %bitcast.6, bf16[24,2048]{1,0:T(8,128)(2,1)S(1)} %pack.1.rest_0_, bf16[24,2048]{1,0:T(8,128)(2,1)S(1)} %collective-permute-done.3.rest_1_, ...), custom_call_target="tpu_custom_call" | custom-call | tf_op jit(solution)/shard_map/backward/pallas_call | solution.py:359
  (2 shorter events, 0.0 us)
Async XLA Ops:
  0.0 9.7 %copy-start = (s32[12]{0:T(128)S(1)}, s32[12]{0:T(128)}, u32[]{:S(2)}) copy-start(s32[12]{0:T(128)} %npix_ref.3) | copy-start | bytes 148
  0.0 9.7 %copy-start.1 = (s32[64]{0:T(128)S(1)}, s32[64]{0:T(128)}, u32[]{:S(2)}) copy-start(s32[64]{0:T(128)} %param.14) | copy-start | bytes 772
  4.0 8.1 %collective-permute-start = (bf16[24,2048]{1,0:T(8,128)(2,1)S(1)}, bf16[24,2048]{1,0:T(8,128)(2,1)S(1)}, u32[]{:S(2)}, u32[]{:S(2)}) collective-permute-start(bf16[24,2048]{1,0:T(8,128)(2,1)S(1)} %get-tuple-element.24), channel_id=1, source_target_pairs={{0,64},{64,128},{128,192},{192,0},{1,65},{65,129},{129,193},{193,1... | collective-permute-start | bytes 294920 | tf_op jit(solution)/shard_map/ppermute | solution.py:379
  6.1 6.5 %collective-permute-start.1 = (bf16[24,2048]{1,0:T(8,128)(2,1)S(1)}, bf16[24,2048]{1,0:T(8,128)(2,1)S(1)}, u32[]{:S(2)}, u32[]{:S(2)}) collective-permute-start(bf16[24,2048]{1,0:T(8,128)(2,1)S(1)} %get-tuple-element.25), channel_id=1, source_target_pairs={{0,128},{64,192},{128,0},{192,64},{1,129},{65,193},{129,1},{193,65... | collective-permute-start | bytes 294920 | tf_op jit(solution)/shard_map/ppermute | solution.py:379
  8.5 4.0 %collective-permute-start.2 = (bf16[24,2048]{1,0:T(8,128)(2,1)S(1)}, bf16[24,2048]{1,0:T(8,128)(2,1)S(1)}, u32[]{:S(2)}, u32[]{:S(2)}) collective-permute-start(bf16[24,2048]{1,0:T(8,128)(2,1)S(1)} %get-tuple-element.26), channel_id=1, source_target_pairs={{0,192},{64,0},{128,64},{192,128},{1,193},{65,1},{129,65},{193,129... | collective-permute-start | bytes 294920 | tf_op jit(solution)/shard_map/ppermute | solution.py:379
  12.6 51.0 %slice-start = ((s8[6291456]{0:T(1024)(128)(4,1)}), s8[4194304]{0:T(1024)(128)(4,1)S(1)}, s32[]{:S(2)}) async-start(s8[6291456]{0:T(1024)(128)(4,1)} %bitcast.5), calls=%async_computation.2 | async-start | bytes 8388608
  36.1 27.4 %slice-start.1 = ((s8[6291456]{0:T(1024)(128)(4,1)}), s8[2097152]{0:T(1024)(128)(4,1)S(1)}, s32[]{:S(2)}) async-start(s8[6291456]{0:T(1024)(128)(4,1)} %bitcast.5), calls=%async_computation.3 | async-start | bytes 4194304
  54.0 5.3 %collective-permute-start.5 = (bf16[24,2048]{1,0:T(8,128)(2,1)S(1)}, bf16[24,2048]{1,0:T(8,128)(2,1)S(1)}, u32[]{:S(2)}, u32[]{:S(2)}) collective-permute-start(bf16[24,2048]{1,0:T(8,128)(2,1)S(1)} %pack.1.rest_0_), channel_id=1, source_target_pairs={{0,192},{64,0},{128,64},{192,128},{1,193},{65,1},{129,65},{193,129... | collective-permute-start | bytes 294920 | tf_op jit(solution)/shard_map/ppermute | solution.py:379
  57.1 5.0 %collective-permute-start.4 = (bf16[24,2048]{1,0:T(8,128)(2,1)S(1)}, bf16[24,2048]{1,0:T(8,128)(2,1)S(1)}, u32[]{:S(2)}, u32[]{:S(2)}) collective-permute-start(bf16[24,2048]{1,0:T(8,128)(2,1)S(1)} %pack.1.rest_0_), channel_id=1, source_target_pairs={{0,128},{64,192},{128,0},{192,64},{1,129},{65,193},{129,1},{193,65... | collective-permute-start | bytes 294920 | tf_op jit(solution)/shard_map/ppermute | solution.py:379
  58.6 5.0 %collective-permute-start.3 = (bf16[24,2048]{1,0:T(8,128)(2,1)S(1)}, bf16[24,2048]{1,0:T(8,128)(2,1)S(1)}, u32[]{:S(2)}, u32[]{:S(2)}) collective-permute-start(bf16[24,2048]{1,0:T(8,128)(2,1)S(1)} %pack.1.rest_0_), channel_id=1, source_target_pairs={{0,64},{64,128},{128,192},{192,0},{1,65},{65,129},{129,193},{193,1... | collective-permute-start | bytes 294920 | tf_op jit(solution)/shard_map/ppermute | solution.py:379

commit v6 on v5

--- a/solution.py
+++ b/solution.py
@@ -12,7 +12,7 @@
 LANES = 128
 ROWS = 8
 QUARTERS = 4
-STEPS = 4
+STEPS = 8
 FINE = 64
 SINE = [(-1) ** n / math.factorial(2 * n + 1) for n in range(6)]
 
@@ -65,8 +65,10 @@
         )
         for q in range(STEPS)
     ]
-    for copy in small_copies + copies:
+    for copy in small_copies:
         copy.start()
+    for copy in copies:
+        copy.start(priority=1)
     for copy in small_copies:
         copy.wait()
     chan_pos = lax.axis_index("chan")
@@ -330,17 +332,17 @@
     used = height // QUARTERS
     comps = base_ref.shape[0] // 2
     rows = jnp.concatenate([part[...] for part in parts], axis=0)
-    owner = lax.broadcasted_iota(jnp.int32, rows.shape, 0) % height // used
+    local_deg = leg_ref.shape[1]
+    owner = lax.broadcasted_iota(jnp.int32, (local_deg, rows.shape[0]), 1) % height // used
     total = None
     for q in range(QUARTERS):
-        mine = jnp.where(owner == q, rows.astype(jnp.float32), 0.0).astype(jnp.bfloat16)
         product = lax.dot_general(
             leg_ref[0, :, q * block : (q + 1) * block],
-            mine,
+            rows,
             (((1,), (1,)), ((), ())),
             preferred_element_type=jnp.float32,
         )
-        total = product if q == 0 else total + product
+        total = product if q == 0 else jnp.where(owner == q, product, total)
     acc_ref[...] = total.T
     sums = [base_ref[pl.ds(2 * k, 2), :] for k in range(comps)]
     for s in range(len(parts)):

time: 66.7 us -> 65.7 us (0.985)
  starting transfers between devices: 11 us -> 9.4 us
  waiting for transfers between devices: 4.73 us -> 5.56 us
    ppermute x6, starting transfers between devices: 11 us -> 9.4 us  [shift(): return lax.ppermute(x, 'chan', [(d, (d + s) % chans) for d in range(chans)])]
    ppermute x6, waiting for transfers between devices: 4.73 us -> 5.56 us  [shift(): return lax.ppermute(x, 'chan', [(d, (d + s) % chans) for d in range(chans)])]
  transfers between devices with their start and end apart: 6 -> 6, of which waited for: 3 -> 4; matrix products, arithmetic and copies ran while one was open for 0% -> 0% of each run, Pallas kernels for 4% -> 4%
where the time goes in v6:
time: 65.7 us; the launch traced here: 64.6 us
  blocking collectives  38.6 us (59%)
  Pallas kernels  11.1 us (17%)
  starting transfers between devices  9.4 us (14%)
  waiting for transfers between devices  5.56 us (8%)
    all_to_all x1, blocking collectives, on_device(): lax.all_to_all(chunks, ('mset', 'blk'), split_axis=0, concat_axis=0, tile...  23.5 us
    all_to_all x1, blocking collectives, on_device(): lax.all_to_all(returned, ('mset', 'blk'), split_axis=0, concat_axis=0, ti...  15.1 us
    ppermute x6, starting transfers between devices, shift(): return lax.ppermute(x, 'chan', [(d, (d + s) % chans) for d in range(chans)])  9.4 us
    ppermute x6, waiting for transfers between devices, shift(): return lax.ppermute(x, 'chan', [(d, (d + s) % chans) for d in range(chans)])  5.56 us
    pallas_call x1, Pallas kernels, forward(): pl.pallas_call(functools.partial(forward_body, chans, slots, pixels), in_...  3.33 us
    pallas_call x1, Pallas kernels, middle(): pl.pallas_call(middle_body, in_specs=[whole(pltpu.SMEM), whole(), whole()...  2.82 us
    pallas_call x1, Pallas kernels, backward(): pl.pallas_call(backward_body, in_specs=[whole()] * (3 + len(parts)), out_...  2.49 us
    pallas_call x1, Pallas kernels, make_tables(): pl.pallas_call(table_body, in_specs=[whole(pltpu.SMEM), whole(), whole(pl...  2.34 us
  transfers between devices with their start and end apart: 6, of which 4 were waited for; matrix products, arithmetic and copies ran while one was open for 0% of the time, Pallas kernels for 4%

profile of v6, /device:TPU:1, one launch (start us, length us, event | category | flops | bytes accessed | tf_op | source)
XLA Modules:
  0.0 64.6 jit_solution(12864927577278824947)
XLA Ops:
  0.0 0.0 copy-start
  0.0 0.0 copy-start.1
  0.0 3.3 %forward.1 = (bf16[24,2048]{1,0:T(8,128)(2,1)S(1)}, bf16[24,2048]{1,0:T(8,128)(2,1)S(1)}, bf16[24,2048]{1,0:T(8,128)(2,1)S(1)}, bf16[24,2048]{1,0:T(8,128)(2,1)S...) custom-call(s32[12]{0:T(128)} %npix_ref.3, f32[3,12]{1,0:T(4,128)} %bitcast.9, bf16[3,2,384]{2,1,0:T(2,128)(2,1)} %bitcast.8, ...), custom_call_target="tpu_custom_call" | custom-call | flops 201326592 | bytes 6291456 | tf_op jit(solution)/shard_map/forward/pallas_call | solution.py:110
  3.3 2.1 %collective-permute-start = (bf16[24,2048]{1,0:T(8,128)(2,1)S(1)}, bf16[24,2048]{1,0:T(8,128)(2,1)S(1)}, u32[]{:S(2)}, u32[]{:S(2)}) collective-permute-start(bf16[24,2048]{1,0:T(8,128)(2,1)S(1)} %get-tuple-element.24), channel_id=1, source_target_pairs={{0,64},{64,128},{128,192},{192,0},{1,65},{65,129},{129,193},{193,1... | collective-permute-start | bytes 294920 | tf_op jit(solution)/shard_map/ppermute | solution.py:381
  5.5 2.4 %collective-permute-start.1 = (bf16[24,2048]{1,0:T(8,128)(2,1)S(1)}, bf16[24,2048]{1,0:T(8,128)(2,1)S(1)}, u32[]{:S(2)}, u32[]{:S(2)}) collective-permute-start(bf16[24,2048]{1,0:T(8,128)(2,1)S(1)} %get-tuple-element.25), channel_id=1, source_target_pairs={{0,128},{64,192},{128,0},{192,64},{1,129},{65,193},{129,1},{193,65... | collective-permute-start | bytes 294920 | tf_op jit(solution)/shard_map/ppermute | solution.py:381
  7.9 1.2 %collective-permute-start.2 = (bf16[24,2048]{1,0:T(8,128)(2,1)S(1)}, bf16[24,2048]{1,0:T(8,128)(2,1)S(1)}, u32[]{:S(2)}, u32[]{:S(2)}) collective-permute-start(bf16[24,2048]{1,0:T(8,128)(2,1)S(1)} %get-tuple-element.26), channel_id=1, source_target_pairs={{0,192},{64,0},{128,64},{192,128},{1,193},{65,1},{129,65},{193,129... | collective-permute-start | bytes 294920 | tf_op jit(solution)/shard_map/ppermute | solution.py:381
  9.1 0.0 copy-done
  9.1 0.0 copy-done.1
  9.1 2.3 %make_tables.1 = (bf16[3,8192,128]{2,1,0:T(8,128)(2,1)S(1)}, bf16[3,128,8192]{2,1,0:T(8,128)(2,1)S(1)}) custom-call(s32[12]{0:T(128)S(1)} %copy-done, s32[1,64]{1,0:T(1,128)S(1)} %bitcast.7, bf16[3,128,8192]{2,1,0:T(8,128)(2,1)} %noise_any.1), custom_call_target="tpu_custom_call" | custom-call | flops 15728640 | bytes 6291456 | tf_op jit(solution)/shard_map/make_tables/pallas_call | solution.py:235
  11.4 0.0 collective-permute-done.refs_1_
  11.4 0.5 collective-permute-done.1.refs_2_
  11.9 0.0 collective-permute-done.2.refs_3_
  11.9 0.0 slice-start
  11.9 0.1 add_parts.1
  12.0 23.5 %all_to_all.10.spec_ref = bf16[64,8,128]{2,1,0:T(8,128)(2,1)S(1)} all-to-all(bf16[64,8,128]{2,1,0:T(8,128)(2,1)S(1)} %add_parts.1), channel_id=1, replica_groups=mesh['chan'=4,'mset'=8,'blk'=8] {'mset','blk'}, dimensions={0} | all-to-all | bytes 262144 | tf_op jit(solution)/shard_map/all_to_all | solution.py:390
  35.5 0.0 slice-start.1
  35.5 2.8 %middle.1 = bf16[64,8,128]{2,1,0:T(8,128)(2,1)S(1)} custom-call(s32[12]{0:T(128)S(1)} %copy-done, bf16[64,8,128]{2,1,0:T(8,128)(2,1)S(1)} %all_to_all.10.spec_ref, bf16[3,8192,128]{2,1,0:T(8,128)(2,1)S(1)} %get-tuple-element.31.table_ref, bf16[3,128,8192]{2,1,0:T(8,128)(2,1)S(1)} %get-tuple-element.32.noise_ref), custom_call_target="tpu_custom_call" | custom-call | tf_op jit(solution)/shard_map/middle/pallas_call | solution.py:295
  38.3 15.1 %all_to_all.11.chunk_ref = bf16[64,8,128]{2,1,0:T(8,128)(2,1)S(1)} all-to-all(bf16[64,8,128]{2,1,0:T(8,128)(2,1)S(1)} %middle.1), channel_id=1, replica_groups=mesh['chan'=4,'mset'=8,'blk'=8] {'mset','blk'}, dimensions={0} | all-to-all | bytes 262144 | tf_op jit(solution)/shard_map/all_to_all | solution.py:392
  53.4 3.0 %collective-permute-start.5 = (bf16[24,2048]{1,0:T(8,128)(2,1)S(1)}, bf16[24,2048]{1,0:T(8,128)(2,1)S(1)}, u32[]{:S(2)}, u32[]{:S(2)}) collective-permute-start(bf16[24,2048]{1,0:T(8,128)(2,1)S(1)} %pack.1.rest_0_), channel_id=1, source_target_pairs={{0,192},{64,0},{128,64},{192,128},{1,193},{65,1},{129,65},{193,129... | collective-permute-start | bytes 294920 | tf_op jit(solution)/shard_map/ppermute | solution.py:381
  56.4 0.0 collective-permute-start.4
  56.4 0.7 %collective-permute-start.3 = (bf16[24,2048]{1,0:T(8,128)(2,1)S(1)}, bf16[24,2048]{1,0:T(8,128)(2,1)S(1)}, u32[]{:S(2)}, u32[]{:S(2)}) collective-permute-start(bf16[24,2048]{1,0:T(8,128)(2,1)S(1)} %pack.1.rest_0_), channel_id=1, source_target_pairs={{0,64},{64,128},{128,192},{192,0},{1,65},{65,129},{129,193},{193,1... | collective-permute-start | bytes 294920 | tf_op jit(solution)/shard_map/ppermute | solution.py:381
  57.1 1.4 %collective-permute-done.5.rest_3_ = bf16[24,2048]{1,0:T(8,128)(2,1)S(1)} collective-permute-done((bf16[24,2048]{1,0:T(8,128)(2,1)S(1)}, bf16[24,2048]{1,0:T(8,128)(2,1)S(1)}, u32[]{:S(2)}, u32[]{:S(2)}) %collective-permute-start.5) | collective-permute-done | bytes 98336 | tf_op jit(solution)/shard_map/ppermute | solution.py:381
  58.5 3.0 %collective-permute-done.4.rest_2_ = bf16[24,2048]{1,0:T(8,128)(2,1)S(1)} collective-permute-done((bf16[24,2048]{1,0:T(8,128)(2,1)S(1)}, bf16[24,2048]{1,0:T(8,128)(2,1)S(1)}, u32[]{:S(2)}, u32[]{:S(2)}) %collective-permute-start.4) | collective-permute-done | bytes 98336 | tf_op jit(solution)/shard_map/ppermute | solution.py:381
  61.5 0.7 %collective-permute-done.3.rest_1_ = bf16[24,2048]{1,0:T(8,128)(2,1)S(1)} collective-permute-done((bf16[24,2048]{1,0:T(8,128)(2,1)S(1)}, bf16[24,2048]{1,0:T(8,128)(2,1)S(1)}, u32[]{:S(2)}, u32[]{:S(2)}) %collective-permute-start.3) | collective-permute-done | bytes 98336 | tf_op jit(solution)/shard_map/ppermute | solution.py:381
  62.2 0.0 slice-done
  62.2 0.0 slice-done.1
  62.2 2.5 %backward.1 = f32[2,3,1,384]{3,2,1,0:T(1,128)} custom-call(f32[6,384]{1,0:T(8,128)S(1)} %get-tuple-element.19.base_ref, f32[36,384]{1,0:T(8,128)S(1)} %get-tuple-element.20.weight_ref, bf16[1,384,8192]{2,1,0:T(8,128)(2,1)S(1)} %bitcast.6, bf16[24,2048]{1,0:T(8,128)(2,1)S(1)} %pack.1.rest_0_, bf16[24,2048]{1,0:T(8,128)(2,1)S(1)} %collective-permute-done.3.rest_1_, ...), custom_call_target="tpu_custom_call" | custom-call | tf_op jit(solution)/shard_map/backward/pallas_call | solution.py:361
  (2 shorter events, 0.0 us)
Async XLA Ops:
  0.0 9.1 %copy-start = (s32[12]{0:T(128)S(1)}, s32[12]{0:T(128)}, u32[]{:S(2)}) copy-start(s32[12]{0:T(128)} %npix_ref.3) | copy-start | bytes 148
  0.0 9.1 %copy-start.1 = (s32[64]{0:T(128)S(1)}, s32[64]{0:T(128)}, u32[]{:S(2)}) copy-start(s32[64]{0:T(128)} %param.14) | copy-start | bytes 772
  3.3 8.1 %collective-permute-start = (bf16[24,2048]{1,0:T(8,128)(2,1)S(1)}, bf16[24,2048]{1,0:T(8,128)(2,1)S(1)}, u32[]{:S(2)}, u32[]{:S(2)}) collective-permute-start(bf16[24,2048]{1,0:T(8,128)(2,1)S(1)} %get-tuple-element.24), channel_id=1, source_target_pairs={{0,64},{64,128},{128,192},{192,0},{1,65},{65,129},{129,193},{193,1... | collective-permute-start | bytes 294920 | tf_op jit(solution)/shard_map/ppermute | solution.py:381
  5.5 6.5 %collective-permute-start.1 = (bf16[24,2048]{1,0:T(8,128)(2,1)S(1)}, bf16[24,2048]{1,0:T(8,128)(2,1)S(1)}, u32[]{:S(2)}, u32[]{:S(2)}) collective-permute-start(bf16[24,2048]{1,0:T(8,128)(2,1)S(1)} %get-tuple-element.25), channel_id=1, source_target_pairs={{0,128},{64,192},{128,0},{192,64},{1,129},{65,193},{129,1},{193,65... | collective-permute-start | bytes 294920 | tf_op jit(solution)/shard_map/ppermute | solution.py:381
  7.9 4.0 %collective-permute-start.2 = (bf16[24,2048]{1,0:T(8,128)(2,1)S(1)}, bf16[24,2048]{1,0:T(8,128)(2,1)S(1)}, u32[]{:S(2)}, u32[]{:S(2)}) collective-permute-start(bf16[24,2048]{1,0:T(8,128)(2,1)S(1)} %get-tuple-element.26), channel_id=1, source_target_pairs={{0,192},{64,0},{128,64},{192,128},{1,193},{65,1},{129,65},{193,129... | collective-permute-start | bytes 294920 | tf_op jit(solution)/shard_map/ppermute | solution.py:381
  11.9 50.2 %slice-start = ((s8[6291456]{0:T(1024)(128)(4,1)}), s8[4194304]{0:T(1024)(128)(4,1)S(1)}, s32[]{:S(2)}) async-start(s8[6291456]{0:T(1024)(128)(4,1)} %bitcast.5), calls=%async_computation.2 | async-start | bytes 8388608
  35.5 26.6 %slice-start.1 = ((s8[6291456]{0:T(1024)(128)(4,1)}), s8[2097152]{0:T(1024)(128)(4,1)S(1)}, s32[]{:S(2)}) async-start(s8[6291456]{0:T(1024)(128)(4,1)} %bitcast.5), calls=%async_computation.3 | async-start | bytes 4194304
  53.4 5.1 %collective-permute-start.5 = (bf16[24,2048]{1,0:T(8,128)(2,1)S(1)}, bf16[24,2048]{1,0:T(8,128)(2,1)S(1)}, u32[]{:S(2)}, u32[]{:S(2)}) collective-permute-start(bf16[24,2048]{1,0:T(8,128)(2,1)S(1)} %pack.1.rest_0_), channel_id=1, source_target_pairs={{0,192},{64,0},{128,64},{192,128},{1,193},{65,1},{129,65},{193,129... | collective-permute-start | bytes 294920 | tf_op jit(solution)/shard_map/ppermute | solution.py:381
  56.4 5.1 %collective-permute-start.4 = (bf16[24,2048]{1,0:T(8,128)(2,1)S(1)}, bf16[24,2048]{1,0:T(8,128)(2,1)S(1)}, u32[]{:S(2)}, u32[]{:S(2)}) collective-permute-start(bf16[24,2048]{1,0:T(8,128)(2,1)S(1)} %pack.1.rest_0_), channel_id=1, source_target_pairs={{0,128},{64,192},{128,0},{192,64},{1,129},{65,193},{129,1},{193,65... | collective-permute-start | bytes 294920 | tf_op jit(solution)/shard_map/ppermute | solution.py:381
  56.4 5.7 %collective-permute-start.3 = (bf16[24,2048]{1,0:T(8,128)(2,1)S(1)}, bf16[24,2048]{1,0:T(8,128)(2,1)S(1)}, u32[]{:S(2)}, u32[]{:S(2)}) collective-permute-start(bf16[24,2048]{1,0:T(8,128)(2,1)S(1)} %pack.1.rest_0_), channel_id=1, source_target_pairs={{0,64},{64,128},{128,192},{192,0},{1,65},{65,129},{129,193},{193,1... | collective-permute-start | bytes 294920 | tf_op jit(solution)/shard_map/ppermute | solution.py:381

commit v7 on v6

--- a/solution.py
+++ b/solution.py
@@ -263,7 +263,6 @@
     for s in range(slots):
         halves = [full_ref[pl.ds(2 * s + i, mode_count, stride=ROWS), :] for i in range(2)]
         turned_ref[s] = jnp.concatenate(halves, axis=0).T.astype(jnp.bfloat16)
-    full_ref[...] = jnp.zeros((flat, LANES), jnp.float32)
 
     def one_channel(j, carry):
         spectra = turned_ref[j]
@@ -383,7 +382,7 @@
     *parts, base, weights = forward(
         cycle_pixels, mixing_t, harm, beam_window, prior_inv, legendre, chans, slots, pixels
     )
-    parts = [parts[0]] + [shift(parts[s], s) for s in range(1, chans)]
+    parts = [parts[0]] + [shift(parts[s], s) for s in (1, chans - 1, *range(2, chans - 1))]
     tables, noise = make_tables(cycle_pixels, mode_index[None, :], inv_noise)
     tables, noise, parts = lax.optimization_barrier((tables, noise, parts))
     chunks = add_parts(parts)

time: 65.7 us -> 65.3 us (level); the launches traced: 64.6 us -> 65.1 us
  Pallas kernels: 11.1 us -> 13.3 us
  starting transfers between devices: 9.4 us -> 7.28 us
    ppermute x6, starting transfers between devices: 9.4 us -> 7.28 us  [shift(): return lax.ppermute(x, 'chan', [(d, (d + s) % chans) for d in range(chans)])]
    pallas_call x1, Pallas kernels: 2.82 us -> 4.25 us  [middle(): pl.pallas_call(middle_body, in_specs=[whole(pltpu.SMEM), whole(), whole()...]
    pallas_call x1, Pallas kernels: 2.34 us -> 3.13 us  [make_tables(): pl.pallas_call(table_body, in_specs=[whole(pltpu.SMEM), whole(), whole(pl...]
  transfers between devices with their start and end apart: 6 -> 6, of which waited for: 4 -> 4; matrix products, arithmetic and copies ran while one was open for 0% -> 0% of each run, Pallas kernels for 4% -> 5%
where the time goes in v7:
time: 65.3 us; the launch traced here: 65.1 us
  blocking collectives  38.8 us (59%)
  Pallas kernels  13.3 us (20%)
  starting transfers between devices  7.28 us (11%)
  waiting for transfers between devices  5.65 us (9%)
    all_to_all x1, blocking collectives, on_device(): lax.all_to_all(chunks, ('mset', 'blk'), split_axis=0, concat_axis=0, tile...  23.8 us
    all_to_all x1, blocking collectives, on_device(): lax.all_to_all(returned, ('mset', 'blk'), split_axis=0, concat_axis=0, ti...  15.1 us
    ppermute x6, starting transfers between devices, shift(): return lax.ppermute(x, 'chan', [(d, (d + s) % chans) for d in range(chans)])  7.28 us
    ppermute x6, waiting for transfers between devices, shift(): return lax.ppermute(x, 'chan', [(d, (d + s) % chans) for d in range(chans)])  5.65 us
    pallas_call x1, Pallas kernels, middle(): pl.pallas_call(middle_body, in_specs=[whole(pltpu.SMEM), whole(), whole()...  4.25 us
    pallas_call x1, Pallas kernels, forward(): pl.pallas_call(functools.partial(forward_body, chans, slots, pixels), in_...  3.33 us
    pallas_call x1, Pallas kernels, make_tables(): pl.pallas_call(table_body, in_specs=[whole(pltpu.SMEM), whole(), whole(pl...  3.13 us
    pallas_call x1, Pallas kernels, backward(): pl.pallas_call(backward_body, in_specs=[whole()] * (3 + len(parts)), out_...  2.49 us
  transfers between devices with their start and end apart: 6, of which 4 were waited for; matrix products, arithmetic and copies ran while one was open for 0% of the time, Pallas kernels for 5%

profile of v7, /device:TPU:1, one launch (start us, length us, event | category | flops | bytes accessed | tf_op | source)
XLA Modules:
  0.0 65.1 jit_solution(6822861914403036702)
XLA Ops:
  0.0 0.0 copy-start
  0.0 0.0 copy-start.1
  0.0 3.3 %forward.1 = (bf16[24,2048]{1,0:T(8,128)(2,1)S(1)}, bf16[24,2048]{1,0:T(8,128)(2,1)S(1)}, bf16[24,2048]{1,0:T(8,128)(2,1)S(1)}, bf16[24,2048]{1,0:T(8,128)(2,1)S...) custom-call(s32[12]{0:T(128)} %npix_ref.3, f32[3,12]{1,0:T(4,128)} %bitcast.9, bf16[3,2,384]{2,1,0:T(2,128)(2,1)} %bitcast.8, ...), custom_call_target="tpu_custom_call" | custom-call | flops 201326592 | bytes 6291456 | tf_op jit(solution)/shard_map/forward/pallas_call | solution.py:110
  3.3 2.1 %collective-permute-start = (bf16[24,2048]{1,0:T(8,128)(2,1)S(1)}, bf16[24,2048]{1,0:T(8,128)(2,1)S(1)}, u32[]{:S(2)}, u32[]{:S(2)}) collective-permute-start(bf16[24,2048]{1,0:T(8,128)(2,1)S(1)} %get-tuple-element.24), channel_id=1, source_target_pairs={{0,64},{64,128},{128,192},{192,0},{1,65},{65,129},{129,193},{193,1... | collective-permute-start | bytes 294920 | tf_op jit(solution)/shard_map/ppermute | solution.py:380
  5.5 1.4 %collective-permute-start.1 = (bf16[24,2048]{1,0:T(8,128)(2,1)S(1)}, bf16[24,2048]{1,0:T(8,128)(2,1)S(1)}, u32[]{:S(2)}, u32[]{:S(2)}) collective-permute-start(bf16[24,2048]{1,0:T(8,128)(2,1)S(1)} %get-tuple-element.25), channel_id=1, source_target_pairs={{0,192},{64,0},{128,64},{192,128},{1,193},{65,1},{129,65},{193,129... | collective-permute-start | bytes 294920 | tf_op jit(solution)/shard_map/ppermute | solution.py:380
  6.8 1.6 %collective-permute-start.2 = (bf16[24,2048]{1,0:T(8,128)(2,1)S(1)}, bf16[24,2048]{1,0:T(8,128)(2,1)S(1)}, u32[]{:S(2)}, u32[]{:S(2)}) collective-permute-start(bf16[24,2048]{1,0:T(8,128)(2,1)S(1)} %get-tuple-element.26), channel_id=1, source_target_pairs={{0,128},{64,192},{128,0},{192,64},{1,129},{65,193},{129,1},{193,65... | collective-permute-start | bytes 294920 | tf_op jit(solution)/shard_map/ppermute | solution.py:380
  8.4 0.0 copy-done
  8.5 0.0 copy-done.1
  8.5 3.1 %make_tables.1 = (bf16[3,8192,128]{2,1,0:T(8,128)(2,1)S(1)}, bf16[3,128,8192]{2,1,0:T(8,128)(2,1)S(1)}) custom-call(s32[12]{0:T(128)S(1)} %copy-done, s32[1,64]{1,0:T(1,128)S(1)} %bitcast.7, bf16[3,128,8192]{2,1,0:T(8,128)(2,1)} %noise_any.1), custom_call_target="tpu_custom_call" | custom-call | flops 15728640 | bytes 6291456 | tf_op jit(solution)/shard_map/make_tables/pallas_call | solution.py:235
  11.6 0.0 collective-permute-done.refs_1_
  11.6 0.0 collective-permute-done.1.refs_2_
  11.6 0.6 collective-permute-done.2.refs_3_
  12.2 0.0 slice-start
  12.2 0.1 add_parts.1
  12.3 23.8 %all_to_all.10.spec_ref = bf16[64,8,128]{2,1,0:T(8,128)(2,1)S(1)} all-to-all(bf16[64,8,128]{2,1,0:T(8,128)(2,1)S(1)} %add_parts.1), channel_id=1, replica_groups=mesh['chan'=4,'mset'=8,'blk'=8] {'mset','blk'}, dimensions={0} | all-to-all | bytes 262144 | tf_op jit(solution)/shard_map/all_to_all | solution.py:389
  36.0 0.0 slice-start.1
  36.0 4.2 %middle.1 = bf16[64,8,128]{2,1,0:T(8,128)(2,1)S(1)} custom-call(s32[12]{0:T(128)S(1)} %copy-done, bf16[64,8,128]{2,1,0:T(8,128)(2,1)S(1)} %all_to_all.10.spec_ref, bf16[3,8192,128]{2,1,0:T(8,128)(2,1)S(1)} %get-tuple-element.31.table_ref, bf16[3,128,8192]{2,1,0:T(8,128)(2,1)S(1)} %get-tuple-element.32.noise_ref), custom_call_target="tpu_custom_call" | custom-call | tf_op jit(solution)/shard_map/middle/pallas_call | solution.py:294
  40.3 15.1 %all_to_all.11.chunk_ref = bf16[64,8,128]{2,1,0:T(8,128)(2,1)S(1)} all-to-all(bf16[64,8,128]{2,1,0:T(8,128)(2,1)S(1)} %middle.1), channel_id=1, replica_groups=mesh['chan'=4,'mset'=8,'blk'=8] {'mset','blk'}, dimensions={0} | all-to-all | bytes 262144 | tf_op jit(solution)/shard_map/all_to_all | solution.py:391
  55.4 0.2 collective-permute-start.5
  55.5 1.8 %collective-permute-start.4 = (bf16[24,2048]{1,0:T(8,128)(2,1)S(1)}, bf16[24,2048]{1,0:T(8,128)(2,1)S(1)}, u32[]{:S(2)}, u32[]{:S(2)}) collective-permute-start(bf16[24,2048]{1,0:T(8,128)(2,1)S(1)} %pack.1.rest_0_), channel_id=1, source_target_pairs={{0,128},{64,192},{128,0},{192,64},{1,129},{65,193},{129,1},{193,65... | collective-permute-start | bytes 294920 | tf_op jit(solution)/shard_map/ppermute | solution.py:380
  57.3 0.2 collective-permute-start.3
  57.5 1.4 %collective-permute-done.5.rest_3_ = bf16[24,2048]{1,0:T(8,128)(2,1)S(1)} collective-permute-done((bf16[24,2048]{1,0:T(8,128)(2,1)S(1)}, bf16[24,2048]{1,0:T(8,128)(2,1)S(1)}, u32[]{:S(2)}, u32[]{:S(2)}) %collective-permute-start.5) | collective-permute-done | bytes 98336 | tf_op jit(solution)/shard_map/ppermute | solution.py:380
  58.9 1.6 %collective-permute-done.4.rest_2_ = bf16[24,2048]{1,0:T(8,128)(2,1)S(1)} collective-permute-done((bf16[24,2048]{1,0:T(8,128)(2,1)S(1)}, bf16[24,2048]{1,0:T(8,128)(2,1)S(1)}, u32[]{:S(2)}, u32[]{:S(2)}) %collective-permute-start.4) | collective-permute-done | bytes 98336 | tf_op jit(solution)/shard_map/ppermute | solution.py:380
  60.5 2.1 %collective-permute-done.3.rest_1_ = bf16[24,2048]{1,0:T(8,128)(2,1)S(1)} collective-permute-done((bf16[24,2048]{1,0:T(8,128)(2,1)S(1)}, bf16[24,2048]{1,0:T(8,128)(2,1)S(1)}, u32[]{:S(2)}, u32[]{:S(2)}) %collective-permute-start.3) | collective-permute-done | bytes 98336 | tf_op jit(solution)/shard_map/ppermute | solution.py:380
  62.6 0.0 slice-done
  62.6 0.0 slice-done.1
  62.6 2.5 %backward.1 = f32[2,3,1,384]{3,2,1,0:T(1,128)} custom-call(f32[6,384]{1,0:T(8,128)S(1)} %get-tuple-element.19.base_ref, f32[36,384]{1,0:T(8,128)S(1)} %get-tuple-element.20.weight_ref, bf16[1,384,8192]{2,1,0:T(8,128)(2,1)S(1)} %bitcast.6, bf16[24,2048]{1,0:T(8,128)(2,1)S(1)} %pack.1.rest_0_, bf16[24,2048]{1,0:T(8,128)(2,1)S(1)} %collective-permute-done.3.rest_1_, ...), custom_call_target="tpu_custom_call" | custom-call | tf_op jit(solution)/shard_map/backward/pallas_call | solution.py:360
  (2 shorter events, 0.0 us)
Async XLA Ops:
  0.0 8.4 %copy-start = (s32[12]{0:T(128)S(1)}, s32[12]{0:T(128)}, u32[]{:S(2)}) copy-start(s32[12]{0:T(128)} %npix_ref.3) | copy-start | bytes 148
  0.0 8.5 %copy-start.1 = (s32[64]{0:T(128)S(1)}, s32[64]{0:T(128)}, u32[]{:S(2)}) copy-start(s32[64]{0:T(128)} %param.14) | copy-start | bytes 772
  3.3 8.3 %collective-permute-start = (bf16[24,2048]{1,0:T(8,128)(2,1)S(1)}, bf16[24,2048]{1,0:T(8,128)(2,1)S(1)}, u32[]{:S(2)}, u32[]{:S(2)}) collective-permute-start(bf16[24,2048]{1,0:T(8,128)(2,1)S(1)} %get-tuple-element.24), channel_id=1, source_target_pairs={{0,64},{64,128},{128,192},{192,0},{1,65},{65,129},{129,193},{193,1... | collective-permute-start | bytes 294920 | tf_op jit(solution)/shard_map/ppermute | solution.py:380
  5.5 6.2 %collective-permute-start.1 = (bf16[24,2048]{1,0:T(8,128)(2,1)S(1)}, bf16[24,2048]{1,0:T(8,128)(2,1)S(1)}, u32[]{:S(2)}, u32[]{:S(2)}) collective-permute-start(bf16[24,2048]{1,0:T(8,128)(2,1)S(1)} %get-tuple-element.25), channel_id=1, source_target_pairs={{0,192},{64,0},{128,64},{192,128},{1,193},{65,1},{129,65},{193,129... | collective-permute-start | bytes 294920 | tf_op jit(solution)/shard_map/ppermute | solution.py:380
  6.8 5.4 %collective-permute-start.2 = (bf16[24,2048]{1,0:T(8,128)(2,1)S(1)}, bf16[24,2048]{1,0:T(8,128)(2,1)S(1)}, u32[]{:S(2)}, u32[]{:S(2)}) collective-permute-start(bf16[24,2048]{1,0:T(8,128)(2,1)S(1)} %get-tuple-element.26), channel_id=1, source_target_pairs={{0,128},{64,192},{128,0},{192,64},{1,129},{65,193},{129,1},{193,65... | collective-permute-start | bytes 294920 | tf_op jit(solution)/shard_map/ppermute | solution.py:380
  12.2 50.4 %slice-start = ((s8[6291456]{0:T(1024)(128)(4,1)}), s8[4194304]{0:T(1024)(128)(4,1)S(1)}, s32[]{:S(2)}) async-start(s8[6291456]{0:T(1024)(128)(4,1)} %bitcast.5), calls=%async_computation.2 | async-start | bytes 8388608
  36.0 26.6 %slice-start.1 = ((s8[6291456]{0:T(1024)(128)(4,1)}), s8[2097152]{0:T(1024)(128)(4,1)S(1)}, s32[]{:S(2)}) async-start(s8[6291456]{0:T(1024)(128)(4,1)} %bitcast.5), calls=%async_computation.3 | async-start | bytes 4194304
  55.4 3.5 %collective-permute-start.5 = (bf16[24,2048]{1,0:T(8,128)(2,1)S(1)}, bf16[24,2048]{1,0:T(8,128)(2,1)S(1)}, u32[]{:S(2)}, u32[]{:S(2)}) collective-permute-start(bf16[24,2048]{1,0:T(8,128)(2,1)S(1)} %pack.1.rest_0_), channel_id=1, source_target_pairs={{0,192},{64,0},{128,64},{192,128},{1,193},{65,1},{129,65},{193,129... | collective-permute-start | bytes 294920 | tf_op jit(solution)/shard_map/ppermute | solution.py:380
  55.5 5.0 %collective-permute-start.4 = (bf16[24,2048]{1,0:T(8,128)(2,1)S(1)}, bf16[24,2048]{1,0:T(8,128)(2,1)S(1)}, u32[]{:S(2)}, u32[]{:S(2)}) collective-permute-start(bf16[24,2048]{1,0:T(8,128)(2,1)S(1)} %pack.1.rest_0_), channel_id=1, source_target_pairs={{0,128},{64,192},{128,0},{192,64},{1,129},{65,193},{129,1},{193,65... | collective-permute-start | bytes 294920 | tf_op jit(solution)/shard_map/ppermute | solution.py:380
  57.3 5.3 %collective-permute-start.3 = (bf16[24,2048]{1,0:T(8,128)(2,1)S(1)}, bf16[24,2048]{1,0:T(8,128)(2,1)S(1)}, u32[]{:S(2)}, u32[]{:S(2)}) collective-permute-start(bf16[24,2048]{1,0:T(8,128)(2,1)S(1)} %pack.1.rest_0_), channel_id=1, source_target_pairs={{0,64},{64,128},{128,192},{192,0},{1,65},{65,129},{129,193},{193,1... | collective-permute-start | bytes 294920 | tf_op jit(solution)/shard_map/ppermute | solution.py:380

commit v8 on v7

--- a/solution.py
+++ b/solution.py
@@ -32,6 +32,10 @@
 def filter_row(beam_ref, npix_ref, channel, degrees, total_deg, pixels):
     band_limit = total_deg * npix_ref[channel] // pixels - 1
     return jnp.where(degrees <= band_limit, beam_ref[pl.ds(channel, 1), :], 0.0)
+
+
+def last_order(chans):
+    return [0, 1, chans - 1, *range(2, chans - 1)]
 
 
 def degrees_of(shape, chan_pos):
@@ -82,7 +86,8 @@
             filt = filter_row(beam_ref, npix_ref, c, degrees, local_deg * chans, pixels)
             rows_ref[pl.ds(s * ROWS + 2 * j, 2), :] = mixture * filt
             for k in range(len(comps)):
-                row = ((chans - s) % chans * slots + j) * len(comps) + k
+                place = last_order(chans).index((chans - s) % chans)
+                row = (place * slots + j) * len(comps) + k
                 weight_ref[pl.ds(row, 1), :] = mix_ref[k, c] * filt
         rest_rows = ROWS - 2 * slots
         rows_ref[pl.ds(s * ROWS + 2 * slots, rest_rows), :] = jnp.zeros(
@@ -254,7 +259,9 @@
     )(npix, modes, *in_hbm(inv_noise))
 
 
-def middle_body(npix_ref, spec_ref, table_ref, noise_ref, out_ref, full_ref, turned_ref):
+def middle_body(npix_any, spec_ref, table_ref, noise_ref, out_ref, full_ref, turned_ref, npix_ref, sem):
+    copy = pltpu.make_async_copy(npix_any, npix_ref, sem)
+    copy.start()
     mode_count = spec_ref.shape[0]
     slots, _, pixels = noise_ref.shape
     flat = mode_count * ROWS
@@ -263,6 +270,8 @@
     for s in range(slots):
         halves = [full_ref[pl.ds(2 * s + i, mode_count, stride=ROWS), :] for i in range(2)]
         turned_ref[s] = jnp.concatenate(halves, axis=0).T.astype(jnp.bfloat16)
+
+    copy.wait()
 
     def one_channel(j, carry):
         spectra = turned_ref[j]
@@ -293,12 +302,14 @@
     mode_count = spectra.shape[0]
     return pl.pallas_call(
         middle_body,
-        in_specs=[whole(pltpu.SMEM), whole(), whole(), whole()],
+        in_specs=[whole(pl.ANY), whole(), whole(), whole()],
         out_specs=whole(),
         out_shape=jax.ShapeDtypeStruct(spectra.shape, jnp.bfloat16),
         scratch_shapes=[
             pltpu.VMEM((mode_count * ROWS, LANES), jnp.float32),
             pltpu.VMEM((slots, cycle_dev, 2 * mode_count), jnp.bfloat16),
+            pltpu.SMEM(npix.shape, npix.dtype),
+            pltpu.SemaphoreType.DMA,
         ],
         compiler_params=pltpu.CompilerParams(vmem_limit_bytes=20 * MIB),
         name="middle",
@@ -390,7 +401,7 @@
     returned = middle(cycle_pixels, spectra, tables, noise)
     own = lax.all_to_all(returned, ("mset", "blk"), split_axis=0, concat_axis=0, tiled=True)
     own = pack(own, 2 * slots)
-    gathered = [own] + [shift(own, s) for s in range(1, chans)]
+    gathered = [own] + [shift(own, s) for s in last_order(chans)[1:]]
     return backward(base, weights, legendre, gathered)
 
 

time: 65.3 us -> 65.7 us (level)
  waiting for transfers between devices: 5.65 us -> 4.9 us
    ppermute x6, waiting for transfers between devices: 5.65 us -> 4.9 us  [shift(): return lax.ppermute(x, 'chan', [(d, (d + s) % chans) for d in range(chans)])]
where the time goes in v8:
time: 65.7 us; the launch traced here: 64.9 us
  blocking collectives  38.8 us (59%)
  Pallas kernels  13.2 us (20%)
  starting transfers between devices  7.89 us (12%)
  waiting for transfers between devices  4.9 us (7%)
    all_to_all x1, blocking collectives, on_device(): lax.all_to_all(chunks, ('mset', 'blk'), split_axis=0, concat_axis=0, tile...  23.8 us
    all_to_all x1, blocking collectives, on_device(): lax.all_to_all(returned, ('mset', 'blk'), split_axis=0, concat_axis=0, ti...  15.1 us
    ppermute x6, starting transfers between devices, shift(): return lax.ppermute(x, 'chan', [(d, (d + s) % chans) for d in range(chans)])  7.89 us
    ppermute x6, waiting for transfers between devices, shift(): return lax.ppermute(x, 'chan', [(d, (d + s) % chans) for d in range(chans)])  4.9 us
    pallas_call x1, Pallas kernels, middle(): pl.pallas_call(middle_body, in_specs=[whole(pl.ANY), whole(), whole(), wh...  4.15 us
    pallas_call x1, Pallas kernels, forward(): pl.pallas_call(functools.partial(forward_body, chans, slots, pixels), in_...  3.33 us
    pallas_call x1, Pallas kernels, make_tables(): pl.pallas_call(table_body, in_specs=[whole(pltpu.SMEM), whole(), whole(pl...  3.13 us
    pallas_call x1, Pallas kernels, backward(): pl.pallas_call(backward_body, in_specs=[whole()] * (3 + len(parts)), out_...  2.49 us
  transfers between devices with their start and end apart: 6, of which 4 were waited for; matrix products, arithmetic and copies ran while one was open for 0% of the time, Pallas kernels for 5%

profile of v8, /device:TPU:1, one launch (start us, length us, event | category | flops | bytes accessed | tf_op | source)
XLA Modules:
  0.0 64.9 jit_solution(15637991005203731155)
XLA Ops:
  0.0 0.0 copy-start
  0.0 0.0 copy-start.1
  0.0 3.3 %forward.1 = (bf16[24,2048]{1,0:T(8,128)(2,1)S(1)}, bf16[24,2048]{1,0:T(8,128)(2,1)S(1)}, bf16[24,2048]{1,0:T(8,128)(2,1)S(1)}, bf16[24,2048]{1,0:T(8,128)(2,1)S...) custom-call(s32[12]{0:T(128)} %npix_any.3, f32[3,12]{1,0:T(4,128)} %bitcast.9, bf16[3,2,384]{2,1,0:T(2,128)(2,1)} %bitcast.8, ...), custom_call_target="tpu_custom_call" | custom-call | flops 201326592 | bytes 6291456 | tf_op jit(solution)/shard_map/forward/pallas_call | solution.py:115
  3.3 2.1 %collective-permute-start = (bf16[24,2048]{1,0:T(8,128)(2,1)S(1)}, bf16[24,2048]{1,0:T(8,128)(2,1)S(1)}, u32[]{:S(2)}, u32[]{:S(2)}) collective-permute-start(bf16[24,2048]{1,0:T(8,128)(2,1)S(1)} %get-tuple-element.24), channel_id=1, source_target_pairs={{0,64},{64,128},{128,192},{192,0},{1,65},{65,129},{129,193},{193,1... | collective-permute-start | bytes 294920 | tf_op jit(solution)/shard_map/ppermute | solution.py:391
  5.5 1.4 %collective-permute-start.1 = (bf16[24,2048]{1,0:T(8,128)(2,1)S(1)}, bf16[24,2048]{1,0:T(8,128)(2,1)S(1)}, u32[]{:S(2)}, u32[]{:S(2)}) collective-permute-start(bf16[24,2048]{1,0:T(8,128)(2,1)S(1)} %get-tuple-element.25), channel_id=1, source_target_pairs={{0,192},{64,0},{128,64},{192,128},{1,193},{65,1},{129,65},{193,129... | collective-permute-start | bytes 294920 | tf_op jit(solution)/shard_map/ppermute | solution.py:391
  6.8 1.6 %collective-permute-start.2 = (bf16[24,2048]{1,0:T(8,128)(2,1)S(1)}, bf16[24,2048]{1,0:T(8,128)(2,1)S(1)}, u32[]{:S(2)}, u32[]{:S(2)}) collective-permute-start(bf16[24,2048]{1,0:T(8,128)(2,1)S(1)} %get-tuple-element.26), channel_id=1, source_target_pairs={{0,128},{64,192},{128,0},{192,64},{1,129},{65,193},{129,1},{193,65... | collective-permute-start | bytes 294920 | tf_op jit(solution)/shard_map/ppermute | solution.py:391
  8.4 0.0 copy-done
  8.5 0.0 copy-done.1
  8.5 3.1 %make_tables.1 = (bf16[3,8192,128]{2,1,0:T(8,128)(2,1)S(1)}, bf16[3,128,8192]{2,1,0:T(8,128)(2,1)S(1)}) custom-call(s32[12]{0:T(128)S(1)} %copy-done, s32[1,64]{1,0:T(1,128)S(1)} %bitcast.7, bf16[3,128,8192]{2,1,0:T(8,128)(2,1)} %noise_any.1), custom_call_target="tpu_custom_call" | custom-call | flops 15728640 | bytes 6291456 | tf_op jit(solution)/shard_map/make_tables/pallas_call | solution.py:240
  11.6 0.0 collective-permute-done.refs_1_
  11.6 0.0 collective-permute-done.1.refs_2_
  11.6 0.6 collective-permute-done.2.refs_3_
  12.2 0.0 slice-start
  12.2 0.1 add_parts.1
  12.3 23.8 %all_to_all.10.spec_ref = bf16[64,8,128]{2,1,0:T(8,128)(2,1)S(1)} all-to-all(bf16[64,8,128]{2,1,0:T(8,128)(2,1)S(1)} %add_parts.1), channel_id=1, replica_groups=mesh['chan'=4,'mset'=8,'blk'=8] {'mset','blk'}, dimensions={0} | all-to-all | bytes 262144 | tf_op jit(solution)/shard_map/all_to_all | solution.py:400
  36.0 0.0 slice-start.1
  36.0 4.1 %middle.1 = bf16[64,8,128]{2,1,0:T(8,128)(2,1)S(1)} custom-call(s32[12]{0:T(128)S(1)} %copy-done, bf16[64,8,128]{2,1,0:T(8,128)(2,1)S(1)} %all_to_all.10.spec_ref, bf16[3,8192,128]{2,1,0:T(8,128)(2,1)S(1)} %get-tuple-element.31.table_ref, bf16[3,128,8192]{2,1,0:T(8,128)(2,1)S(1)} %get-tuple-element.32.noise_ref), custom_call_target="tpu_custom_call" | custom-call | tf_op jit(solution)/shard_map/middle/pallas_call | solution.py:303
  40.2 15.1 %all_to_all.11.chunk_ref = bf16[64,8,128]{2,1,0:T(8,128)(2,1)S(1)} all-to-all(bf16[64,8,128]{2,1,0:T(8,128)(2,1)S(1)} %middle.1), channel_id=1, replica_groups=mesh['chan'=4,'mset'=8,'blk'=8] {'mset','blk'}, dimensions={0} | all-to-all | bytes 262144 | tf_op jit(solution)/shard_map/all_to_all | solution.py:402
  55.3 1.3 %collective-permute-start.5 = (bf16[24,2048]{1,0:T(8,128)(2,1)S(1)}, bf16[24,2048]{1,0:T(8,128)(2,1)S(1)}, u32[]{:S(2)}, u32[]{:S(2)}) collective-permute-start(bf16[24,2048]{1,0:T(8,128)(2,1)S(1)} %pack.1.rest_0_), channel_id=1, source_target_pairs={{0,128},{64,192},{128,0},{192,64},{1,129},{65,193},{129,1},{193,65... | collective-permute-start | bytes 294920 | tf_op jit(solution)/shard_map/ppermute | solution.py:391
  56.6 0.4 collective-permute-start.4
  57.0 1.1 %collective-permute-start.3 = (bf16[24,2048]{1,0:T(8,128)(2,1)S(1)}, bf16[24,2048]{1,0:T(8,128)(2,1)S(1)}, u32[]{:S(2)}, u32[]{:S(2)}) collective-permute-start(bf16[24,2048]{1,0:T(8,128)(2,1)S(1)} %pack.1.rest_0_), channel_id=1, source_target_pairs={{0,64},{64,128},{128,192},{192,0},{1,65},{65,129},{129,193},{193,1... | collective-permute-start | bytes 294920 | tf_op jit(solution)/shard_map/ppermute | solution.py:391
  58.0 2.3 %collective-permute-done.5.rest_3_ = bf16[24,2048]{1,0:T(8,128)(2,1)S(1)} collective-permute-done((bf16[24,2048]{1,0:T(8,128)(2,1)S(1)}, bf16[24,2048]{1,0:T(8,128)(2,1)S(1)}, u32[]{:S(2)}, u32[]{:S(2)}) %collective-permute-start.5) | collective-permute-done | bytes 98336 | tf_op jit(solution)/shard_map/ppermute | solution.py:391
  60.3 0.4 collective-permute-done.4.rest_2_
  60.8 1.6 %collective-permute-done.3.rest_1_ = bf16[24,2048]{1,0:T(8,128)(2,1)S(1)} collective-permute-done((bf16[24,2048]{1,0:T(8,128)(2,1)S(1)}, bf16[24,2048]{1,0:T(8,128)(2,1)S(1)}, u32[]{:S(2)}, u32[]{:S(2)}) %collective-permute-start.3) | collective-permute-done | bytes 98336 | tf_op jit(solution)/shard_map/ppermute | solution.py:391
  62.4 0.0 slice-done
  62.4 0.0 slice-done.1
  62.4 2.5 %backward.1 = f32[2,3,1,384]{3,2,1,0:T(1,128)} custom-call(f32[6,384]{1,0:T(8,128)S(1)} %get-tuple-element.19.base_ref, f32[36,384]{1,0:T(8,128)S(1)} %get-tuple-element.20.weight_ref, bf16[1,384,8192]{2,1,0:T(8,128)(2,1)S(1)} %bitcast.6, bf16[24,2048]{1,0:T(8,128)(2,1)S(1)} %pack.1.rest_0_, bf16[24,2048]{1,0:T(8,128)(2,1)S(1)} %collective-permute-done.3.rest_1_, ...), custom_call_target="tpu_custom_call" | custom-call | tf_op jit(solution)/shard_map/backward/pallas_call | solution.py:371
  (2 shorter events, 0.0 us)
Async XLA Ops:
  0.0 8.4 %copy-start = (s32[12]{0:T(128)S(1)}, s32[12]{0:T(128)}, u32[]{:S(2)}) copy-start(s32[12]{0:T(128)} %npix_any.3) | copy-start | bytes 148
  0.0 8.5 %copy-start.1 = (s32[64]{0:T(128)S(1)}, s32[64]{0:T(128)}, u32[]{:S(2)}) copy-start(s32[64]{0:T(128)} %param.14) | copy-start | bytes 772
  3.3 8.3 %collective-permute-start = (bf16[24,2048]{1,0:T(8,128)(2,1)S(1)}, bf16[24,2048]{1,0:T(8,128)(2,1)S(1)}, u32[]{:S(2)}, u32[]{:S(2)}) collective-permute-start(bf16[24,2048]{1,0:T(8,128)(2,1)S(1)} %get-tuple-element.24), channel_id=1, source_target_pairs={{0,64},{64,128},{128,192},{192,0},{1,65},{65,129},{129,193},{193,1... | collective-permute-start | bytes 294920 | tf_op jit(solution)/shard_map/ppermute | solution.py:391
  5.5 6.2 %collective-permute-start.1 = (bf16[24,2048]{1,0:T(8,128)(2,1)S(1)}, bf16[24,2048]{1,0:T(8,128)(2,1)S(1)}, u32[]{:S(2)}, u32[]{:S(2)}) collective-permute-start(bf16[24,2048]{1,0:T(8,128)(2,1)S(1)} %get-tuple-element.25), channel_id=1, source_target_pairs={{0,192},{64,0},{128,64},{192,128},{1,193},{65,1},{129,65},{193,129... | collective-permute-start | bytes 294920 | tf_op jit(solution)/shard_map/ppermute | solution.py:391
  6.8 5.4 %collective-permute-start.2 = (bf16[24,2048]{1,0:T(8,128)(2,1)S(1)}, bf16[24,2048]{1,0:T(8,128)(2,1)S(1)}, u32[]{:S(2)}, u32[]{:S(2)}) collective-permute-start(bf16[24,2048]{1,0:T(8,128)(2,1)S(1)} %get-tuple-element.26), channel_id=1, source_target_pairs={{0,128},{64,192},{128,0},{192,64},{1,129},{65,193},{129,1},{193,65... | collective-permute-start | bytes 294920 | tf_op jit(solution)/shard_map/ppermute | solution.py:391
  12.2 50.2 %slice-start = ((s8[6291456]{0:T(1024)(128)(4,1)}), s8[4194304]{0:T(1024)(128)(4,1)S(1)}, s32[]{:S(2)}) async-start(s8[6291456]{0:T(1024)(128)(4,1)} %bitcast.5), calls=%async_computation.2 | async-start | bytes 8388608
  36.0 26.3 %slice-start.1 = ((s8[6291456]{0:T(1024)(128)(4,1)}), s8[2097152]{0:T(1024)(128)(4,1)S(1)}, s32[]{:S(2)}) async-start(s8[6291456]{0:T(1024)(128)(4,1)} %bitcast.5), calls=%async_computation.3 | async-start | bytes 4194304
  55.3 5.1 %collective-permute-start.5 = (bf16[24,2048]{1,0:T(8,128)(2,1)S(1)}, bf16[24,2048]{1,0:T(8,128)(2,1)S(1)}, u32[]{:S(2)}, u32[]{:S(2)}) collective-permute-start(bf16[24,2048]{1,0:T(8,128)(2,1)S(1)} %pack.1.rest_0_), channel_id=1, source_target_pairs={{0,128},{64,192},{128,0},{192,64},{1,129},{65,193},{129,1},{193,65... | collective-permute-start | bytes 294920 | tf_op jit(solution)/shard_map/ppermute | solution.py:391
  56.6 4.2 %collective-permute-start.4 = (bf16[24,2048]{1,0:T(8,128)(2,1)S(1)}, bf16[24,2048]{1,0:T(8,128)(2,1)S(1)}, u32[]{:S(2)}, u32[]{:S(2)}) collective-permute-start(bf16[24,2048]{1,0:T(8,128)(2,1)S(1)} %pack.1.rest_0_), channel_id=1, source_target_pairs={{0,192},{64,0},{128,64},{192,128},{1,193},{65,1},{129,65},{193,129... | collective-permute-start | bytes 294920 | tf_op jit(solution)/shard_map/ppermute | solution.py:391
  57.0 5.4 %collective-permute-start.3 = (bf16[24,2048]{1,0:T(8,128)(2,1)S(1)}, bf16[24,2048]{1,0:T(8,128)(2,1)S(1)}, u32[]{:S(2)}, u32[]{:S(2)}) collective-permute-start(bf16[24,2048]{1,0:T(8,128)(2,1)S(1)} %pack.1.rest_0_), channel_id=1, source_target_pairs={{0,64},{64,128},{128,192},{192,0},{1,65},{65,129},{129,193},{193,1... | collective-permute-start | bytes 294920 | tf_op jit(solution)/shard_map/ppermute | solution.py:391
